TPU v7x, 128 devices: a whole 4x4x4 slice. The times are simulated.
128 devices in a mesh: group: 16 (over x, z), local: 8 (over y, core).
Axes of the slice: x: 4, y: 4, z: 4, core: 2. Of those that a mesh axis runs over, the one named last changes fastest.
Arguments:
- states_in: bfloat16 [128, 7168], P(('group', 'local')), may hold values from -24 to 24
- queries: bfloat16 [128, 128, 576], P(('group', 'local')), may hold values from -320 to 320
- kv_cache: bfloat16 [128, 1024, 576], P(('group', 'local')), may hold values from -5 to 5
- kv_new: bfloat16 [128, 576], P(('group', 'local')), may hold values from -12 to 12
- lengths: int32 [128], P(('group', 'local')), may hold values from 2 to 1024, as said below
- w_uv: bfloat16 [128, 512, 128], P(('group', 'local')), may hold values from -1.5 to 1.5
- w_out: bfloat16 [16384, 7168], P(('group', 'local')), may hold values from -0.046875 to 0.046875
- norm_gain: float32 [7168], replicated, may hold values from 0.25 to 1.75
- expert_ids: int32 [128, 8], P(('group', 'local')), may hold values from 0 to 47, as said below
- route_scores: float32 [128, 8], P(('group', 'local')), may hold values from 0.05 to 1
- w_gate: bfloat16 [48, 7168, 1024], P('group', None, 'local'), may hold values from -0.0625 to 0.0625
- w_up: bfloat16 [48, 7168, 1024], P('group', None, 'local'), may hold values from -0.0625 to 0.0625
- w_down: bfloat16 [48, 1024, 7168], P('group', 'local'), may hold values from -0.1875 to 0.1875
Outputs:
- residual: bfloat16 [128, 7168], P(('group', 'local'))
- layer_out: bfloat16 [128, 7168], P(('group', 'local'))
Inputs may be any that keep to these rules, and one draw needn't show every extreme that they name: Each request attends to the first lengths entries of its cache and to its new token; some request has all 1024. `expert_ids`: each row names 8 different experts, all within at most 4 groups, where group g holds experts g * 6 to g * 6 + 5.
All inputs are finite; a program needn't handle non-finite values.
Results may differ from a plain program's by a relative error of at most 0.015.
Values may be sent and summed in bfloat16 or wider, within the bound.
No kernel may reach another device: no remote copies, remote signals or barrier semaphores. Data moves between devices by JAX's collectives and lax.ppermute only.
A program may use at most 128 MiB of HBM per device.

v0:
```python
import jax
import jax.numpy as jnp
from jax import lax
from jax.sharding import PartitionSpec as P

LAT = 512
ROPE = 64
VD = 128
NGRP = 8


def expert_term(slot_rows, weights, w_gate, w_up, w_down):
    result = jnp.zeros((slot_rows.shape[0], w_down.shape[2]), jnp.float32)
    for expert in range(w_gate.shape[0]):
        gate_proj = jnp.dot(slot_rows, w_gate[expert], preferred_element_type=jnp.float32)
        up_proj = jnp.dot(slot_rows, w_up[expert], preferred_element_type=jnp.float32)
        active = (jax.nn.silu(gate_proj) * up_proj).astype(jnp.bfloat16)
        output = jnp.dot(active, w_down[expert], preferred_element_type=jnp.float32)
        result = result + weights[:, expert : expert + 1].astype(jnp.float32) * output
    return result


def body(
    states_in,
    queries,
    kv_cache,
    kv_new,
    lengths,
    w_uv,
    w_out,
    norm_gain,
    expert_ids,
    route_scores,
    w_gate,
    w_up,
    w_down,
):
    requests = queries.shape[0]
    cache_len = kv_cache.shape[1]
    group_count = lax.axis_size("group")
    local_count = lax.axis_size("local")
    softmax_scale = (VD + ROPE) ** (-0.5)
    cached = (
        jnp.einsum("rhc,rkc->rhk", queries, kv_cache, preferred_element_type=jnp.float32)
        * softmax_scale
    )
    own_score = (
        jnp.einsum("rhc,rc->rh", queries, kv_new, preferred_element_type=jnp.float32)
        * softmax_scale
    )
    visible = lax.broadcasted_iota(jnp.int32, (requests, 1, cache_len), 2) < lengths[:, None, None]
    highest = jnp.maximum(jnp.max(jnp.where(visible, cached, -1e30), axis=2), own_score)
    weights_cached = jnp.exp(jnp.where(visible, cached - highest[:, :, None], -1e30))
    weight_own = jnp.exp(own_score - highest)
    denominator = jnp.sum(weights_cached, axis=2) + weight_own
    probs_cached = (weights_cached / denominator[:, :, None]).astype(jnp.bfloat16)
    prob_own = (weight_own / denominator).astype(jnp.bfloat16)
    blended = jnp.einsum(
        "rhk,rkl->rhl", probs_cached, kv_cache[:, :, :LAT], preferred_element_type=jnp.float32
    )
    blended = blended + prob_own.astype(jnp.float32)[:, :, None] * kv_new[:, None, :LAT].astype(
        jnp.float32
    )
    latent_out = blended.astype(jnp.bfloat16)
    by_head = lax.all_to_all(
        latent_out, ("group", "local"), split_axis=1, concat_axis=0, tiled=True
    )
    rows_total = by_head.shape[0]
    head_values = jnp.einsum(
        "rhl,hlv->rhv", by_head, w_uv, preferred_element_type=jnp.float32
    ).astype(jnp.bfloat16)
    value_rows = head_values.reshape(rows_total, -1)
    attention = lax.psum_scatter(
        jnp.dot(value_rows, w_out, preferred_element_type=jnp.float32),
        ("group", "local"),
        scatter_dimension=0,
        tiled=True,
    )
    residual = (states_in.astype(jnp.float32) + attention).astype(jnp.bfloat16)
    widened = residual.astype(jnp.float32)
    normed = (
        widened * lax.rsqrt(jnp.mean(widened * widened, axis=1, keepdims=True) + 1e-06) * norm_gain
    ).astype(jnp.bfloat16)
    route_weights = (2.5 * route_scores / jnp.sum(route_scores, axis=1, keepdims=True)).astype(
        jnp.bfloat16
    )
    per_block = w_gate.shape[0]
    expert_total = per_block * group_count
    span = group_count // NGRP
    experts_in_group = per_block * span
    chosen = expert_ids[:, :, None] == lax.broadcasted_iota(jnp.int32, (1, 1, expert_total), 2)
    dense_weights = jnp.sum(
        jnp.where(chosen, route_weights.astype(jnp.float32)[:, :, None], 0.0), axis=1
    )
    by_block = dense_weights.reshape(requests, group_count, per_block)
    block_group = lax.broadcasted_iota(jnp.int32, (1, 1, group_count), 2) // span
    in_group = jnp.any(expert_ids[:, :, None] // experts_in_group == block_group, axis=1)
    position = jnp.cumsum(in_group.astype(jnp.int32), axis=0) - 1
    slot_index = lax.broadcasted_iota(jnp.int32, (group_count, requests, requests), 1)
    packing = in_group.T[:, None, :] & (position.T[:, None, :] == slot_index)
    pack_half = packing.astype(jnp.bfloat16)
    send_rows = jnp.einsum(
        "gcr,rd->gcd", pack_half, normed, preferred_element_type=jnp.float32
    ).astype(jnp.bfloat16)
    send_weights = jnp.einsum(
        "gcr,rgj->gcj", packing.astype(jnp.float32), by_block, precision=lax.Precision.HIGHEST
    ).astype(jnp.bfloat16)
    copies = jnp.broadcast_to(
        send_rows[:, None], (group_count, local_count) + send_rows.shape[1:]
    ).reshape(group_count * local_count, requests, send_rows.shape[2])
    copies_weights = jnp.broadcast_to(
        send_weights[:, None], (group_count, local_count) + send_weights.shape[1:]
    ).reshape(group_count * local_count, requests, send_weights.shape[2])
    got_rows, got_weights = (
        lax.all_to_all(copies, ("group", "local"), split_axis=0, concat_axis=0, tiled=True),
        lax.all_to_all(copies_weights, ("group", "local"), split_axis=0, concat_axis=0, tiled=True),
    )
    partial_sums = expert_term(
        got_rows.reshape(-1, got_rows.shape[2]),
        got_weights.reshape(-1, got_weights.shape[2]),
        w_gate,
        w_up,
        w_down,
    )
    came_back = lax.all_to_all(
        partial_sums.reshape(group_count * local_count, requests, partial_sums.shape[1]).astype(
            jnp.bfloat16
        ),
        ("group", "local"),
        split_axis=0,
        concat_axis=0,
        tiled=True,
    ).astype(jnp.float32)
    returned = jnp.sum(
        came_back.reshape(group_count, local_count, requests, came_back.shape[2]), axis=1
    ).astype(jnp.bfloat16)
    expert_sum = jnp.einsum("gcr,gcd->rd", pack_half, returned, preferred_element_type=jnp.float32)
    layer_out = (residual.astype(jnp.float32) + expert_sum).astype(jnp.bfloat16)
    return (residual, layer_out)


def solution(mesh):
    in_specs = (
        P(("group", "local"), None),
        P(("group", "local"), None, None),
        P(("group", "local"), None, None),
        P(("group", "local"), None),
        P(("group", "local")),
        P(("group", "local"), None, None),
        P(("group", "local"), None),
        P(),
        P(("group", "local"), None),
        P(("group", "local"), None),
        P("group", None, "local"),
        P("group", None, "local"),
        P("group", "local", None),
    )
    out_specs = (P(("group", "local"), None), P(("group", "local"), None))
    return jax.shard_map(body, mesh=mesh, in_specs=in_specs, out_specs=out_specs, check_vma=False)
```

profile of v0, /device:TPU:1, one launch (start us, length us, event | category | flops | bytes accessed | tf_op | source)
XLA Modules:
  0.0 340.6 jit_solution(13489606514735457168)
XLA Ops:
  8.1 0.7 slice_convert_fusion
  8.8 1.8 select_reduce_fusion
  11.8 0.5 broadcast.263
  12.3 1.4 reduce.11
  13.8 21.3 %all_to_all.24 = bf16[128,2,256]{2,1,0:T(2,128)(2,1)S(1)} all-to-all(bf16[128,2,256]{2,1,0:T(2,128)(2,1)S(1)} %reshape.402), channel_id=1, replica_groups=mesh['group'=16,'local'=8] {'group','local'}, dimensions={0} | all-to-all | bytes 262144 | tf_op jit(solution)/shard_map/all_to_all | solution.py:65
  35.3 2.6 fusion.72
  37.9 0.6 copy-done.9
  38.5 0.6 reduce_sum.46
  39.1 0.6 bitcast_convert_fusion.3
  40.4 0.8 copy.29
  41.2 4.4 %all-to-all-start.1 = ((bf16[128,1,3]{2,1,0:T(2,128)(2,1)}), bf16[128,1,3]{2,1,0:T(2,128)(2,1)S(1)}, u32[]{:S(2)}, u32[]{:S(2)}) async-start(bf16[128,1,3]{2,1,0:T(2,128)(2,1)} %copy.29), calls=%async_computation.1 | async-start | bytes 131072 | tf_op jit(solution)/shard_map/all_to_all | solution.py:116
  45.6 142.2 %all-reduce.3.cloned.1.call-done = f32[128,7168]{1,0:T(8,128)} async-done(((f32[128,7168]{1,0:T(8,128)}), f32[128,7168]{1,0:T(8,128)}) %all-reduce.3.cloned.1.call-update) | async-done | bytes 3670032
  187.9 1.6 multiply_reduce_fusion
  190.2 1.5 broadcast_bitcast_fusion
  191.7 4.2 %reduce.12 = bf16[128,7168]{1,0:T(8,128)(2,1)} reduce(bf16[128,1,7168]{2,0,1:T(8,128)(2,1)} %broadcast_bitcast_fusion, bf16[]{:T(256)} %broadcast.263), dimensions={1}, to_apply=%copy.31.reduce_sub_computation | reduce | bytes 3670018 | tf_op jit(solution)/shard_map/broadcast_in_dim | solution.py:108
  195.9 5.4 %reshape.404 = bf16[128,2,3584]{2,1,0:T(2,128)(2,1)} reshape(bf16[128,7168]{1,0:T(8,128)(2,1)} %reduce.12) | data formatting | bytes 3670016
  201.3 7.0 %all-to-all-start.2 = ((bf16[128,2,3584]{2,1,0:T(2,128)(2,1)}), bf16[128,2,3584]{2,1,0:T(2,128)(2,1)}, u32[]{:S(2)}, u32[]{:S(2)}) async-start(bf16[128,2,3584]{2,1,0:T(2,128)(2,1)} %reshape.404), calls=%async_computation.2 | async-start | bytes 3670016 | tf_op jit(solution)/shard_map/all_to_all | solution.py:115
  208.4 27.0 %all-to-all-done.2 = bf16[128,2,3584]{2,1,0:T(2,128)(2,1)} async-done(((bf16[128,2,3584]{2,1,0:T(2,128)(2,1)}), bf16[128,2,3584]{2,1,0:T(2,128)(2,1)}, u32[]{:S(2)}, u32[]{:S(2)}) %all-to-all-start.2) | async-done | bytes 1835040 | tf_op jit(solution)/shard_map/all_to_all | solution.py:115
  235.4 11.5 %reshape.405 = bf16[128,1,7168]{2,1,0:T(2,128)(2,1)} reshape(bf16[128,2,3584]{2,1,0:T(2,128)(2,1)} %all-to-all-done.2) | data formatting | bytes 3670016
  246.9 2.6 copy.34
  249.5 2.8 fusion.11
  252.4 2.2 fusion.7
  254.6 2.2 fusion.15
  256.7 5.6 %convolution_multiply_fusion.2 = f32[128,7168]{1,0:T(8,128)} fusion(bf16[3,128,7168]{2,1,0:T(8,128)(2,1)} %param.25, f32[128]{0:T(128)S(1)} %get-tuple-element.8, bf16[3,7168,128]{2,1,0:T(8,128)(2,1)} %param.24, bf16[128,1,7168]{2,0,1:T(8,128)(2,1)} %copy-done.1, f32[128,128]{1,0:T(8,128)S(1)} %fusion.15), kind=kOutput, calls=%fused_computation.4 | convolution fusion | flops 470777856 | bytes 9241088 | tf_op jit(solution)/shard_map/dot_general | solution.py:18
  262.4 6.7 %fusion.1 = f32[128,7168]{1,0:T(8,128)} fusion(f32[128,7168]{1,0:T(8,128)} %convolution_multiply_fusion.2, bf16[3,128,7168]{2,1,0:T(8,128)(2,1)} %param.25, f32[128]{0:T(128)S(1)} %get-tuple-element.7, bf16[3,7168,128]{2,1,0:T(8,128)(2,1)} %param.24, bf16[128,1,7168]{2,0,1:T(8,128)(2,1)} %copy-done.1, f32[128,128]{1,0:T(8,128)S(1)} %fusion.11), kind=kOutput, calls=%fused_computation.3 | convolution fusion | flops 471695360 | bytes 12911104 | tf_op jit(solution)/shard_map/dot_general | solution.py:18
  269.1 6.2 %fusion.3 = bf16[128,1,7168]{2,0,1:T(8,128)(2,1)} fusion(f32[128,7168]{1,0:T(8,128)} %fusion.1, bf16[3,128,7168]{2,1,0:T(8,128)(2,1)} %param.25, f32[128]{0:T(128)S(1)} %get-tuple-element.6, bf16[3,7168,128]{2,1,0:T(8,128)(2,1)} %param.24, bf16[128,1,7168]{2,0,1:T(8,128)(2,1)} %copy-done.1, f32[128,128]{1,0:T(8,128)S(1)} %fusion.7), kind=kOutput, calls=%fused_computation.6 | convolution fusion | flops 472612864 | bytes 11076096 | tf_op jit(solution)/shard_map/dot_general | solution.py:18
  275.3 4.2 %reduce.13 = bf16[128,7168]{1,0:T(8,128)(2,1)} reduce(bf16[128,1,7168]{2,0,1:T(8,128)(2,1)} %fusion.3, bf16[]{:T(256)} %broadcast.263), dimensions={1}, to_apply=%copy.32.reduce_sub_computation | reduce | bytes 3670018 | tf_op jit(solution)/shard_map/convert_element_type | solution.py:126
  279.5 5.4 %reshape.406 = bf16[128,2,3584]{2,1,0:T(2,128)(2,1)} reshape(bf16[128,7168]{1,0:T(8,128)(2,1)} %reduce.13) | data formatting | bytes 3670016
  284.9 33.1 %all_to_all.25 = bf16[128,2,3584]{2,1,0:T(2,128)(2,1)} all-to-all(bf16[128,2,3584]{2,1,0:T(2,128)(2,1)} %reshape.406), channel_id=1, replica_groups=mesh['group'=16,'local'=8] {'group','local'}, dimensions={0} | all-to-all | bytes 3670016 | tf_op jit(solution)/shard_map/all_to_all | solution.py:125
  318.0 11.5 %reshape.407 = bf16[128,1,7168]{2,1,0:T(2,128)(2,1)} reshape(bf16[128,2,3584]{2,1,0:T(2,128)(2,1)} %all_to_all.25) | data formatting | bytes 3670016
  329.5 3.5 %bitcast_reduce_fusion = bf16[16,7168]{1,0:T(8,128)(2,1)S(1)} fusion(bf16[128,1,7168]{2,1,0:T(2,128)(2,1)} %reshape.407), kind=kLoop, calls=%fused_computation.9 | loop fusion | flops 802816 | bytes 2064384 | tf_op jit(solution)/shard_map/reduce_sum | solution.py:134
  333.0 0.8 fusion.4
  (46 shorter events, 2.2 us)
Async XLA Ops:
  7.2 28.1 %copy-start = (bf16[128,7168]{1,0:T(8,128)(2,1)S(1)}, bf16[128,7168]{1,0:T(8,128)(2,1)}, u32[]{:S(2)}) copy-start(bf16[128,7168]{1,0:T(8,128)(2,1)} %param.19) | copy-start | bytes 5505028
  7.2 3.5 %copy-start.8 = (bf16[1,576]{1,0:T(2,128)(2,1)S(1)}, bf16[1,576]{1,0:T(2,128)(2,1)}, u32[]{:S(2)}) copy-start(bf16[1,576]{1,0:T(2,128)(2,1)} %param.16) | copy-start | bytes 3460
  7.2 3.9 %copy-start.2 = (bf16[1,1024,576]{1,2,0:T(8,128)(2,1)S(1)}, bf16[1,1024,576]{1,2,0:T(8,128)(2,1)}, u32[]{:S(2)}) copy-start(bf16[1,1024,576]{1,2,0:T(8,128)(2,1)} %param.15) | copy-start | bytes 3538948
  7.2 3.5 %copy-start.3 = (bf16[1,128,576]{1,2,0:T(8,128)(2,1)S(1)}, bf16[1,128,576]{1,2,0:T(8,128)(2,1)}, u32[]{:S(2)}) copy-start(bf16[1,128,576]{1,2,0:T(8,128)(2,1)} %param.14) | copy-start | bytes 442372
  7.2 180.6 %all-reduce.3.cloned.1.call-start = ((), (), s32[]{:S(2)}) async-start(), calls=%async_computation.4 | async-start | bytes 7340032
  11.1 24.2 %copy-start.4 = (bf16[1,512,128]{2,1,0:T(8,128)(2,1)S(1)}, bf16[1,512,128]{2,1,0:T(8,128)(2,1)}, u32[]{:S(2)}) copy-start(bf16[1,512,128]{2,1,0:T(8,128)(2,1)} %param.18) | copy-start | bytes 393220
  37.9 0.7 copy-start.9
  37.9 1.9 copy-start.10
  37.9 150.0 %copy-start.6 = (bf16[1,7168]{1,0:T(2,128)(2,1)S(1)}, bf16[1,7168]{1,0:T(2,128)(2,1)}, u32[]{:S(2)}) copy-start(bf16[1,7168]{1,0:T(2,128)(2,1)} %param.13) | copy-start | bytes 43012
  37.9 152.2 %copy-start.7 = (f32[7168]{0:T(1024)S(1)}, f32[7168]{0:T(1024)}, u32[]{:S(2)}) copy-start(f32[7168]{0:T(1024)} %param.20) | copy-start | bytes 86020
  41.2 160.1 %all-to-all-start.1 = ((bf16[128,1,3]{2,1,0:T(2,128)(2,1)}), bf16[128,1,3]{2,1,0:T(2,128)(2,1)S(1)}, u32[]{:S(2)}, u32[]{:S(2)}) async-start(bf16[128,1,3]{2,1,0:T(2,128)(2,1)} %copy.29), calls=%async_computation.1 | async-start | bytes 131072 | tf_op jit(solution)/shard_map/all_to_all | solution.py:116
  189.5 143.5 %copy-start.5 = (bf16[1,7168]{1,0:T(2,128)(2,1)}, bf16[1,7168]{1,0:T(2,128)(2,1)S(1)}, u32[]{:S(2)}) copy-start(bf16[1,7168]{1,0:T(2,128)(2,1)S(1)} %get-tuple-element.3) | copy-start | bytes 43012
  201.3 34.1 %all-to-all-start.2 = ((bf16[128,2,3584]{2,1,0:T(2,128)(2,1)}), bf16[128,2,3584]{2,1,0:T(2,128)(2,1)}, u32[]{:S(2)}, u32[]{:S(2)}) async-start(bf16[128,2,3584]{2,1,0:T(2,128)(2,1)} %reshape.404), calls=%async_computation.2 | async-start | bytes 3670016 | tf_op jit(solution)/shard_map/all_to_all | solution.py:115
  249.5 5.0 %copy-start.1 = (bf16[128,1,7168]{2,0,1:T(8,128)(2,1)}, bf16[128,1,7168]{2,0,1:T(8,128)(2,1)S(1)}, u32[]{:S(2)}) copy-start(bf16[128,1,7168]{2,0,1:T(8,128)(2,1)S(1)} %copy.34) | copy-start | bytes 5505028
Sparse Core Ops, SparseCore 0:
  38.0 149.7 all-reduce.2
where the time goes:
time: 342 us; the launch traced here: 341 us
  waiting for transfers between devices  169 us (49%)
  blocking collectives  54.5 us (16%)
  local copies, waits for them, and re-layouts  40.5 us (12%)
  matrix products  31.6 us (9%)
  other arithmetic  17.6 us (5%)
  between operations  15.7 us (5%)
  starting transfers between devices  11.5 us (3%)
    unnamed x2, waiting for transfers between devices  142 us
    unnamed x30, local copies, waits for them, and re-layouts  37.6 us
    all_to_all x1, blocking collectives, body(): lax.all_to_all(partial_sums.reshape(group_count * local_count, requests,...  33.1 us
    all_to_all x1, waiting for transfers between devices, body(): lax.all_to_all(copies, ('group', 'local'), split_axis=0, concat_axis=0, t...  27 us
    all_to_all x1, blocking collectives, body(): lax.all_to_all(latent_out, ('group', 'local'), split_axis=1, concat_axis=...  21.3 us
    dot_general x3, matrix products, expert_term(): output = jnp.dot(active, w_down[expert], preferred_element_type=jnp.float32)  18.5 us
    dot_general x3, matrix products, expert_term(): jnp.dot(slot_rows, w_gate[expert], preferred_element_type=jnp.float32)  7.18 us
    all_to_all x1, starting transfers between devices, body(): lax.all_to_all(copies, ('group', 'local'), split_axis=0, concat_axis=0, t...  7.02 us
  transfers between devices with their start and end apart: 3, of which 2 were waited for; matrix products, arithmetic and copies ran while one was open for 5% of the time, Pallas kernels for 0%

commit v1 on v0

v1 whole, which is shorter than its diff:
```python
import jax
import jax.numpy as jnp
from jax import lax
from jax.experimental import pallas as pl
from jax.experimental.pallas import tpu as pltpu
from jax.sharding import Mesh, PartitionSpec as P

LAT = 512
ROPE = 64
VD = 128
NX, NZ, NY = 4, 4, 4
CHIPS = NX * NZ * NY
GROUPS = NX * NZ
CHIP_AXES = ("x", "z", "y")
ALL_AXES = ("x", "z", "y", "core")
SWAP = [(0, 1), (1, 0)]
BF = jnp.bfloat16
F32 = jnp.float32


def swap(value):
    return lax.ppermute(value, "core", SWAP)


def exchange(value):
    return lax.all_to_all(value, CHIP_AXES, split_axis=0, concat_axis=0, tiled=True)


def interleave(core, own, other):
    first = jnp.where(core == 0, own, other)
    second = jnp.where(core == 0, other, own)
    return jnp.stack([first, second], axis=1).reshape((-1,) + own.shape[1:])


def out_kernel(core_ref, values_ref, own_ref, other_ref, out_ref):
    del core_ref
    weights = jnp.concatenate([own_ref[...], other_ref[...]], axis=0)
    product = jnp.dot(values_ref[...], weights, preferred_element_type=F32)
    out_ref[...] = product.astype(BF).reshape(out_ref.shape)


def out_projection(core, values, own, other):
    rows = values.shape[0]
    wide = own.shape[1] // 8
    spec = pl.BlockSpec((own.shape[0], wide), lambda y, c: (0, 4 * c[0] + y))
    return pl.pallas_call(
        out_kernel,
        grid_spec=pltpu.PrefetchScalarGridSpec(
            num_scalar_prefetch=1,
            grid=(NY,),
            in_specs=[pl.BlockSpec(values.shape, lambda y, c: (0, 0)), spec, spec],
            out_specs=pl.BlockSpec((rows // 8, 1, 8, wide), lambda y, c: (0, y, 0, 0)),
        ),
        out_shape=jax.ShapeDtypeStruct((rows // 8, NY, 8, wide), BF),
        name="out_projection",
    )(core[None], values, own, other)


def gate_up_kernel(
    core_ref, own_ref, other_ref, gain_ref, route_ref, gate_ref, up_ref, act_ref, inverse_ref, sum_ref
):
    del core_ref
    step = pl.program_id(0)
    rows = act_ref.shape[0]
    wide = own_ref.shape[-1]
    experts = gate_ref.shape[0]

    def part(ref, y):
        return ref[:, y].reshape(rows, wide)

    @pl.when(step == 0)
    def _():
        total = jnp.zeros((rows, 1), F32)
        for ref in (own_ref, other_ref):
            for y in range(NY):
                piece = part(ref, y).astype(F32)
                total = total + jnp.sum(piece * piece, axis=1, keepdims=True)
        inverse_ref[...] = lax.rsqrt(total / (8 * wide) + 1e-06)
        sum_ref[...] = jnp.zeros_like(sum_ref)

    def accumulate(ref, y):
        piece = jnp.concatenate([part(ref, y), part(ref, y + 1)], axis=1).astype(F32)
        normed = (piece * inverse_ref[...] * gain_ref[...]).astype(BF)
        for e in range(experts):
            weights = jnp.concatenate([gate_ref[e], up_ref[e]], axis=1)
            sum_ref[e] += jnp.dot(normed, weights, preferred_element_type=F32)

    for index, (ref, y) in enumerate(((own_ref, 0), (own_ref, 2), (other_ref, 0), (other_ref, 2))):
        pl.when(step == index)(lambda ref=ref, y=y: accumulate(ref, y))

    @pl.when(step == 3)
    def _():
        for e in range(experts):
            hidden = act_ref.shape[1] // experts
            gate = sum_ref[e, :, :hidden]
            up = sum_ref[e, :, hidden:]
            active = gate / (1.0 + jnp.exp(-gate)) * up
            active = active * route_ref[:, e : e + 1].astype(F32)
            act_ref[:, e * hidden : (e + 1) * hidden] = active.astype(BF)


def gate_up(core, own, other, gain, route, w_gate, w_up):
    groups, _, eight, wide = own.shape
    rows = groups * eight
    experts, model, hidden = w_gate.shape

    def block(step, c):
        half = jnp.where(step < 2, c[0], 1 - c[0])
        return 2 * half + step % 2

    weights = pl.BlockSpec((experts, 2 * wide, hidden), lambda s, c: (0, block(s, c), 0))
    whole = pl.BlockSpec(own.shape, lambda s, c: (0, 0, 0, 0))
    return pl.pallas_call(
        gate_up_kernel,
        grid_spec=pltpu.PrefetchScalarGridSpec(
            num_scalar_prefetch=1,
            grid=(4,),
            in_specs=[
                whole,
                whole,
                pl.BlockSpec((1, 2 * wide), lambda s, c: (0, block(s, c))),
                pl.BlockSpec(route.shape, lambda s, c: (0, 0)),
                weights,
                weights,
            ],
            out_specs=pl.BlockSpec((rows, experts * hidden), lambda s, c: (0, 0)),
            scratch_shapes=[
                pltpu.VMEM((rows, 1), F32),
                pltpu.VMEM((experts, rows, 2 * hidden), F32),
            ],
        ),
        out_shape=jax.ShapeDtypeStruct((rows, experts * hidden), BF),
        name="gate_up",
    )(core[None], own, other, gain[None], route, w_gate, w_up)


def down_kernel(core_ref, act_own_ref, act_other_ref, own_ref, other_ref, out_ref):
    del core_ref
    act = jnp.concatenate([act_own_ref[...], act_other_ref[...]], axis=1)
    weights = jnp.concatenate([own_ref[...], other_ref[...]], axis=0)
    out_ref[...] = jnp.dot(act, weights, preferred_element_type=F32).astype(BF)


def down(core, act_own, act_other, own, other):
    rows = act_own.shape[0]
    wide = own.shape[1] // 8
    act = pl.BlockSpec(act_own.shape, lambda y, c: (0, 0))
    spec = pl.BlockSpec((own.shape[0], wide), lambda y, c: (0, 4 * c[0] + y))
    return pl.pallas_call(
        down_kernel,
        grid_spec=pltpu.PrefetchScalarGridSpec(
            num_scalar_prefetch=1,
            grid=(NY,),
            in_specs=[act, act, spec, spec],
            out_specs=pl.BlockSpec((rows, wide), lambda y, c: (0, y)),
        ),
        out_shape=jax.ShapeDtypeStruct((rows, NY * wide), BF),
        name="down",
    )(core[None], act_own, act_other, own, other)


def attend(queries, kv_cache, kv_new, lengths):
    cache_len = kv_cache.shape[1]
    requests = queries.shape[0]
    softmax_scale = (VD + ROPE) ** (-0.5)
    cached = (
        jnp.einsum("rhc,rkc->rhk", queries, kv_cache, preferred_element_type=F32) * softmax_scale
    )
    own_score = jnp.einsum("rhc,rc->rh", queries, kv_new, preferred_element_type=F32) * softmax_scale
    visible = lax.broadcasted_iota(jnp.int32, (requests, 1, cache_len), 2) < lengths[:, None, None]
    highest = jnp.maximum(jnp.max(jnp.where(visible, cached, -1e30), axis=2), own_score)
    weights_cached = jnp.exp(jnp.where(visible, cached - highest[:, :, None], -1e30))
    weight_own = jnp.exp(own_score - highest)
    denominator = jnp.sum(weights_cached, axis=2) + weight_own
    probs_cached = (weights_cached / denominator[:, :, None]).astype(BF)
    prob_own = (weight_own / denominator).astype(BF)
    blended = jnp.einsum(
        "rhk,rkl->rhl", probs_cached, kv_cache[:, :, :LAT], preferred_element_type=F32
    )
    blended = blended + prob_own.astype(F32)[:, :, None] * kv_new[:, None, :LAT].astype(F32)
    return blended.astype(BF)


def body(
    states_in,
    queries,
    kv_cache,
    kv_new,
    lengths,
    w_uv,
    w_out,
    norm_gain,
    expert_ids,
    route_scores,
    w_gate,
    w_up,
    w_down,
):
    core = lax.axis_index("core")
    group = lax.axis_index("x") * NZ + lax.axis_index("z")
    y_at = lax.axis_index("y")
    model = states_in.shape[1]
    half = model // 2
    wide = half // NY
    experts = w_gate.shape[0]
    expert_total = experts * GROUPS
    down_own = w_down.reshape(-1, model)
    uv_other = swap(w_uv)
    out_other = swap(w_out)
    down_other = swap(down_own)
    states_swapped = swap(states_in)

    latent_out = attend(queries, kv_cache, kv_new, lengths)[0]

    route_weights = (2.5 * route_scores / jnp.sum(route_scores, axis=1, keepdims=True)).astype(BF)
    chosen = expert_ids[:, :, None] == lax.broadcasted_iota(jnp.int32, (1, 1, expert_total), 2)
    dense_weights = jnp.sum(jnp.where(chosen, route_weights.astype(F32)[:, :, None], 0.0), axis=1)
    by_block = dense_weights.reshape(GROUPS, 1, 1, experts).astype(BF)
    by_block = jnp.broadcast_to(
        jnp.pad(by_block, ((0, 0), (0, 0), (0, 0), (0, 128 - experts))), (GROUPS, NY, 2, 128)
    ).reshape(CHIPS, 2, 128)

    own_half = lax.dynamic_slice_in_dim(states_in, core * half, half, 1)
    other_half = lax.dynamic_slice_in_dim(states_swapped, core * half, half, 1)
    chip_states = interleave(core, own_half, other_half)
    chip_states = chip_states.reshape(2, NY, wide).transpose(1, 0, 2)
    chip_states = jnp.broadcast_to(chip_states[None], (GROUPS, NY, 2, wide)).reshape(CHIPS, 2, wide)

    sent = jnp.concatenate([latent_out.reshape(CHIPS, 2, LAT), by_block, chip_states], axis=2)
    got = exchange(sent)

    latent_own = lax.dynamic_index_in_dim(got, core, 1, keepdims=False)[:, :LAT]
    latent_other = lax.dynamic_index_in_dim(got, 1 - core, 1, keepdims=False)[:, :LAT]
    route_rows = got[:, 0, LAT : LAT + 128]
    my_states = lax.dynamic_slice_in_dim(got[:, :, LAT + 128 :], group * NY, NY, 0).reshape(8, wide)

    value_own = jnp.dot(latent_own, w_uv[0], preferred_element_type=F32).astype(BF)
    value_other = jnp.dot(latent_other, uv_other[0], preferred_element_type=F32).astype(BF)
    mine = jnp.concatenate([value_own, value_other, route_rows], axis=1)
    theirs_sent = jnp.concatenate([value_other, value_own, route_rows], axis=1)
    rows_all = interleave(core, mine, swap(theirs_sent))
    values = rows_all[:, : 2 * VD]
    route = rows_all[:, 2 * VD :]

    partial = out_projection(core, values, w_out, out_other)
    partial = exchange(partial.reshape(CHIPS, 8, wide))
    attention = jnp.sum(partial.astype(F32), axis=0)
    residual_part = (my_states.astype(F32) + attention).astype(BF)
    rows_own = exchange(jnp.broadcast_to(residual_part[None], (CHIPS, 8, wide)))
    rows_other = swap(rows_own)
    rows_own = rows_own.reshape(GROUPS, NY, 8, wide)
    rows_other = rows_other.reshape(GROUPS, NY, 8, wide)

    act = gate_up(core, rows_own, rows_other, norm_gain, route, w_gate, w_up)
    act_other = swap(act)
    output = down(core, act, act_other, down_own, down_other)
    output = output.reshape(CHIPS, 2, half // 128, 128).transpose(0, 2, 1, 3)
    output = exchange(output.reshape(CHIPS, half // 64, 128))
    expert_sum = jnp.sum(output.astype(F32), axis=0)
    expert_sum = expert_sum.reshape(half // 128, 2, 128).transpose(1, 0, 2).reshape(2, half)

    def chip_rows(rows):
        mine = lax.dynamic_index_in_dim(rows, group, 0, keepdims=False)
        mine = lax.dynamic_slice_in_dim(mine, 2 * y_at, 2, 1)
        return mine.transpose(1, 0, 2).reshape(2, half)

    residual_own = chip_rows(rows_own)
    residual_other = chip_rows(rows_other)
    layer_half = (residual_own.astype(F32) + expert_sum).astype(BF)
    layer_mine = lax.dynamic_slice_in_dim(layer_half, core, 1, 0)
    layer_got = swap(lax.dynamic_slice_in_dim(layer_half, 1 - core, 1, 0))
    residual_mine = lax.dynamic_slice_in_dim(residual_own, core, 1, 0)
    residual_got = lax.dynamic_slice_in_dim(residual_other, core, 1, 0)

    def joined(mine, got):
        return jnp.where(
            core == 0, jnp.concatenate([mine, got], axis=1), jnp.concatenate([got, mine], axis=1)
        )

    return (joined(residual_mine, residual_got), joined(layer_mine, layer_got))


def solution(mesh):
    fine = Mesh(mesh.devices.reshape(NX, NZ, NY, 2), ALL_AXES)
    rows = P(ALL_AXES, None)
    cube = P(ALL_AXES, None, None)
    in_specs = (
        rows,
        cube,
        cube,
        rows,
        P(ALL_AXES),
        cube,
        rows,
        P(),
        rows,
        rows,
        P(("x", "z"), None, ("y", "core")),
        P(("x", "z"), None, ("y", "core")),
        P(("x", "z"), ("y", "core"), None),
    )
    return jax.shard_map(body, mesh=fine, in_specs=in_specs, out_specs=(rows, rows), check_vma=False)
```

time: 342 us -> 135 us (0.39)
  waiting for transfers between devices: 169 us -> 44.1 us
  blocking collectives: 54.5 us -> 19.9 us
  local copies, waits for them, and re-layouts: 40.5 us -> 11.4 us
  matrix products: 31.6 us -> 2.7 us
  starting transfers between devices: 11.5 us -> 30.6 us
  Pallas kernels: 0 us -> 16.4 us
  between operations: 15.7 us -> 1.65 us
  other arithmetic: 17.6 us -> 7.24 us
    unnamed x2 -> x0, waiting for transfers between devices: 142 us -> none
    all_to_all x2 -> x1, blocking collectives: 54.5 us -> 19.9 us  [exchange(): lax.all_to_all(value, CHIP_AXES, split_axis=0, concat_axis=0, tiled=True)]
    unnamed x30 -> x21, local copies, waits for them, and re-layouts: 37.6 us -> 3.05 us
    dot_general x11 -> x5, matrix products: 31.6 us -> 2.7 us  [the longest x1 1.76 us: attend(): jnp.einsum('rhc,rkc->rhk', queries, kv_cache, preferred_element_type=F32)]
    pallas_call x0 -> x3, Pallas kernels: none -> 16.4 us  [the longest x1 7.41 us: gate_up(): pl.pallas_call(gate_up_kernel, grid_spec=pltpu.PrefetchScalarGridSpec(num...]
    all_to_all x2 -> x3, waiting for transfers between devices: 27 us -> 40.4 us  [exchange(): lax.all_to_all(value, CHIP_AXES, split_axis=0, concat_axis=0, tiled=True)]
    ppermute x0 -> x8, starting transfers between devices: none -> 10 us  [swap(): return lax.ppermute(value, 'core', SWAP)]
    all_to_all x2 -> x3, starting transfers between devices: 11.4 us -> 20.5 us  [exchange(): lax.all_to_all(value, CHIP_AXES, split_axis=0, concat_axis=0, tiled=True)]
  transfers between devices with their start and end apart: 3 -> 11, of which waited for: 2 -> 7; matrix products, arithmetic and copies ran while one was open for 5% -> 10% of each run, Pallas kernels for 0% -> 9%
where the time goes in v1:
time: 135 us; the launch traced here: 134 us
  waiting for transfers between devices  44.1 us (33%)
  starting transfers between devices  30.6 us (23%)
  blocking collectives  19.9 us (15%)
  Pallas kernels  16.4 us (12%)
  local copies, waits for them, and re-layouts  11.4 us (8%)
  other arithmetic  7.24 us (5%)
  matrix products  2.7 us (2%)
  between operations  1.65 us (1%)
    all_to_all x3, waiting for transfers between devices, exchange(): lax.all_to_all(value, CHIP_AXES, split_axis=0, concat_axis=0, tiled=True)  40.4 us
    all_to_all x3, starting transfers between devices, exchange(): lax.all_to_all(value, CHIP_AXES, split_axis=0, concat_axis=0, tiled=True)  20.5 us
    all_to_all x1, blocking collectives, exchange(): lax.all_to_all(value, CHIP_AXES, split_axis=0, concat_axis=0, tiled=True)  19.9 us
    ppermute x8, starting transfers between devices, swap(): return lax.ppermute(value, 'core', SWAP)  10 us
    pallas_call x1, Pallas kernels, gate_up(): pl.pallas_call(gate_up_kernel, grid_spec=pltpu.PrefetchScalarGridSpec(num...  7.41 us
    pallas_call x1, Pallas kernels, down(): pl.pallas_call(down_kernel, grid_spec=pltpu.PrefetchScalarGridSpec(num_sc...  4.92 us
    pallas_call x1, Pallas kernels, out_projection(): pl.pallas_call(out_kernel, grid_spec=pltpu.PrefetchScalarGridSpec(num_sca...  4.03 us
    ppermute x8, waiting for transfers between devices, swap(): return lax.ppermute(value, 'core', SWAP)  3.71 us
  transfers between devices with their start and end apart: 11, of which 7 were waited for; matrix products, arithmetic and copies ran while one was open for 10% of the time, Pallas kernels for 9%

profile of v1, /device:TPU:1, one launch (start us, length us, event | category | flops | bytes accessed | tf_op | source)
XLA Modules:
  0.0 133.8 jit_solution(11967666922082490898)
XLA Ops:
  0.7 1.5 %collective-permute-start = (bf16[1,7168]{1,0:T(2,128)(2,1)}, bf16[1,7168]{1,0:T(2,128)(2,1)S(1)}, u32[]{:S(2)}, u32[]{:S(2)}) collective-permute-start(bf16[1,7168]{1,0:T(2,128)(2,1)} %param.13), channel_id=1, source_target_pairs={{0,1},{1,0},{2,3},{3,2},{4,5},{5,4},{6,7},{7,6},{8,9},{9,8},{10,11... | collective-permute-start | bytes 43016 | tf_op jit(solution)/shard_map/ppermute | solution.py:22
  3.3 1.3 reduce_sum.46
  4.6 1.3 bitcast_convert_fusion
  5.9 0.7 slice_convert_fusion
  6.6 0.7 select_reduce_fusion.1
  7.4 1.8 %select_reduce_fusion = (f32[128]{0:T(128)S(1)}, f32[128,1024]{1,0:T(8,128)S(1)}) fusion(pred[1024]{0:T(1024)(128)(4,1)S(1)} %iota_compare_fusion.1, bf16[1,1024,576]{1,2,0:T(8,128)(2,1)} %param.15, bf16[1,128,576]{1,2,0:T(8,128)(2,1)S(1)} %copy-done), kind=kOutput, calls=%fused_computation.14 | convolution fusion | flops 151388032 | bytes 1852928 | tf_op jit(solution)/shard_map/rhc,rkc->rhk/dot_general | solution.py:167
  10.7 1.1 pad_maximum_fusion
  11.8 11.2 %all-to-all-start = ((bf16[64,2,1536]{2,1,0:T(2,128)(2,1)}), bf16[64,2,1536]{2,1,0:T(2,128)(2,1)S(1)}, u32[]{:S(2)}, u32[]{:S(2)}) async-start(bf16[64,2,1536]{2,1,0:T(2,128)(2,1)} %pad_maximum_fusion), calls=%async_computation | async-start | bytes 786432 | tf_op jit(solution)/shard_map/all_to_all | solution.py:26
  23.5 10.4 %all-to-all-done = bf16[64,2,1536]{2,1,0:T(2,128)(2,1)S(1)} async-done(((bf16[64,2,1536]{2,1,0:T(2,128)(2,1)}), bf16[64,2,1536]{2,1,0:T(2,128)(2,1)S(1)}, u32[]{:S(2)}, u32[]{:S(2)}) %all-to-all-start) | async-done | bytes 393248 | tf_op jit(solution)/shard_map/all_to_all | solution.py:26
  34.0 0.8 constant_dynamic-slice_fusion.6
  35.2 2.0 %collective-permute-start.2 = (bf16[64,384]{1,0:T(8,128)(2,1)S(1)}, bf16[64,384]{1,0:T(8,128)(2,1)S(1)}, u32[]{:S(2)}, u32[]{:S(2)}) collective-permute-start(bf16[64,384]{1,0:T(8,128)(2,1)S(1)} %pad_maximum_fusion.2), channel_id=1, source_target_pairs={{0,1},{1,0},{2,3},{3,2},{4,5},{5,4},{6,7},{7,6},{8,9},{9,8},{10,11... | collective-permute-start | bytes 147464 | tf_op jit(solution)/shard_map/ppermute | solution.py:22
  37.1 0.9 collective-permute-done.2
  38.9 1.2 copy-done.2
  40.1 4.0 %out_projection.1 = bf16[16,4,8,896]{3,2,1,0:T(8,128)(2,1)} custom-call(s32[1]{0:T(128)} %bitcast.12.core_ref, bf16[128,256]{1,0:T(8,128)(2,1)} %slice.36.values_ref, bf16[128,7168]{1,0:T(8,128)(2,1)} %own_ref.1, bf16[128,7168]{1,0:T(8,128)(2,1)} %copy-done.2), custom_call_target="tpu_custom_call" | custom-call | tf_op jit(solution)/shard_map/out_projection/pallas_call | solution.py:46
  44.2 4.7 %all-to-all-start.1 = ((bf16[64,8,896]{2,1,0:T(8,128)(2,1)}), bf16[64,8,896]{2,1,0:T(8,128)(2,1)S(1)}, u32[]{:S(2)}, u32[]{:S(2)}) async-start(bf16[64,8,896]{2,1,0:T(8,128)(2,1)} %bitcast.86), calls=%async_computation.1 | async-start | bytes 1835008 | tf_op jit(solution)/shard_map/all_to_all | solution.py:26
  49.0 15.7 %all-to-all-done.1 = bf16[64,8,896]{2,1,0:T(8,128)(2,1)S(1)} async-done(((bf16[64,8,896]{2,1,0:T(8,128)(2,1)}), bf16[64,8,896]{2,1,0:T(8,128)(2,1)S(1)}, u32[]{:S(2)}, u32[]{:S(2)}) %all-to-all-start.1) | async-done | bytes 917536 | tf_op jit(solution)/shard_map/all_to_all | solution.py:26
  65.0 19.9 %all_to_all.20 = bf16[64,8,896]{2,1,0:T(8,128)(2,1)S(1)} all-to-all(bf16[64,8,896]{2,1,0:T(8,128)(2,1)S(1)} %broadcast_in_dim.77), channel_id=1, replica_groups=mesh['x'=4,'z'=4,'y'=4,'core'=2] {'x','z','y'}, dimensions={0} | all-to-all | bytes 1835008 | tf_op jit(solution)/shard_map/all_to_all | solution.py:26
  84.9 3.0 %collective-permute-start.4 = (bf16[64,8,896]{2,1,0:T(8,128)(2,1)S(1)}, bf16[64,8,896]{2,1,0:T(8,128)(2,1)S(1)}, u32[]{:S(2)}, u32[]{:S(2)}) collective-permute-start(bf16[64,8,896]{2,1,0:T(8,128)(2,1)S(1)} %all_to_all.20), channel_id=1, source_target_pairs={{0,1},{1,0},{2,3},{3,2},{4,5},{5,4},{6,7},{7,6},{8,9},{9,8},{10,11... | collective-permute-start | bytes 2752520 | tf_op jit(solution)/shard_map/ppermute | solution.py:22
  88.5 1.5 %collective-permute-done.4 = bf16[64,8,896]{2,1,0:T(8,128)(2,1)S(1)} collective-permute-done((bf16[64,8,896]{2,1,0:T(8,128)(2,1)S(1)}, bf16[64,8,896]{2,1,0:T(8,128)(2,1)S(1)}, u32[]{:S(2)}, u32[]{:S(2)}) %collective-permute-start.4) | collective-permute-done | bytes 917536 | tf_op jit(solution)/shard_map/ppermute | solution.py:22
  90.0 0.9 copy-done.4
  90.9 7.4 %gate_up.1.act_own_ref = bf16[128,384]{1,0:T(8,128)(2,1)} custom-call(s32[1]{0:T(128)} %bitcast.12.core_ref, bf16[16,4,8,896]{3,2,1,0:T(8,128)(2,1)} %bitcast.84, bf16[16,4,8,896]{3,2,1,0:T(8,128)(2,1)} %bitcast.88, f32[1,7168]{1,0:T(1,128)} %bitcast.100, bf16[128,128]{1,0:T(8,128)(2,1)} %slice.37.route_ref, bf16[3,7168,128]{2,1,0:T(8,128)(2,1)} %gate_ref.1, ...), custom_call_target="tpu_custom_call" | custom-call | tf_op jit(solution)/shard_map/gate_up/pallas_call | solution.py:113
  98.7 1.2 collective-permute-done.5.act_other_ref
  100.5 4.9 %down.1 = bf16[128,3584]{1,0:T(8,128)(2,1)} custom-call(s32[1]{0:T(128)} %bitcast.12.core_ref, bf16[128,384]{1,0:T(8,128)(2,1)} %gate_up.1.act_own_ref, bf16[128,384]{1,0:T(8,128)(2,1)} %copy-done.6, bf16[384,7168]{1,0:T(8,128)(2,1)} %bitcast.82, bf16[384,7168]{1,0:T(8,128)(2,1)} %collective-permute-done.6.other_ref), custom_call_target="tpu_custom_call" | custom-call | tf_op jit(solution)/shard_map/down/pallas_call | solution.py:149
  105.4 1.6 %reshape.345 = bf16[64,2,28,128]{3,2,1,0:T(8,128)(2,1)S(1)} reshape(bf16[128,3584]{1,0:T(8,128)(2,1)} %down.1) | data formatting | bytes 1835008 | tf_op jit(solution)/shard_map/reshape | solution.py:257
  107.7 1.5 %copy.39 = bf16[64,56,128]{2,1,0:T(8,128)(2,1)} copy(bf16[64,56,128]{2,0,1:T(8,128)(2,1)S(1)} %bitcast.87) | data formatting | bytes 1835008 | tf_op jit(solution)/shard_map/reshape | solution.py:258
  109.2 4.6 %all-to-all-start.3 = ((bf16[64,56,128]{2,1,0:T(8,128)(2,1)}), bf16[64,56,128]{2,1,0:T(8,128)(2,1)S(1)}, u32[]{:S(2)}, u32[]{:S(2)}) async-start(bf16[64,56,128]{2,1,0:T(8,128)(2,1)} %copy.39), calls=%async_computation.3 | async-start | bytes 1835008 | tf_op jit(solution)/shard_map/all_to_all | solution.py:26
  113.9 0.8 constant_dynamic-slice_fusion.5
  114.7 0.8 constant_dynamic-slice_fusion.3
  115.6 14.2 %all-to-all-done.3 = bf16[64,56,128]{2,1,0:T(8,128)(2,1)S(1)} async-done(((bf16[64,56,128]{2,1,0:T(8,128)(2,1)}), bf16[64,56,128]{2,1,0:T(8,128)(2,1)S(1)}, u32[]{:S(2)}, u32[]{:S(2)}) %all-to-all-start.3) | async-done | bytes 917536 | tf_op jit(solution)/shard_map/all_to_all | solution.py:26
  130.1 2.3 %collective-permute-start.7 = (bf16[1,3584]{1,0:T(2,128)(2,1)S(1)}, bf16[1,3584]{1,0:T(2,128)(2,1)S(1)}, u32[]{:S(2)}, u32[]{:S(2)}) collective-permute-start(bf16[1,3584]{1,0:T(2,128)(2,1)S(1)} %get-tuple-element.9), channel_id=1, source_target_pairs={{0,1},{1,0},{2,3},{3,2},{4,5},{5,4},{6,7},{7,6},{8,9},{9,8},{10,11... | collective-permute-start | bytes 21512 | tf_op jit(solution)/shard_map/ppermute | solution.py:22
  132.3 0.7 broadcast_select_fusion.1
  133.2 0.7 broadcast_select_fusion
  (65 shorter events, 6.8 us)
Async XLA Ops:
  0.6 6.8 %copy-start = (bf16[1,128,576]{1,2,0:T(8,128)(2,1)S(1)}, bf16[1,128,576]{1,2,0:T(8,128)(2,1)}, u32[]{:S(2)}) copy-start(bf16[1,128,576]{1,2,0:T(8,128)(2,1)} %param.14) | copy-start | bytes 442372
  0.6 8.5 %copy-start.7 = (bf16[1,576]{1,0:T(2,128)(2,1)S(1)}, bf16[1,576]{1,0:T(2,128)(2,1)}, u32[]{:S(2)}) copy-start(bf16[1,576]{1,0:T(2,128)(2,1)} %param.16) | copy-start | bytes 3460
  0.7 8.9 %copy-start.3 = (bf16[1,1024,576]{1,2,0:T(8,128)(2,1)S(1)}, bf16[1,1024,576]{1,2,0:T(8,128)(2,1)}, u32[]{:S(2)}) copy-start(bf16[1,1024,576]{1,2,0:T(8,128)(2,1)} %param.15) | copy-start | bytes 3538948
  0.7 9.5 %collective-permute-start = (bf16[1,7168]{1,0:T(2,128)(2,1)}, bf16[1,7168]{1,0:T(2,128)(2,1)S(1)}, u32[]{:S(2)}, u32[]{:S(2)}) collective-permute-start(bf16[1,7168]{1,0:T(2,128)(2,1)} %param.13), channel_id=1, source_target_pairs={{0,1},{1,0},{2,3},{3,2},{4,5},{5,4},{6,7},{7,6},{8,9},{9,8},{10,11... | collective-permute-start | bytes 43016 | tf_op jit(solution)/shard_map/ppermute | solution.py:22
  2.1 36.7 %collective-permute-start.3 = (bf16[128,7168]{1,0:T(8,128)(2,1)}, bf16[128,7168]{1,0:T(8,128)(2,1)S(1)}, u32[]{:S(2)}, u32[]{:S(2)}) collective-permute-start(bf16[128,7168]{1,0:T(8,128)(2,1)} %own_ref.1), channel_id=1, source_target_pairs={{0,1},{1,0},{2,3},{3,2},{4,5},{5,4},{6,7},{7,6},{8,9},{9,8},{10,11... | collective-permute-start | bytes 5505032 | tf_op jit(solution)/shard_map/ppermute | solution.py:22
  2.2 97.7 %collective-permute-start.6 = (bf16[384,7168]{1,0:T(8,128)(2,1)}, bf16[384,7168]{1,0:T(8,128)(2,1)}, u32[]{:S(2)}, u32[]{:S(2)}) collective-permute-start(bf16[384,7168]{1,0:T(8,128)(2,1)} %bitcast.81), channel_id=1, source_target_pairs={{0,1},{1,0},{2,3},{3,2},{4,5},{5,4},{6,7},{7,6},{8,9},{9,8},{10,11... | collective-permute-start | bytes 16515080 | tf_op jit(solution)/shard_map/ppermute | solution.py:22
  9.6 0.8 copy-start.8
  10.1 12.9 %copy-start.5 = (bf16[1,512,128]{2,1,0:T(8,128)(2,1)S(1)}, bf16[1,512,128]{2,1,0:T(8,128)(2,1)}, u32[]{:S(2)}) copy-start(bf16[1,512,128]{2,1,0:T(8,128)(2,1)} %param.18) | copy-start | bytes 393220
  11.8 22.1 %all-to-all-start = ((bf16[64,2,1536]{2,1,0:T(2,128)(2,1)}), bf16[64,2,1536]{2,1,0:T(2,128)(2,1)S(1)}, u32[]{:S(2)}, u32[]{:S(2)}) async-start(bf16[64,2,1536]{2,1,0:T(2,128)(2,1)} %pad_maximum_fusion), calls=%async_computation | async-start | bytes 786432 | tf_op jit(solution)/shard_map/all_to_all | solution.py:26
  23.1 11.9 %collective-permute-start.1 = (bf16[1,512,128]{2,1,0:T(8,128)(2,1)S(1)}, bf16[1,512,128]{2,1,0:T(8,128)(2,1)S(1)}, u32[]{:S(2)}, u32[]{:S(2)}) collective-permute-start(bf16[1,512,128]{2,1,0:T(8,128)(2,1)S(1)} %copy-done.5), channel_id=1, source_target_pairs={{0,1},{1,0},{2,3},{3,2},{4,5},{5,4},{6,7},{7,6},{8,9},{9,8},{10,11... | collective-permute-start | bytes 393224 | tf_op jit(solution)/shard_map/ppermute | solution.py:22
  35.2 2.8 %collective-permute-start.2 = (bf16[64,384]{1,0:T(8,128)(2,1)S(1)}, bf16[64,384]{1,0:T(8,128)(2,1)S(1)}, u32[]{:S(2)}, u32[]{:S(2)}) collective-permute-start(bf16[64,384]{1,0:T(8,128)(2,1)S(1)} %pad_maximum_fusion.2), channel_id=1, source_target_pairs={{0,1},{1,0},{2,3},{3,2},{4,5},{5,4},{6,7},{7,6},{8,9},{9,8},{10,11... | collective-permute-start | bytes 147464 | tf_op jit(solution)/shard_map/ppermute | solution.py:22
  38.9 1.3 copy-start.2
  44.2 20.6 %all-to-all-start.1 = ((bf16[64,8,896]{2,1,0:T(8,128)(2,1)}), bf16[64,8,896]{2,1,0:T(8,128)(2,1)S(1)}, u32[]{:S(2)}, u32[]{:S(2)}) async-start(bf16[64,8,896]{2,1,0:T(8,128)(2,1)} %bitcast.86), calls=%async_computation.1 | async-start | bytes 1835008 | tf_op jit(solution)/shard_map/all_to_all | solution.py:26
  84.9 5.1 %copy-start.1 = (bf16[64,8,896]{2,1,0:T(8,128)(2,1)}, bf16[64,8,896]{2,1,0:T(8,128)(2,1)S(1)}, u32[]{:S(2)}) copy-start(bf16[64,8,896]{2,1,0:T(8,128)(2,1)S(1)} %all_to_all.20) | copy-start | bytes 2752516
  84.9 5.1 %collective-permute-start.4 = (bf16[64,8,896]{2,1,0:T(8,128)(2,1)S(1)}, bf16[64,8,896]{2,1,0:T(8,128)(2,1)S(1)}, u32[]{:S(2)}, u32[]{:S(2)}) collective-permute-start(bf16[64,8,896]{2,1,0:T(8,128)(2,1)S(1)} %all_to_all.20), channel_id=1, source_target_pairs={{0,1},{1,0},{2,3},{3,2},{4,5},{5,4},{6,7},{7,6},{8,9},{9,8},{10,11... | collective-permute-start | bytes 2752520 | tf_op jit(solution)/shard_map/ppermute | solution.py:22
  90.0 0.9 copy-start.4
  98.4 1.5 %collective-permute-start.5 = (bf16[128,384]{1,0:T(8,128)(2,1)}, bf16[128,384]{1,0:T(8,128)(2,1)S(1)}, u32[]{:S(2)}, u32[]{:S(2)}) collective-permute-start(bf16[128,384]{1,0:T(8,128)(2,1)} %gate_up.1.act_own_ref), channel_id=1, source_target_pairs={{0,1},{1,0},{2,3},{3,2},{4,5},{5,4},{6,7},{7,6},{8,9},{9,8},{10,11... | collective-permute-start | bytes 294920 | tf_op jit(solution)/shard_map/ppermute | solution.py:22
  99.9 0.6 copy-start.6
  109.2 20.6 %all-to-all-start.3 = ((bf16[64,56,128]{2,1,0:T(8,128)(2,1)}), bf16[64,56,128]{2,1,0:T(8,128)(2,1)S(1)}, u32[]{:S(2)}, u32[]{:S(2)}) async-start(bf16[64,56,128]{2,1,0:T(8,128)(2,1)} %copy.39), calls=%async_computation.3 | async-start | bytes 1835008 | tf_op jit(solution)/shard_map/all_to_all | solution.py:26
  130.1 3.1 %collective-permute-start.7 = (bf16[1,3584]{1,0:T(2,128)(2,1)S(1)}, bf16[1,3584]{1,0:T(2,128)(2,1)S(1)}, u32[]{:S(2)}, u32[]{:S(2)}) collective-permute-start(bf16[1,3584]{1,0:T(2,128)(2,1)S(1)} %get-tuple-element.9), channel_id=1, source_target_pairs={{0,1},{1,0},{2,3},{3,2},{4,5},{5,4},{6,7},{7,6},{8,9},{9,8},{10,11... | collective-permute-start | bytes 21512 | tf_op jit(solution)/shard_map/ppermute | solution.py:22

commit v2 on v1

v2 whole, which is shorter than its diff:
```python
import jax
import jax.numpy as jnp
from jax import lax
from jax.experimental import pallas as pl
from jax.experimental.pallas import tpu as pltpu
from jax.sharding import Mesh, PartitionSpec as P

LAT = 512
ROPE = 64
VD = 128
NX, NZ, NY = 4, 4, 4
CHIPS = NX * NZ * NY
GROUPS = NX * NZ
CHIP_AXES = ("x", "z", "y")
ALL_AXES = ("x", "z", "y", "core")
SWAP = [(0, 1), (1, 0)]
BF = jnp.bfloat16
F32 = jnp.float32


def swap(value):
    return lax.ppermute(value, "core", SWAP)


def exchange(value):
    return lax.all_to_all(value, CHIP_AXES, split_axis=0, concat_axis=0, tiled=True)


def limit(mib):
    return pltpu.CompilerParams(vmem_limit_bytes=mib * 1024 * 1024)


SENT_ROWS = 24
ROUTE_ROW = 8
STATE_ROW = 9


def attend_kernel(
    length_ref, query_ref, cache_ref, newest_ref, states_ref, ids_ref, score_ref, sent_ref, latent_ref, pack_ref
):
    heads = query_ref.shape[1]
    positions = cache_ref.shape[1]
    lanes = 128
    softmax_scale = (VD + ROPE) ** (-0.5)
    contract_first = (((0,), (0,)), ((), ()))
    query = query_ref[...]
    cached = lax.dot_general(query, cache_ref[...], contract_first, preferred_element_type=F32)
    cached = cached * softmax_scale
    newest = newest_ref[...]
    newest_rows = jnp.broadcast_to(newest, (8, newest.shape[1]))
    own_score = lax.dot_general(
        query, newest_rows, (((0,), (1,)), ((), ())), preferred_element_type=F32
    )[:, :1]
    own_score = own_score * softmax_scale
    visible = lax.broadcasted_iota(jnp.int32, (heads, positions), 1) < length_ref[0]
    cached = jnp.where(visible, cached, -1e30)
    highest = jnp.maximum(jnp.max(cached, axis=1, keepdims=True), own_score)
    weights = jnp.where(visible, jnp.exp(cached - highest), 0.0)
    weight_own = jnp.exp(own_score - highest)
    denominator = jnp.sum(weights, axis=1, keepdims=True) + weight_own
    probs = (weights / denominator).astype(BF)
    prob_own = (weight_own / denominator).astype(BF).astype(F32)
    blended = lax.dot_general(
        probs, cache_ref[:LAT, :], (((1,), (1,)), ((), ())), preferred_element_type=F32
    )
    blended = blended + prob_own * newest[:, :LAT].astype(F32)
    for t in range(LAT // lanes):
        latent_ref[t] = blended[:, t * lanes : (t + 1) * lanes]

    pieces = states_ref[...].astype(F32)
    half = pieces.shape[1] // 2
    wide = half // NY
    tiles = wide // lanes
    for y in range(NY):
        for side in range(2):
            for t in range(tiles):
                at = side * half + y * wide + t * lanes
                row = y * SENT_ROWS + STATE_ROW + side * tiles + t
                pack_ref[row : row + 1, :] = pieces[:, at : at + lanes]
        pack_ref[(y + 1) * SENT_ROWS - 1 : (y + 1) * SENT_ROWS, :] = jnp.zeros((1, lanes), F32)
    first = pack_ref[: NY * SENT_ROWS, :]
    for g in range(1, GROUPS):
        pack_ref[g * NY * SENT_ROWS : (g + 1) * NY * SENT_ROWS, :] = first

    scores = score_ref[...]
    routes = (2.5 * scores / jnp.sum(scores, axis=1, keepdims=True)).astype(BF).astype(F32)
    ids = ids_ref[...]
    per_block = 3
    block = lax.broadcasted_iota(jnp.int32, (CHIPS, lanes), 0) // NY
    lane = lax.broadcasted_iota(jnp.int32, (CHIPS, lanes), 1)
    expert = jnp.where(lane < per_block, block * per_block + lane, -1)
    dense = jnp.zeros((CHIPS, lanes), F32)
    for k in range(ids.shape[1]):
        dense = dense + jnp.where(expert == ids[:, k : k + 1], routes[:, k : k + 1], 0.0)
    pack_ref[pl.ds(ROUTE_ROW, CHIPS, stride=SENT_ROWS), :] = dense

    for t in range(LAT // lanes):
        for j in range(2):
            piece = latent_ref[t, pl.ds(j, CHIPS, stride=2), :]
            pack_ref[pl.ds(2 * t + j, CHIPS, stride=SENT_ROWS), :] = piece
    sent_ref[...] = pack_ref[...].astype(BF).reshape(sent_ref.shape)


def attend_and_pack(lengths, queries, kv_cache, kv_new, states_in, expert_ids, route_scores):
    whole = pl.BlockSpec(memory_space=pltpu.VMEM)
    return pl.pallas_call(
        attend_kernel,
        in_specs=[pl.BlockSpec(memory_space=pltpu.SMEM)] + [whole] * 6,
        out_specs=whole,
        out_shape=jax.ShapeDtypeStruct((CHIPS, SENT_ROWS, 128), BF),
        scratch_shapes=[
            pltpu.VMEM((LAT // 128, queries.shape[1], 128), F32),
            pltpu.VMEM((CHIPS * SENT_ROWS, 128), F32),
        ],
        compiler_params=limit(24),
        name="attend",
    )(lengths, queries[0].T, kv_cache[0].T, kv_new, states_in, expert_ids, route_scores)


VALUE_ROWS = 3 * CHIPS + 32


def value_kernel(place_ref, got_ref, own_ref, other_ref, mine_ref, send_ref, rows_ref, state_ref):
    core = place_ref[0]
    group = place_ref[1]
    lanes = 128
    rows_ref[...] = got_ref[...].astype(F32).reshape(rows_ref.shape)

    def latent(j):
        pieces = [
            rows_ref[pl.ds(2 * t + j, CHIPS, stride=SENT_ROWS), :].astype(BF) for t in range(LAT // lanes)
        ]
        return jnp.concatenate(pieces, axis=1)

    first, second = latent(0), latent(1)
    latent_own = jnp.where(core == 0, first, second)
    latent_other = jnp.where(core == 0, second, first)
    value_own = jnp.dot(latent_own, own_ref[...], preferred_element_type=F32).astype(BF)
    value_other = jnp.dot(latent_other, other_ref[...], preferred_element_type=F32).astype(BF)
    routes = rows_ref[pl.ds(ROUTE_ROW, CHIPS, stride=SENT_ROWS), :].astype(BF)
    base = pl.multiple_of(group * (NY * SENT_ROWS), 8)
    tiles = 7
    for side in range(2):
        state_ref[side] = jnp.zeros(state_ref.shape[1:], F32)
    for y in range(NY):
        source = rows_ref[pl.ds(base + y * SENT_ROWS, SENT_ROWS), :]
        for side in range(2):
            at = STATE_ROW + side * tiles
            state_ref[side, 8 * y : 8 * y + tiles, :] = source[at : at + tiles, :]
    low, high = state_ref[0], state_ref[1]
    for ref, a, b in ((mine_ref, value_own, value_other), (send_ref, value_other, value_own)):
        ref[:CHIPS, :] = a
        ref[CHIPS : 2 * CHIPS, :] = b
        ref[2 * CHIPS : 3 * CHIPS, :] = routes
    mine_ref[3 * CHIPS :, :] = jnp.where(core == 0, low, high).astype(BF)
    send_ref[3 * CHIPS :, :] = jnp.where(core == 0, high, low).astype(BF)


def project_values(place, got, own, other):
    whole = pl.BlockSpec(memory_space=pltpu.VMEM)
    out = jax.ShapeDtypeStruct((VALUE_ROWS, 128), BF)
    return pl.pallas_call(
        value_kernel,
        in_specs=[pl.BlockSpec(memory_space=pltpu.SMEM)] + [whole] * 3,
        out_specs=(whole, whole),
        out_shape=(out, out),
        scratch_shapes=[
            pltpu.VMEM((CHIPS * SENT_ROWS, 128), F32),
            pltpu.VMEM((2, 32, 128), F32),
        ],
        compiler_params=limit(16),
        name="values",
    )(place, got, own, other)


def out_kernel(
    place_ref, mine_ref, got_ref, own_ref, other_ref, out_ref, route_ref, states_ref, rows_ref, values_ref
):
    step = pl.program_id(0)
    core = place_ref[0]
    lanes = 128

    @pl.when(step == 0)
    def _():
        mine = mine_ref[...].astype(F32)
        got = got_ref[...].astype(F32)
        even = jnp.where(core == 0, mine, got)
        odd = jnp.where(core == 0, got, mine)
        for part in range(3):
            rows = slice(part * CHIPS, (part + 1) * CHIPS)
            rows_ref[pl.ds(0, CHIPS, stride=2), :] = even[rows]
            rows_ref[pl.ds(1, CHIPS, stride=2), :] = odd[rows]
            if part < 2:
                values_ref[:, part * lanes : (part + 1) * lanes] = rows_ref[...].astype(BF)
            else:
                route_ref[...] = rows_ref[...]
        tiles = states_ref.shape[1] // lanes
        for y in range(NY):
            for t in range(tiles):
                at = 3 * CHIPS + 8 * y + t
                cols = slice(t * lanes, (t + 1) * lanes)
                states_ref[2 * y : 2 * y + 1, cols] = even[at : at + 1, :]
                states_ref[2 * y + 1 : 2 * y + 2, cols] = odd[at : at + 1, :]

    weights = jnp.concatenate([own_ref[...], other_ref[...]], axis=0)
    product = jnp.dot(values_ref[...], weights, preferred_element_type=F32)
    out_ref[...] = product.astype(BF).reshape(out_ref.shape)


def out_projection(place, mine, got, own, other):
    rows = 2 * CHIPS
    wide = own.shape[1] // 8
    spec = pl.BlockSpec((own.shape[0], wide), lambda y, c: (0, 4 * c[0] + y))
    value = pl.BlockSpec(mine.shape, lambda y, c: (0, 0))
    return pl.pallas_call(
        out_kernel,
        grid_spec=pltpu.PrefetchScalarGridSpec(
            num_scalar_prefetch=1,
            grid=(NY,),
            in_specs=[value, value, spec, spec],
            out_specs=(
                pl.BlockSpec((rows // 8, 1, 8, wide), lambda y, c: (0, y, 0, 0)),
                pl.BlockSpec((rows, 128), lambda y, c: (0, 0)),
                pl.BlockSpec((8, wide), lambda y, c: (0, 0)),
            ),
            scratch_shapes=[pltpu.VMEM((rows, 128), F32), pltpu.VMEM((rows, 2 * VD), BF)],
        ),
        out_shape=(
            jax.ShapeDtypeStruct((rows // 8, NY, 8, wide), BF),
            jax.ShapeDtypeStruct((rows, 128), F32),
            jax.ShapeDtypeStruct((8, wide), F32),
        ),
        compiler_params=limit(16),
        name="out_projection",
    )(place, mine, got, own, other)


def gate_up_kernel(
    core_ref, own_ref, other_ref, gain_ref, route_ref, gate_ref, up_ref, act_ref, inverse_ref, sum_ref
):
    del core_ref
    step = pl.program_id(0)
    rows = act_ref.shape[0]
    wide = own_ref.shape[-1]
    experts = gate_ref.shape[0]

    def part(ref, y):
        return ref[:, y].reshape(rows, wide)

    @pl.when(step == 0)
    def _():
        total = jnp.zeros((rows, 1), F32)
        for ref in (own_ref, other_ref):
            for y in range(NY):
                piece = part(ref, y).astype(F32)
                total = total + jnp.sum(piece * piece, axis=1, keepdims=True)
        inverse_ref[...] = lax.rsqrt(total / (8 * wide) + 1e-06)
        sum_ref[...] = jnp.zeros_like(sum_ref)

    def accumulate(ref, y):
        piece = jnp.concatenate([part(ref, y), part(ref, y + 1)], axis=1).astype(F32)
        normed = (piece * inverse_ref[...] * gain_ref[...]).astype(BF)
        for e in range(experts):
            weights = jnp.concatenate([gate_ref[e], up_ref[e]], axis=1)
            sum_ref[e] += jnp.dot(normed, weights, preferred_element_type=F32)

    for index, (ref, y) in enumerate(((own_ref, 0), (own_ref, 2), (other_ref, 0), (other_ref, 2))):
        pl.when(step == index)(lambda ref=ref, y=y: accumulate(ref, y))

    @pl.when(step == 3)
    def _():
        for e in range(experts):
            hidden = act_ref.shape[1] // experts
            gate = sum_ref[e, :, :hidden]
            up = sum_ref[e, :, hidden:]
            active = gate / (1.0 + jnp.exp(-gate)) * up
            active = active * route_ref[:, e : e + 1]
            act_ref[:, e * hidden : (e + 1) * hidden] = active.astype(BF)


def gate_up(core, own, other, gain, route, w_gate, w_up):
    groups, _, eight, wide = own.shape
    rows = groups * eight
    experts, model, hidden = w_gate.shape

    def block(step, c):
        half = jnp.where(step < 2, c[0], 1 - c[0])
        return 2 * half + step % 2

    weights = pl.BlockSpec((experts, 2 * wide, hidden), lambda s, c: (0, block(s, c), 0))
    whole = pl.BlockSpec(own.shape, lambda s, c: (0, 0, 0, 0))
    return pl.pallas_call(
        gate_up_kernel,
        grid_spec=pltpu.PrefetchScalarGridSpec(
            num_scalar_prefetch=1,
            grid=(4,),
            in_specs=[
                whole,
                whole,
                pl.BlockSpec((1, 2 * wide), lambda s, c: (0, block(s, c))),
                pl.BlockSpec(route.shape, lambda s, c: (0, 0)),
                weights,
                weights,
            ],
            out_specs=pl.BlockSpec((rows, experts * hidden), lambda s, c: (0, 0)),
            scratch_shapes=[
                pltpu.VMEM((rows, 1), F32),
                pltpu.VMEM((experts, rows, 2 * hidden), F32),
            ],
        ),
        out_shape=jax.ShapeDtypeStruct((rows, experts * hidden), BF),
        compiler_params=limit(24),
        name="gate_up",
    )(core, own, other, gain[None], route, w_gate, w_up)


def down_kernel(core_ref, act_own_ref, act_other_ref, own_ref, other_ref, out_ref, sum_ref, pack_ref):
    del core_ref
    step = pl.program_id(0)
    lanes = 128
    stride = out_ref.shape[1]
    act = jnp.concatenate([act_own_ref[...], act_other_ref[...]], axis=1)
    weights = jnp.concatenate([own_ref[...], other_ref[...]], axis=0)
    product = jnp.dot(act, weights, preferred_element_type=F32)
    tiles = weights.shape[1] // lanes
    for t in range(tiles):
        sum_ref[t] = product[:, t * lanes : (t + 1) * lanes]

    def place(y):
        for t in range(tiles):
            for j in range(2):
                piece = sum_ref[t, pl.ds(j, CHIPS, stride=2), :]
                pack_ref[pl.ds(2 * (y * tiles + t) + j, CHIPS, stride=stride), :] = piece

    for index in range(NY):
        pl.when(step == index)(lambda index=index: place(index))

    @pl.when(step == NY - 1)
    def _():
        out_ref[...] = pack_ref[...].astype(BF).reshape(out_ref.shape)


def down(core, act_own, act_other, own, other):
    rows = act_own.shape[0]
    wide = own.shape[1] // 8
    out_rows = 2 * NY * wide // 128
    act = pl.BlockSpec(act_own.shape, lambda y, c: (0, 0))
    spec = pl.BlockSpec((own.shape[0], wide), lambda y, c: (0, 4 * c[0] + y))
    return pl.pallas_call(
        down_kernel,
        grid_spec=pltpu.PrefetchScalarGridSpec(
            num_scalar_prefetch=1,
            grid=(NY,),
            in_specs=[act, act, spec, spec],
            out_specs=pl.BlockSpec((CHIPS, out_rows, 128), lambda y, c: (0, 0, 0)),
            scratch_shapes=[
                pltpu.VMEM((wide // 128, rows, 128), F32),
                pltpu.VMEM((CHIPS * out_rows, 128), F32),
            ],
        ),
        out_shape=jax.ShapeDtypeStruct((CHIPS, out_rows, 128), BF),
        compiler_params=limit(20),
        name="down",
    )(core, act_own, act_other, own, other)


def body(
    states_in,
    queries,
    kv_cache,
    kv_new,
    lengths,
    w_uv,
    w_out,
    norm_gain,
    expert_ids,
    route_scores,
    w_gate,
    w_up,
    w_down,
):
    core = lax.axis_index("core")
    group = lax.axis_index("x") * NZ + lax.axis_index("z")
    y_at = lax.axis_index("y")
    model = states_in.shape[1]
    half = model // 2
    wide = half // NY
    down_own = w_down.reshape(-1, model)
    uv_other = swap(w_uv)
    out_other = swap(w_out)
    down_other = swap(down_own)
    place = jnp.stack([core, group])

    sent = attend_and_pack(
        lengths, queries, kv_cache, kv_new, states_in, expert_ids, route_scores
    )
    got = exchange(sent)
    mine, send = project_values(place, got, w_uv[0], uv_other[0])
    partial, route, my_states = out_projection(place, mine, swap(send), w_out, out_other)
    partial = exchange(partial.reshape(CHIPS, 8, wide))
    attention = jnp.sum(partial.astype(F32), axis=0)
    residual_part = (my_states + attention).astype(BF)
    rows_own = exchange(jnp.broadcast_to(residual_part[None], (CHIPS, 8, wide)))
    rows_other = swap(rows_own)
    rows_own = rows_own.reshape(GROUPS, NY, 8, wide)
    rows_other = rows_other.reshape(GROUPS, NY, 8, wide)

    act = gate_up(place, rows_own, rows_other, norm_gain, route, w_gate, w_up)
    act_other = swap(act)
    output = down(place, act, act_other, down_own, down_other)
    output = exchange(output)
    expert_sum = jnp.sum(output.astype(F32), axis=0)
    expert_sum = expert_sum.reshape(half // 128, 2, 128).transpose(1, 0, 2).reshape(2, half)

    def chip_rows(rows):
        mine = lax.dynamic_index_in_dim(rows, group, 0, keepdims=False)
        mine = lax.dynamic_slice_in_dim(mine, 2 * y_at, 2, 1)
        return mine.transpose(1, 0, 2).reshape(2, half)

    residual_own = chip_rows(rows_own)
    residual_other = chip_rows(rows_other)
    layer_half = (residual_own.astype(F32) + expert_sum).astype(BF)
    layer_mine = lax.dynamic_slice_in_dim(layer_half, core, 1, 0)
    layer_got = swap(lax.dynamic_slice_in_dim(layer_half, 1 - core, 1, 0))
    residual_mine = lax.dynamic_slice_in_dim(residual_own, core, 1, 0)
    residual_got = lax.dynamic_slice_in_dim(residual_other, core, 1, 0)

    def joined(mine, got):
        return jnp.where(
            core == 0, jnp.concatenate([mine, got], axis=1), jnp.concatenate([got, mine], axis=1)
        )

    return (joined(residual_mine, residual_got), joined(layer_mine, layer_got))


def solution(mesh):
    fine = Mesh(mesh.devices.reshape(NX, NZ, NY, 2), ALL_AXES)
    rows = P(ALL_AXES, None)
    cube = P(ALL_AXES, None, None)
    in_specs = (
        rows,
        cube,
        cube,
        rows,
        P(ALL_AXES),
        cube,
        rows,
        P(),
        rows,
        rows,
        P(("x", "z"), None, ("y", "core")),
        P(("x", "z"), None, ("y", "core")),
        P(("x", "z"), ("y", "core"), None),
    )
    return jax.shard_map(body, mesh=fine, in_specs=in_specs, out_specs=(rows, rows), check_vma=False)
```

time: 135 us -> 123 us (0.911)
  blocking collectives: 19.9 us -> 40.3 us
  waiting for transfers between devices: 44.1 us -> 29.9 us
  other arithmetic: 7.24 us -> 1.76 us
  starting transfers between devices: 30.6 us -> 26 us
  local copies, waits for them, and re-layouts: 11.4 us -> 8.28 us
  matrix products: 2.7 us -> 0 us
  Pallas kernels: 16.4 us -> 14.3 us
    all_to_all x1 -> x2, blocking collectives: 19.9 us -> 40.3 us  [exchange(): lax.all_to_all(value, CHIP_AXES, split_axis=0, concat_axis=0, tiled=True)]
    all_to_all x3 -> x2, waiting for transfers between devices: 40.4 us -> 24.5 us  [exchange(): lax.all_to_all(value, CHIP_AXES, split_axis=0, concat_axis=0, tiled=True)]
    unnamed x21 -> x30, local copies, waits for them, and re-layouts: 3.05 us -> 8.08 us
    all_to_all x3 -> x2, starting transfers between devices: 20.5 us -> 15.9 us  [exchange(): lax.all_to_all(value, CHIP_AXES, split_axis=0, concat_axis=0, tiled=True)]
    reshape x3 -> x0, local copies, waits for them, and re-layouts: 3.2 us -> none  [the longest x1 1.62 us: body(): output = output.reshape(CHIPS, 2, half // 128, 128).transpose(0, 2, 1, 3)]
    pallas_call x1, Pallas kernels: 7.41 us -> 4.29 us  [gate_up(): pl.pallas_call(gate_up_kernel, grid_spec=pltpu.PrefetchScalarGridSpec(num...]
    dot_general x5 -> x0, matrix products: 2.7 us -> none  [the longest x1 1.76 us: attend(): jnp.einsum('rhc,rkc->rhk', queries, kv_cache, preferred_element_type=F32)]
    pallas_call x0 -> x2, Pallas kernels: none -> 2.53 us  [the longest x1 1.3 us: project_values(): pl.pallas_call(value_kernel, in_specs=[pl.BlockSpec(memory_space=pltpu.SM...]
  transfers between devices with their start and end apart: 11 -> 9, of which waited for: 7 -> 7; matrix products, arithmetic and copies ran while one was open for 10% -> 1% of each run, Pallas kernels for 9% -> 7%
where the time goes in v2:
time: 123 us; the launch traced here: 122 us
  blocking collectives  40.3 us (33%)
  waiting for transfers between devices  29.9 us (24%)
  starting transfers between devices  26 us (21%)
  Pallas kernels  14.3 us (12%)
  local copies, waits for them, and re-layouts  8.28 us (7%)
  other arithmetic  1.76 us (1%)
  between operations  1.46 us (1%)
    all_to_all x2, blocking collectives, exchange(): lax.all_to_all(value, CHIP_AXES, split_axis=0, concat_axis=0, tiled=True)  40.3 us
    all_to_all x2, waiting for transfers between devices, exchange(): lax.all_to_all(value, CHIP_AXES, split_axis=0, concat_axis=0, tiled=True)  24.5 us
    all_to_all x2, starting transfers between devices, exchange(): lax.all_to_all(value, CHIP_AXES, split_axis=0, concat_axis=0, tiled=True)  15.9 us
    ppermute x7, starting transfers between devices, swap(): return lax.ppermute(value, 'core', SWAP)  10.1 us
    unnamed x30, local copies, waits for them, and re-layouts  8.08 us
    pallas_call x1, Pallas kernels, down(): pl.pallas_call(down_kernel, grid_spec=pltpu.PrefetchScalarGridSpec(num_sc...  5.59 us
    ppermute x7, waiting for transfers between devices, swap(): return lax.ppermute(value, 'core', SWAP)  5.36 us
    pallas_call x1, Pallas kernels, gate_up(): pl.pallas_call(gate_up_kernel, grid_spec=pltpu.PrefetchScalarGridSpec(num...  4.29 us
  transfers between devices with their start and end apart: 9, of which 7 were waited for; matrix products, arithmetic and copies ran while one was open for 1% of the time, Pallas kernels for 7%

profile of v2, /device:TPU:1, one launch (start us, length us, event | category | flops | bytes accessed | tf_op | source)
XLA Modules:
  0.0 121.9 jit_solution(15090161996884570020)
XLA Ops:
  0.6 1.5 %collective-permute-start.5 = (bf16[384,7168]{1,0:T(8,128)(2,1)}, bf16[384,7168]{1,0:T(8,128)(2,1)}, u32[]{:S(2)}, u32[]{:S(2)}) collective-permute-start(bf16[384,7168]{1,0:T(8,128)(2,1)} %bitcast.32), channel_id=1, source_target_pairs={{0,1},{1,0},{2,3},{3,2},{4,5},{5,4},{6,7},{7,6},{8,9},{9,8},{10,11... | collective-permute-start | bytes 16515080 | tf_op jit(solution)/shard_map/ppermute | solution.py:22
  2.9 1.3 %copy-done.3 = bf16[1,1024,576]{1,2,0:T(8,128)(2,1)S(1)} copy-done((bf16[1,1024,576]{1,2,0:T(8,128)(2,1)S(1)}, bf16[1,1024,576]{1,2,0:T(8,128)(2,1)}, u32[]{:S(2)}) %copy-start.3) | copy-done | bytes 1179672
  4.1 0.9 copy-done.4
  5.0 0.7 copy-done.6
  5.8 0.7 copy-done.8
  6.5 0.7 copy-done.9
  7.1 0.7 copy-done.10
  7.8 1.2 %attend.1 = bf16[64,24,128]{2,1,0:T(8,128)(2,1)S(1)} custom-call(s32[1]{0:T(128)S(6)} %copy.15.length_ref, bf16[576,128]{1,0:T(8,128)(2,1)S(1)} %bitcast.42, bf16[576,1024]{1,0:T(8,128)(2,1)S(1)} %bitcast.38, bf16[1,576]{1,0:T(2,128)(2,1)S(1)} %copy-done.8, bf16[1,7168]{1,0:T(2,128)(2,1)S(1)} %copy-done.6, s32[1,8]{1,0:T(1,128)S(1)} %copy-done.9, ...), custom_call_target="tpu_custom_call" | custom-call | tf_op jit(solution)/shard_map/attend/pallas_call | solution.py:106
  9.0 0.7 copy-done.2
  9.7 11.2 %all-to-all-start = ((bf16[64,24,128]{2,1,0:T(8,128)(2,1)}), bf16[64,24,128]{2,1,0:T(8,128)(2,1)S(1)}, u32[]{:S(2)}, u32[]{:S(2)}) async-start(bf16[64,24,128]{2,1,0:T(8,128)(2,1)} %copy-done.2), calls=%async_computation | async-start | bytes 786432 | tf_op jit(solution)/shard_map/all_to_all | solution.py:26
  21.0 0.8 collective-permute-start
  21.8 1.3 %collective-permute-done = bf16[1,512,128]{2,1,0:T(8,128)(2,1)} collective-permute-done((bf16[1,512,128]{2,1,0:T(8,128)(2,1)}, bf16[1,512,128]{2,1,0:T(8,128)(2,1)}, u32[]{:S(2)}, u32[]{:S(2)}) %collective-permute-start) | collective-permute-done | bytes 131104 | tf_op jit(solution)/shard_map/ppermute | solution.py:22
  23.1 8.7 %all-to-all-done.got_ref = bf16[64,24,128]{2,1,0:T(8,128)(2,1)S(1)} async-done(((bf16[64,24,128]{2,1,0:T(8,128)(2,1)}), bf16[64,24,128]{2,1,0:T(8,128)(2,1)S(1)}, u32[]{:S(2)}, u32[]{:S(2)}) %all-to-all-start) | async-done | bytes 393248 | tf_op jit(solution)/shard_map/all_to_all | solution.py:26
  31.8 0.9 copy-done.5
  32.7 1.3 %values.1 = (bf16[224,128]{1,0:T(8,128)(2,1)S(1)}, bf16[224,128]{1,0:T(8,128)(2,1)S(1)}) custom-call(s32[2]{0:T(128)S(1)} %pad_add_fusion.place_ref.core_ref, bf16[64,24,128]{2,1,0:T(8,128)(2,1)S(1)} %all-to-all-done.got_ref, bf16[512,128]{1,0:T(8,128)(2,1)S(1)} %bitcast.43, bf16[512,128]{1,0:T(8,128)(2,1)} %bitcast.7.other_ref), custom_call_target="tpu_custom_call" | custom-call | tf_op jit(solution)/shard_map/values/pallas_call | solution.py:162
  34.0 2.0 %collective-permute-start.1 = (bf16[224,128]{1,0:T(8,128)(2,1)S(1)}, bf16[224,128]{1,0:T(8,128)(2,1)S(1)}, u32[]{:S(2)}, u32[]{:S(2)}) collective-permute-start(bf16[224,128]{1,0:T(8,128)(2,1)S(1)} %get-tuple-element.8), channel_id=1, source_target_pairs={{0,1},{1,0},{2,3},{3,2},{4,5},{5,4},{6,7},{7,6},{8,9},{9,8},{10,11... | collective-permute-start | bytes 172040 | tf_op jit(solution)/shard_map/ppermute | solution.py:22
  36.0 0.9 collective-permute-done.1.got_ref
  36.9 1.5 %copy-done.1 = bf16[128,7168]{1,0:T(8,128)(2,1)S(1)} copy-done((bf16[128,7168]{1,0:T(8,128)(2,1)S(1)}, bf16[128,7168]{1,0:T(8,128)(2,1)}, u32[]{:S(2)}) %copy-start.1) | copy-done | bytes 1835032
  38.4 1.9 %out_projection.1 = (bf16[16,4,8,896]{3,2,1,0:T(8,128)(2,1)S(1)}, f32[128,128]{1,0:T(8,128)S(1)}, f32[8,896]{1,0:T(8,128)S(1)}) custom-call(s32[2]{0:T(128)S(1)} %pad_add_fusion.place_ref.core_ref, bf16[224,128]{1,0:T(8,128)(2,1)S(1)} %get-tuple-element.7.mine_ref, bf16[224,128]{1,0:T(8,128)(2,1)S(1)} %collective-permute-done.1.got_ref, ...), custom_call_target="tpu_custom_call" | custom-call | tf_op jit(solution)/shard_map/out_projection/pallas_call | solution.py:215
  40.3 20.4 %all_to_all.20 = bf16[64,8,896]{2,1,0:T(8,128)(2,1)S(1)} all-to-all(bf16[64,8,896]{2,1,0:T(8,128)(2,1)S(1)} %bitcast.41), channel_id=1, replica_groups=mesh['x'=4,'z'=4,'y'=4,'core'=2] {'x','z','y'}, dimensions={0} | all-to-all | bytes 1835008 | tf_op jit(solution)/shard_map/all_to_all | solution.py:26
  61.0 19.9 %all_to_all.21 = bf16[64,8,896]{2,1,0:T(8,128)(2,1)S(1)} all-to-all(bf16[64,8,896]{2,1,0:T(8,128)(2,1)S(1)} %broadcast_in_dim.4), channel_id=1, replica_groups=mesh['x'=4,'z'=4,'y'=4,'core'=2] {'x','z','y'}, dimensions={0} | all-to-all | bytes 1835008 | tf_op jit(solution)/shard_map/all_to_all | solution.py:26
  80.9 3.0 %collective-permute-start.3 = (bf16[64,8,896]{2,1,0:T(8,128)(2,1)S(1)}, bf16[64,8,896]{2,1,0:T(8,128)(2,1)S(1)}, u32[]{:S(2)}, u32[]{:S(2)}) collective-permute-start(bf16[64,8,896]{2,1,0:T(8,128)(2,1)S(1)} %all_to_all.21), channel_id=1, source_target_pairs={{0,1},{1,0},{2,3},{3,2},{4,5},{5,4},{6,7},{7,6},{8,9},{9,8},{10,11... | collective-permute-start | bytes 2752520 | tf_op jit(solution)/shard_map/ppermute | solution.py:22
  83.9 2.1 %collective-permute-done.3 = bf16[64,8,896]{2,1,0:T(8,128)(2,1)S(1)} collective-permute-done((bf16[64,8,896]{2,1,0:T(8,128)(2,1)S(1)}, bf16[64,8,896]{2,1,0:T(8,128)(2,1)S(1)}, u32[]{:S(2)}, u32[]{:S(2)}) %collective-permute-start.3) | collective-permute-done | bytes 917536 | tf_op jit(solution)/shard_map/ppermute | solution.py:22
  86.0 4.3 %gate_up.1.act_own_ref = bf16[128,384]{1,0:T(8,128)(2,1)S(1)} custom-call(s32[2]{0:T(128)S(1)} %pad_add_fusion.place_ref.core_ref, bf16[16,4,8,896]{3,2,1,0:T(8,128)(2,1)S(1)} %bitcast.36, bf16[16,4,8,896]{3,2,1,0:T(8,128)(2,1)S(1)} %bitcast.39, f32[1,7168]{1,0:T(1,128)S(1)} %bitcast.44, f32[128,128]{1,0:T(8,128)S(1)} %get-tuple-element.11.route_ref, ...), custom_call_target="tpu_custom_call" | custom-call | tf_op jit(solution)/shard_map/gate_up/pallas_call | solution.py:292
  90.3 0.5 collective-permute-start.4
  90.8 0.9 collective-permute-done.4.act_other_ref
  91.7 5.6 %down.1 = bf16[64,56,128]{2,1,0:T(8,128)(2,1)} custom-call(s32[2]{0:T(128)S(1)} %pad_add_fusion.place_ref.core_ref, bf16[128,384]{1,0:T(8,128)(2,1)S(1)} %gate_up.1.act_own_ref, bf16[128,384]{1,0:T(8,128)(2,1)S(1)} %collective-permute-done.4.act_other_ref, bf16[384,7168]{1,0:T(8,128)(2,1)S(1)} %bitcast.35, bf16[384,7168]{1,0:T(8,128)(2,1)} %collective-permute-done.5.other_ref), custom_call_target="tpu_custom_call" | custom-call | tf_op jit(solution)/shard_map/down/pallas_call | solution.py:349
  97.3 4.6 %all-to-all-start.3 = ((bf16[64,56,128]{2,1,0:T(8,128)(2,1)}), bf16[64,56,128]{2,1,0:T(8,128)(2,1)S(1)}, u32[]{:S(2)}, u32[]{:S(2)}) async-start(bf16[64,56,128]{2,1,0:T(8,128)(2,1)} %down.1), calls=%async_computation.3 | async-start | bytes 1835008 | tf_op jit(solution)/shard_map/all_to_all | solution.py:26
  102.1 15.9 %all-to-all-done.3 = bf16[64,56,128]{2,1,0:T(8,128)(2,1)S(1)} async-done(((bf16[64,56,128]{2,1,0:T(8,128)(2,1)}), bf16[64,56,128]{2,1,0:T(8,128)(2,1)S(1)}, u32[]{:S(2)}, u32[]{:S(2)}) %all-to-all-start.3) | async-done | bytes 917536 | tf_op jit(solution)/shard_map/all_to_all | solution.py:26
  118.2 2.2 %collective-permute-start.6 = (bf16[1,3584]{1,0:T(2,128)(2,1)S(1)}, bf16[1,3584]{1,0:T(2,128)(2,1)S(1)}, u32[]{:S(2)}, u32[]{:S(2)}) collective-permute-start(bf16[1,3584]{1,0:T(2,128)(2,1)S(1)} %get-tuple-element.13), channel_id=1, source_target_pairs={{0,1},{1,0},{2,3},{3,2},{4,5},{5,4},{6,7},{7,6},{8,9},{9,8},{10,11... | collective-permute-start | bytes 21512 | tf_op jit(solution)/shard_map/ppermute | solution.py:22
  120.4 0.7 broadcast_select_fusion.1
  121.3 0.7 broadcast_select_fusion
  (37 shorter events, 0.9 us)
Async XLA Ops:
  0.6 91.1 %collective-permute-start.5 = (bf16[384,7168]{1,0:T(8,128)(2,1)}, bf16[384,7168]{1,0:T(8,128)(2,1)}, u32[]{:S(2)}, u32[]{:S(2)}) collective-permute-start(bf16[384,7168]{1,0:T(8,128)(2,1)} %bitcast.32), channel_id=1, source_target_pairs={{0,1},{1,0},{2,3},{3,2},{4,5},{5,4},{6,7},{7,6},{8,9},{9,8},{10,11... | collective-permute-start | bytes 16515080 | tf_op jit(solution)/shard_map/ppermute | solution.py:22
  2.1 34.8 %collective-permute-start.2 = (bf16[128,7168]{1,0:T(8,128)(2,1)}, bf16[128,7168]{1,0:T(8,128)(2,1)S(1)}, u32[]{:S(2)}, u32[]{:S(2)}) collective-permute-start(bf16[128,7168]{1,0:T(8,128)(2,1)} %own_ref.1), channel_id=1, source_target_pairs={{0,1},{1,0},{2,3},{3,2},{4,5},{5,4},{6,7},{7,6},{8,9},{9,8},{10,11... | collective-permute-start | bytes 5505032 | tf_op jit(solution)/shard_map/ppermute | solution.py:22
  2.8 1.3 %copy-start.3 = (bf16[1,1024,576]{1,2,0:T(8,128)(2,1)S(1)}, bf16[1,1024,576]{1,2,0:T(8,128)(2,1)}, u32[]{:S(2)}) copy-start(bf16[1,1024,576]{1,2,0:T(8,128)(2,1)} %param.15) | copy-start | bytes 3538948
  4.1 0.9 copy-start.4
  5.0 0.7 copy-start.6
  5.8 0.7 copy-start.8
  6.5 0.7 copy-start.9
  7.1 0.7 copy-start.10
  7.8 78.2 %slice-start = ((s8[5505024]{0:T(1024)(128)(4,1)}), s8[1310720]{0:T(1024)(128)(4,1)S(1)}, s32[]{:S(2)}) async-start(s8[5505024]{0:T(1024)(128)(4,1)} %bitcast.30), calls=%async_computation.4 | async-start | bytes 2621440
  9.0 0.7 copy-start.2
  9.7 22.0 %all-to-all-start = ((bf16[64,24,128]{2,1,0:T(8,128)(2,1)}), bf16[64,24,128]{2,1,0:T(8,128)(2,1)S(1)}, u32[]{:S(2)}, u32[]{:S(2)}) async-start(bf16[64,24,128]{2,1,0:T(8,128)(2,1)} %copy-done.2), calls=%async_computation | async-start | bytes 786432 | tf_op jit(solution)/shard_map/all_to_all | solution.py:26
  21.0 2.1 %collective-permute-start = (bf16[1,512,128]{2,1,0:T(8,128)(2,1)}, bf16[1,512,128]{2,1,0:T(8,128)(2,1)}, u32[]{:S(2)}, u32[]{:S(2)}) collective-permute-start(bf16[1,512,128]{2,1,0:T(8,128)(2,1)} %param.18), channel_id=1, source_target_pairs={{0,1},{1,0},{2,3},{3,2},{4,5},{5,4},{6,7},{7,6},{8,9},{9,8},{10,11... | collective-permute-start | bytes 393224 | tf_op jit(solution)/shard_map/ppermute | solution.py:22
  31.8 0.9 copy-start.5
  32.7 53.3 %copy-start = (bf16[3,7168,128]{2,1,0:T(8,128)(2,1)S(1)}, bf16[3,7168,128]{2,1,0:T(8,128)(2,1)}, u32[]{:S(2)}) copy-start(bf16[3,7168,128]{2,1,0:T(8,128)(2,1)} %up_ref.1) | copy-start | bytes 16515076
  34.0 2.9 %collective-permute-start.1 = (bf16[224,128]{1,0:T(8,128)(2,1)S(1)}, bf16[224,128]{1,0:T(8,128)(2,1)S(1)}, u32[]{:S(2)}, u32[]{:S(2)}) collective-permute-start(bf16[224,128]{1,0:T(8,128)(2,1)S(1)} %get-tuple-element.8), channel_id=1, source_target_pairs={{0,1},{1,0},{2,3},{3,2},{4,5},{5,4},{6,7},{7,6},{8,9},{9,8},{10,11... | collective-permute-start | bytes 172040 | tf_op jit(solution)/shard_map/ppermute | solution.py:22
  36.9 1.5 %copy-start.1 = (bf16[128,7168]{1,0:T(8,128)(2,1)S(1)}, bf16[128,7168]{1,0:T(8,128)(2,1)}, u32[]{:S(2)}) copy-start(bf16[128,7168]{1,0:T(8,128)(2,1)} %own_ref.1) | copy-start | bytes 5505028
  38.4 47.6 %slice-start.1 = ((s8[5505024]{0:T(1024)(128)(4,1)}), s8[4194304]{0:T(1024)(128)(4,1)S(1)}, s32[]{:S(2)}) async-start(s8[5505024]{0:T(1024)(128)(4,1)} %bitcast.30), calls=%async_computation.5 | async-start | bytes 8388608
  60.8 25.2 %copy-start.7 = (f32[7168]{0:T(1024)S(1)}, f32[7168]{0:T(1024)}, u32[]{:S(2)}) copy-start(f32[7168]{0:T(1024)} %param.20) | copy-start | bytes 86020
  80.9 5.1 %collective-permute-start.3 = (bf16[64,8,896]{2,1,0:T(8,128)(2,1)S(1)}, bf16[64,8,896]{2,1,0:T(8,128)(2,1)S(1)}, u32[]{:S(2)}, u32[]{:S(2)}) collective-permute-start(bf16[64,8,896]{2,1,0:T(8,128)(2,1)S(1)} %all_to_all.21), channel_id=1, source_target_pairs={{0,1},{1,0},{2,3},{3,2},{4,5},{5,4},{6,7},{7,6},{8,9},{9,8},{10,11... | collective-permute-start | bytes 2752520 | tf_op jit(solution)/shard_map/ppermute | solution.py:22
  86.0 5.7 %slice-start.2 = ((s8[5505024]{0:T(1024)(128)(4,1)}), s8[4194304]{0:T(1024)(128)(4,1)S(1)}, s32[]{:S(2)}) async-start(s8[5505024]{0:T(1024)(128)(4,1)} %bitcast.33), calls=%async_computation.6 | async-start | bytes 8388608
  86.0 5.7 %slice-start.3 = ((s8[5505024]{0:T(1024)(128)(4,1)}), s8[1310720]{0:T(1024)(128)(4,1)S(1)}, s32[]{:S(2)}) async-start(s8[5505024]{0:T(1024)(128)(4,1)} %bitcast.33), calls=%async_computation.7 | async-start | bytes 2621440
  90.3 1.4 %collective-permute-start.4 = (bf16[128,384]{1,0:T(8,128)(2,1)S(1)}, bf16[128,384]{1,0:T(8,128)(2,1)S(1)}, u32[]{:S(2)}, u32[]{:S(2)}) collective-permute-start(bf16[128,384]{1,0:T(8,128)(2,1)S(1)} %gate_up.1.act_own_ref), channel_id=1, source_target_pairs={{0,1},{1,0},{2,3},{3,2},{4,5},{5,4},{6,7},{7,6},{8,9},{9,8},{10,11... | collective-permute-start | bytes 294920 | tf_op jit(solution)/shard_map/ppermute | solution.py:22
  97.3 20.7 %all-to-all-start.3 = ((bf16[64,56,128]{2,1,0:T(8,128)(2,1)}), bf16[64,56,128]{2,1,0:T(8,128)(2,1)S(1)}, u32[]{:S(2)}, u32[]{:S(2)}) async-start(bf16[64,56,128]{2,1,0:T(8,128)(2,1)} %down.1), calls=%async_computation.3 | async-start | bytes 1835008 | tf_op jit(solution)/shard_map/all_to_all | solution.py:26
  118.2 3.1 %collective-permute-start.6 = (bf16[1,3584]{1,0:T(2,128)(2,1)S(1)}, bf16[1,3584]{1,0:T(2,128)(2,1)S(1)}, u32[]{:S(2)}, u32[]{:S(2)}) collective-permute-start(bf16[1,3584]{1,0:T(2,128)(2,1)S(1)} %get-tuple-element.13), channel_id=1, source_target_pairs={{0,1},{1,0},{2,3},{3,2},{4,5},{5,4},{6,7},{7,6},{8,9},{9,8},{10,11... | collective-permute-start | bytes 21512 | tf_op jit(solution)/shard_map/ppermute | solution.py:22

commit v3 on v2

v3 whole, which is shorter than its diff:
```python
import jax
import jax.numpy as jnp
from jax import lax
from jax.experimental import pallas as pl
from jax.experimental.pallas import tpu as pltpu
from jax.sharding import Mesh, PartitionSpec as P

LAT = 512
ROPE = 64
VD = 128
NX, NZ, NY = 4, 4, 4
QUARTERS = NZ
CHIPS = NX * NZ * NY
GROUPS = NX * NZ
CHIP_AXES = ("x", "y", "z")
ALL_AXES = ("x", "z", "y", "core")
SWAP = [(0, 1), (1, 0)]
BF = jnp.bfloat16
F32 = jnp.float32


def swap(value):
    return lax.ppermute(value, "core", SWAP)


def exchange(value):
    return lax.all_to_all(value, CHIP_AXES, split_axis=0, concat_axis=0, tiled=True)


def limit(mib):
    return pltpu.CompilerParams(vmem_limit_bytes=mib * 1024 * 1024)


SENT_ROWS = 24
ROUTE_ROW = 8
STATE_ROW = 9


def attend_kernel(
    length_ref,
    query_hbm,
    cache_hbm,
    newest_hbm,
    states_hbm,
    ids_hbm,
    score_hbm,
    sent_ref,
    query_ref,
    cache_ref,
    newest_ref,
    states_ref,
    ids_ref,
    score_ref,
    latent_ref,
    pack_ref,
    done,
):
    copies = [
        pltpu.make_async_copy(source, target, done.at[index])
        for index, (source, target) in enumerate(
            (
                (cache_hbm, cache_ref),
                (query_hbm, query_ref),
                (newest_hbm, newest_ref),
                (states_hbm, states_ref),
                (ids_hbm, ids_ref),
                (score_hbm, score_ref),
            )
        )
    ]
    for copy in copies:
        copy.start()
    for copy in copies[3:]:
        copy.wait()
    lanes = 128
    pieces = states_ref[...].astype(F32)
    half = pieces.shape[1] // 2
    wide = half // QUARTERS
    tiles = wide // lanes
    for y in range(NY):
        for side in range(2):
            for t in range(tiles):
                at = side * half + y * wide + t * lanes
                row = y * SENT_ROWS + STATE_ROW + side * tiles + t
                pack_ref[row : row + 1, :] = pieces[:, at : at + lanes]
        pack_ref[(y + 1) * SENT_ROWS - 1 : (y + 1) * SENT_ROWS, :] = jnp.zeros((1, lanes), F32)
    first = pack_ref[: NY * SENT_ROWS, :]
    for g in range(1, GROUPS):
        pack_ref[g * NY * SENT_ROWS : (g + 1) * NY * SENT_ROWS, :] = first

    scores = score_ref[...]
    routes = (2.5 * scores / jnp.sum(scores, axis=1, keepdims=True)).astype(BF).astype(F32)
    ids = ids_ref[...]
    per_block = 3
    chip = lax.broadcasted_iota(jnp.int32, (CHIPS, lanes), 0)
    block = chip // (NY * NZ) * NZ + chip % NZ
    lane = lax.broadcasted_iota(jnp.int32, (CHIPS, lanes), 1)
    expert = jnp.where(lane < per_block, block * per_block + lane, -1)
    dense = jnp.zeros((CHIPS, lanes), F32)
    for k in range(ids.shape[1]):
        dense = dense + jnp.where(expert == ids[:, k : k + 1], routes[:, k : k + 1], 0.0)
    pack_ref[pl.ds(ROUTE_ROW, CHIPS, stride=SENT_ROWS), :] = dense

    for copy in copies[:3]:
        copy.wait()
    heads = query_ref.shape[1]
    positions = cache_ref.shape[1]
    softmax_scale = (VD + ROPE) ** (-0.5)
    contract_first = (((0,), (0,)), ((), ()))
    query = query_ref[...]
    cached = lax.dot_general(query, cache_ref[...], contract_first, preferred_element_type=F32)
    cached = cached * softmax_scale
    newest = newest_ref[...]
    newest_rows = jnp.broadcast_to(newest, (8, newest.shape[1]))
    own_score = lax.dot_general(
        query, newest_rows, (((0,), (1,)), ((), ())), preferred_element_type=F32
    )[:, :1]
    own_score = own_score * softmax_scale
    visible = lax.broadcasted_iota(jnp.int32, (heads, positions), 1) < length_ref[0]
    cached = jnp.where(visible, cached, -1e30)
    highest = jnp.maximum(jnp.max(cached, axis=1, keepdims=True), own_score)
    weights = jnp.where(visible, jnp.exp(cached - highest), 0.0)
    weight_own = jnp.exp(own_score - highest)
    denominator = jnp.sum(weights, axis=1, keepdims=True) + weight_own
    probs = (weights / denominator).astype(BF)
    prob_own = (weight_own / denominator).astype(BF).astype(F32)
    blended = lax.dot_general(
        probs, cache_ref[:LAT, :], (((1,), (1,)), ((), ())), preferred_element_type=F32
    )
    blended = blended + prob_own * newest[:, :LAT].astype(F32)
    for t in range(LAT // lanes):
        latent_ref[t] = blended[:, t * lanes : (t + 1) * lanes]

    for x in range(NX):
        for y in range(NY):
            head = 2 * (x * NZ * NY + y)
            row = (x * NY + y) * NZ * SENT_ROWS
            for t in range(LAT // lanes):
                for j in range(2):
                    piece = latent_ref[t, pl.ds(head + j, NZ, stride=2 * NY), :]
                    pack_ref[pl.ds(row + 2 * t + j, NZ, stride=SENT_ROWS), :] = piece
    sent_ref[...] = pack_ref[...].astype(BF).reshape(sent_ref.shape)


def attend_and_pack(lengths, queries, kv_cache, kv_new, states_in, expert_ids, route_scores):
    whole = pl.BlockSpec(memory_space=pltpu.VMEM)
    inputs = (queries[0].T, kv_cache[0].T, kv_new, states_in, expert_ids, route_scores)
    return pl.pallas_call(
        attend_kernel,
        in_specs=[pl.BlockSpec(memory_space=pltpu.SMEM)]
        + [pl.BlockSpec(memory_space=pltpu.HBM)] * len(inputs),
        out_specs=whole,
        out_shape=jax.ShapeDtypeStruct((CHIPS, SENT_ROWS, 128), BF),
        scratch_shapes=[pltpu.VMEM(value.shape, value.dtype) for value in inputs]
        + [
            pltpu.VMEM((LAT // 128, queries.shape[1], 128), F32),
            pltpu.VMEM((CHIPS * SENT_ROWS, 128), F32),
            pltpu.SemaphoreType.DMA((len(inputs),)),
        ],
        compiler_params=limit(62),
        name="attend",
    )(lengths, *inputs)


VALUE_ROWS = 3 * CHIPS + 32


def value_kernel(
    place_ref,
    got_ref,
    uv_own_hbm,
    uv_other_hbm,
    out_own_hbm,
    out_other_hbm,
    mine_ref,
    send_ref,
    weights_ref,
    own_ref,
    other_ref,
    rows_ref,
    state_ref,
    done,
):
    core = place_ref[0]
    heads = out_own_hbm.shape[0]
    half = weights_ref.shape[1]
    columns = pl.ds(pl.multiple_of(core * half, 128), half)
    copies = [
        pltpu.make_async_copy(source, target, done.at[index])
        for index, (source, target) in enumerate(
            (
                (uv_own_hbm, own_ref),
                (uv_other_hbm, other_ref),
                (out_own_hbm.at[:, columns], weights_ref.at[:heads]),
                (out_other_hbm.at[:, columns], weights_ref.at[heads:]),
            )
        )
    ]
    for copy in copies:
        copy.start()
    group = place_ref[1]
    lanes = 128
    rows_ref[...] = got_ref[...].astype(F32).reshape(rows_ref.shape)

    def latent(j):
        pieces = [
            rows_ref[pl.ds(2 * t + j, CHIPS, stride=SENT_ROWS), :].astype(BF) for t in range(LAT // lanes)
        ]
        return jnp.concatenate(pieces, axis=1)

    first, second = latent(0), latent(1)
    latent_own = jnp.where(core == 0, first, second)
    latent_other = jnp.where(core == 0, second, first)
    copies[0].wait()
    copies[1].wait()
    value_own = jnp.dot(latent_own, own_ref[...], preferred_element_type=F32).astype(BF)
    value_other = jnp.dot(latent_other, other_ref[...], preferred_element_type=F32).astype(BF)
    routes = rows_ref[pl.ds(ROUTE_ROW, CHIPS, stride=SENT_ROWS), :].astype(BF)
    base = pl.multiple_of(group * (NY * SENT_ROWS), 8)
    tiles = 7
    for side in range(2):
        state_ref[side] = jnp.zeros(state_ref.shape[1:], F32)
    for y in range(NY):
        source = rows_ref[pl.ds(base + y * SENT_ROWS, SENT_ROWS), :]
        for side in range(2):
            at = STATE_ROW + side * tiles
            state_ref[side, 8 * y : 8 * y + tiles, :] = source[at : at + tiles, :]
    low, high = state_ref[0], state_ref[1]
    for ref, a, b in ((mine_ref, value_own, value_other), (send_ref, value_other, value_own)):
        ref[:CHIPS, :] = a
        ref[CHIPS : 2 * CHIPS, :] = b
        ref[2 * CHIPS : 3 * CHIPS, :] = routes
    mine_ref[3 * CHIPS :, :] = jnp.where(core == 0, low, high).astype(BF)
    send_ref[3 * CHIPS :, :] = jnp.where(core == 0, high, low).astype(BF)
    copies[2].wait()
    copies[3].wait()


def project_values(place, got, uv_own, uv_other, out_own, out_other):
    whole = pl.BlockSpec(memory_space=pltpu.VMEM)
    outside = pl.BlockSpec(memory_space=pltpu.HBM)
    out = jax.ShapeDtypeStruct((VALUE_ROWS, 128), BF)
    heads, model = out_own.shape
    return pl.pallas_call(
        value_kernel,
        in_specs=[pl.BlockSpec(memory_space=pltpu.SMEM), whole] + [outside] * 4,
        out_specs=(whole, whole, whole),
        out_shape=(out, out, jax.ShapeDtypeStruct((2 * heads, model // 2), BF)),
        scratch_shapes=[
            pltpu.VMEM(uv_own.shape, BF),
            pltpu.VMEM(uv_own.shape, BF),
            pltpu.VMEM((CHIPS * SENT_ROWS, 128), F32),
            pltpu.VMEM((2, 32, 128), F32),
            pltpu.SemaphoreType.DMA((4,)),
        ],
        compiler_params=limit(12),
        name="values",
    )(place, got, uv_own, uv_other, out_own, out_other)


def out_kernel(
    place_ref, mine_ref, got_ref, weights_ref, out_ref, route_ref, states_ref, rows_ref, values_ref
):
    core = place_ref[0]
    lanes = 128
    mine = mine_ref[...].astype(F32)
    got = got_ref[...].astype(F32)
    even = jnp.where(core == 0, mine, got)
    odd = jnp.where(core == 0, got, mine)
    for part in range(3):
        rows = slice(part * CHIPS, (part + 1) * CHIPS)
        rows_ref[part, pl.ds(0, CHIPS, stride=2), :] = even[rows]
        rows_ref[part, pl.ds(1, CHIPS, stride=2), :] = odd[rows]
        if part < 2:
            values_ref[:, part * lanes : (part + 1) * lanes] = rows_ref[part].astype(BF)
        else:
            route_ref[...] = rows_ref[part]
    wide = states_ref.shape[1]
    for q in range(QUARTERS):
        for t in range(wide // lanes):
            at = 3 * CHIPS + 8 * q + t
            cols = slice(t * lanes, (t + 1) * lanes)
            states_ref[2 * q : 2 * q + 1, cols] = even[at : at + 1, :]
            states_ref[2 * q + 1 : 2 * q + 2, cols] = odd[at : at + 1, :]
    values = values_ref[...]
    groups = out_ref.shape[0]
    for q in range(QUARTERS):
        product = jnp.dot(values, weights_ref[:, q * wide : (q + 1) * wide], preferred_element_type=F32)
        out_ref[:, q] = product.astype(BF).reshape(groups, 8, wide)


def out_projection(place, mine, got, weights):
    rows = 2 * CHIPS
    wide = weights.shape[1] // QUARTERS
    whole = pl.BlockSpec(memory_space=pltpu.VMEM)
    return pl.pallas_call(
        out_kernel,
        in_specs=[pl.BlockSpec(memory_space=pltpu.SMEM), whole, whole, whole],
        out_specs=(whole, whole, whole),
        out_shape=(
            jax.ShapeDtypeStruct((rows // 8, QUARTERS, 8, wide), BF),
            jax.ShapeDtypeStruct((rows, 128), F32),
            jax.ShapeDtypeStruct((8, wide), F32),
        ),
        scratch_shapes=[pltpu.VMEM((3, rows, 128), F32), pltpu.VMEM((rows, 2 * VD), BF)],
        compiler_params=limit(12),
        name="out_projection",
    )(place, mine, got, weights)


def half_products(half, rows_ref, gain_ref, gate_ref, up_ref):
    groups, quarters, eight, wide = rows_ref.shape
    rows = groups * eight
    experts = gate_ref.shape[0]
    total = jnp.zeros((rows, 1), F32)
    sums = [None] * experts
    for pair in range(quarters // 2):
        pieces = [rows_ref[:, q].reshape(rows, wide) for q in (2 * pair, 2 * pair + 1)]
        piece = jnp.concatenate(pieces, axis=1).astype(F32)
        total = total + jnp.sum(piece * piece, axis=1, keepdims=True)
        at = pl.ds(pl.multiple_of(half * (quarters * wide) + pair * (2 * wide), 256), 2 * wide)
        scaled = (piece * gain_ref[:, at]).astype(BF)
        for e in range(experts):
            weights = jnp.concatenate([gate_ref[e, at, :], up_ref[e, at, :]], axis=1)
            product = jnp.dot(scaled, weights, preferred_element_type=F32)
            sums[e] = product if sums[e] is None else sums[e] + product
    return total, sums


def first_kernel(place_ref, rows_ref, gain_ref, gate_ref, up_ref, total_ref, sums_ref):
    total, sums = half_products(place_ref[0], rows_ref, gain_ref, gate_ref, up_ref)
    total_ref[...] = jnp.broadcast_to(total, total_ref.shape)
    for e, value in enumerate(sums):
        sums_ref[e] = value


def second_kernel(
    place_ref, rows_ref, gain_ref, gate_ref, up_ref, total_ref, sums_ref, route_ref, act_ref
):
    total, sums = half_products(1 - place_ref[0], rows_ref, gain_ref, gate_ref, up_ref)
    total = total + total_ref[:, :1]
    inverse = lax.rsqrt(total / gain_ref.shape[1] + 1e-06)
    hidden = gate_ref.shape[2]
    for e, value in enumerate(sums):
        value = (value + sums_ref[e]) * inverse
        gate = value[:, :hidden]
        active = gate / (1.0 + jnp.exp(-gate)) * value[:, hidden:]
        active = active * route_ref[:, e : e + 1]
        act_ref[:, e * hidden : (e + 1) * hidden] = active.astype(BF)


def gate_up(place, own, other, gain, route, w_gate, w_up):
    groups, _, eight, wide = own.shape
    rows = groups * eight
    experts, model, hidden = w_gate.shape
    whole = pl.BlockSpec(memory_space=pltpu.VMEM)
    where = pl.BlockSpec(memory_space=pltpu.SMEM)
    total, sums = pl.pallas_call(
        first_kernel,
        in_specs=[where] + [whole] * 4,
        out_specs=(whole, whole),
        out_shape=(
            jax.ShapeDtypeStruct((rows, 128), F32),
            jax.ShapeDtypeStruct((experts, rows, 2 * hidden), F32),
        ),
        compiler_params=limit(12),
        name="gate_up_first",
    )(place, own, gain[None], w_gate, w_up)
    return pl.pallas_call(
        second_kernel,
        in_specs=[where] + [whole] * 7,
        out_specs=whole,
        out_shape=jax.ShapeDtypeStruct((rows, experts * hidden), BF),
        compiler_params=limit(12),
        name="gate_up_second",
    )(place, other, gain[None], w_gate, w_up, total, sums, route)


DOWN_COLUMNS = 512


def down_kernel(place_ref, act_own_ref, act_other_ref, own_ref, other_ref, out_ref, sum_ref, pack_ref):
    core = place_ref[0]
    lanes = 128
    half = own_ref.shape[1] // 2
    act = jnp.concatenate([act_own_ref[...], act_other_ref[...]], axis=1)
    tiles = DOWN_COLUMNS // lanes
    for step in range(half // DOWN_COLUMNS):
        slot = step % 2
        at = pl.ds(pl.multiple_of(core * half + step * DOWN_COLUMNS, 512), DOWN_COLUMNS)
        weights = jnp.concatenate([own_ref[:, at], other_ref[:, at]], axis=0)
        product = jnp.dot(act, weights, preferred_element_type=F32)
        for t in range(tiles):
            sum_ref[slot, t] = product[:, t * lanes : (t + 1) * lanes]
            for j in range(2):
                piece = sum_ref[slot, t, pl.ds(j, CHIPS, stride=2), :]
                pack_ref[slot, pl.ds(2 * t + j, CHIPS, stride=2 * tiles), :] = piece
        rows = slice(step * 2 * tiles, (step + 1) * 2 * tiles)
        out_ref[:, rows, :] = pack_ref[slot].astype(BF).reshape(CHIPS, 2 * tiles, lanes)


def down(place, act_own, act_other, own, other):
    rows = act_own.shape[0]
    out_rows = own.shape[1] // 128
    tiles = DOWN_COLUMNS // 128
    whole = pl.BlockSpec(memory_space=pltpu.VMEM)
    return pl.pallas_call(
        down_kernel,
        in_specs=[pl.BlockSpec(memory_space=pltpu.SMEM)] + [whole] * 4,
        out_specs=whole,
        out_shape=jax.ShapeDtypeStruct((CHIPS, out_rows, 128), BF),
        scratch_shapes=[
            pltpu.VMEM((2, tiles, rows, 128), F32),
            pltpu.VMEM((2, CHIPS * 2 * tiles, 128), F32),
        ],
        compiler_params=limit(8),
        name="down",
    )(place, act_own, act_other, own, other)


def body(
    states_in,
    queries,
    kv_cache,
    kv_new,
    lengths,
    w_uv,
    w_out,
    norm_gain,
    expert_ids,
    route_scores,
    w_gate,
    w_up,
    w_down,
):
    core = lax.axis_index("core")
    group = lax.axis_index("x") * NY + lax.axis_index("y")
    quarter = lax.axis_index("z")
    model = states_in.shape[1]
    half = model // 2
    wide = half // QUARTERS
    down_own = w_down.reshape(-1, model)
    uv_other = swap(w_uv)
    out_other = swap(w_out)
    down_other = swap(down_own)
    place = jnp.stack([core, group])

    sent = attend_and_pack(
        lengths, queries, kv_cache, kv_new, states_in, expert_ids, route_scores
    )
    got = exchange(sent)
    mine, send, weights = project_values(place, got, w_uv[0], uv_other[0], w_out, out_other)
    partial, route, my_states = out_projection(place, mine, swap(send), weights)
    partial = exchange(partial.reshape(CHIPS, 8, wide))
    attention = jnp.sum(partial.astype(F32), axis=0)
    residual_part = (my_states + attention).astype(BF)
    rows_own = exchange(jnp.broadcast_to(residual_part[None], (CHIPS, 8, wide)))
    rows_other = swap(rows_own)
    rows_own = rows_own.reshape(GROUPS, NY, 8, wide)
    rows_other = rows_other.reshape(GROUPS, NY, 8, wide)

    act = gate_up(place, rows_own, rows_other, norm_gain, route, w_gate, w_up)
    act_other = swap(act)
    output = down(place, act, act_other, down_own, down_other)
    output = exchange(output)
    expert_sum = jnp.sum(output.astype(F32), axis=0)
    expert_sum = expert_sum.reshape(half // 128, 2, 128).transpose(1, 0, 2).reshape(2, half)

    def chip_rows(rows):
        mine = lax.dynamic_index_in_dim(rows, group, 0, keepdims=False)
        mine = lax.dynamic_slice_in_dim(mine, 2 * quarter, 2, 1)
        return mine.transpose(1, 0, 2).reshape(2, half)

    residual_own = chip_rows(rows_own)
    residual_other = chip_rows(rows_other)
    layer_half = (residual_own.astype(F32) + expert_sum).astype(BF)
    layer_mine = lax.dynamic_slice_in_dim(layer_half, core, 1, 0)
    layer_got = swap(lax.dynamic_slice_in_dim(layer_half, 1 - core, 1, 0))
    residual_mine = lax.dynamic_slice_in_dim(residual_own, core, 1, 0)
    residual_got = lax.dynamic_slice_in_dim(residual_other, core, 1, 0)

    def joined(mine, got):
        return jnp.where(
            core == 0, jnp.concatenate([mine, got], axis=1), jnp.concatenate([got, mine], axis=1)
        )

    return (joined(residual_mine, residual_got), joined(layer_mine, layer_got))


def solution(mesh):
    fine = Mesh(mesh.devices.reshape(NX, NZ, NY, 2), ALL_AXES)
    rows = P(ALL_AXES, None)
    cube = P(ALL_AXES, None, None)
    in_specs = (
        rows,
        cube,
        cube,
        rows,
        P(ALL_AXES),
        cube,
        rows,
        P(),
        rows,
        rows,
        P(("x", "z"), None, ("y", "core")),
        P(("x", "z"), None, ("y", "core")),
        P(("x", "z"), ("y", "core"), None),
    )
    return jax.shard_map(body, mesh=fine, in_specs=in_specs, out_specs=(rows, rows), check_vma=False)
```

time: 123 us -> 114 us (0.927)
  local copies, waits for them, and re-layouts: 8.28 us -> 0.23 us
  waiting for transfers between devices: 29.9 us -> 28.3 us
    unnamed x30 -> x16, local copies, waits for them, and re-layouts: 8.08 us -> 0.03 us
    pallas_call x3 -> x4, Pallas kernels: 11.8 us -> 8.81 us  [the longest x1 4.84 us: down(): pl.pallas_call(down_kernel, in_specs=[pl.BlockSpec(memory_space=pltpu.SME...]
    pallas_call x1, Pallas kernels: 1.22 us -> 3.51 us  [attend_and_pack(): pl.pallas_call(attend_kernel, in_specs=[pl.BlockSpec(memory_space=pltpu.S...]
    ppermute x7, waiting for transfers between devices: 5.36 us -> 3.55 us  [swap(): return lax.ppermute(value, 'core', SWAP)]
  transfers between devices with their start and end apart: 9 -> 9, of which waited for: 7 -> 7; matrix products, arithmetic and copies ran while one was open for 1% -> 1% of each run, Pallas kernels for 7% -> 9%
where the time goes in v3:
time: 114 us; the launch traced here: 113 us
  blocking collectives  40.4 us (35%)
  waiting for transfers between devices  28.3 us (25%)
  starting transfers between devices  26.2 us (23%)
  Pallas kernels  14.8 us (13%)
  other arithmetic  1.76 us (2%)
  between operations  1.46 us (1%)
    all_to_all x2, blocking collectives, exchange(): lax.all_to_all(value, CHIP_AXES, split_axis=0, concat_axis=0, tiled=True)  40.4 us
    all_to_all x2, waiting for transfers between devices, exchange(): lax.all_to_all(value, CHIP_AXES, split_axis=0, concat_axis=0, tiled=True)  24.8 us
    all_to_all x2, starting transfers between devices, exchange(): lax.all_to_all(value, CHIP_AXES, split_axis=0, concat_axis=0, tiled=True)  15.9 us
    ppermute x7, starting transfers between devices, swap(): return lax.ppermute(value, 'core', SWAP)  10.3 us
    pallas_call x1, Pallas kernels, down(): pl.pallas_call(down_kernel, in_specs=[pl.BlockSpec(memory_space=pltpu.SME...  4.84 us
    ppermute x7, waiting for transfers between devices, swap(): return lax.ppermute(value, 'core', SWAP)  3.55 us
    pallas_call x1, Pallas kernels, attend_and_pack(): pl.pallas_call(attend_kernel, in_specs=[pl.BlockSpec(memory_space=pltpu.S...  3.51 us
    pallas_call x1, Pallas kernels, project_values(): pl.pallas_call(value_kernel, in_specs=[pl.BlockSpec(memory_space=pltpu.SM...  2.47 us
  transfers between devices with their start and end apart: 9, of which 7 were waited for; matrix products, arithmetic and copies ran while one was open for 1% of the time, Pallas kernels for 9%

profile of v3, /device:TPU:1, one launch (start us, length us, event | category | flops | bytes accessed | tf_op | source)
XLA Modules:
  0.0 113.2 jit_solution(18445056310366414209)
XLA Ops:
  0.7 1.5 %collective-permute-start.5 = (bf16[384,7168]{1,0:T(8,128)(2,1)}, bf16[384,7168]{1,0:T(8,128)(2,1)}, u32[]{:S(2)}, u32[]{:S(2)}) collective-permute-start(bf16[384,7168]{1,0:T(8,128)(2,1)} %bitcast.32), channel_id=1, source_target_pairs={{0,1},{1,0},{2,3},{3,2},{4,5},{5,4},{6,7},{7,6},{8,9},{9,8},{10,11... | collective-permute-start | bytes 16515080 | tf_op jit(solution)/shard_map/ppermute | solution.py:23
  2.1 0.1 collective-permute-start.1
  2.9 3.5 %attend.1 = bf16[64,24,128]{2,1,0:T(8,128)(2,1)} custom-call(s32[1]{0:T(128)S(6)} %copy.15.length_ref, bf16[576,128]{1,0:T(8,128)(2,1)} %bitcast.46, bf16[576,1024]{1,0:T(8,128)(2,1)} %bitcast.45, bf16[1,576]{1,0:T(2,128)(2,1)} %newest_hbm.1, bf16[1,7168]{1,0:T(2,128)(2,1)} %states_hbm.1, s32[1,8]{1,0:T(1,128)} %ids_hbm.1, f32[1,8]{1,0:T(1,128)} %score_hbm.1), custom_call_target="tpu_custom_call" | custom-call | tf_op jit(solution)/shard_map/attend/pallas_call | solution.py:148
  6.4 11.3 %all-to-all-start = ((bf16[64,24,128]{2,1,0:T(8,128)(2,1)}), bf16[64,24,128]{2,1,0:T(8,128)(2,1)S(1)}, u32[]{:S(2)}, u32[]{:S(2)}) async-start(bf16[64,24,128]{2,1,0:T(8,128)(2,1)} %attend.1), calls=%async_computation | async-start | bytes 786432 | tf_op jit(solution)/shard_map/all_to_all | solution.py:27
  17.7 0.8 collective-permute-start
  18.4 0.1 pad_add_fusion.place_ref
  18.5 0.9 collective-permute-done
  19.4 9.0 %all-to-all-done.got_ref = bf16[64,24,128]{2,1,0:T(8,128)(2,1)S(1)} async-done(((bf16[64,24,128]{2,1,0:T(8,128)(2,1)}), bf16[64,24,128]{2,1,0:T(8,128)(2,1)S(1)}, u32[]{:S(2)}, u32[]{:S(2)}) %all-to-all-start) | async-done | bytes 393248 | tf_op jit(solution)/shard_map/all_to_all | solution.py:27
  28.4 2.5 %values.1 = (bf16[224,128]{1,0:T(8,128)(2,1)S(1)}, bf16[224,128]{1,0:T(8,128)(2,1)S(1)}, bf16[256,3584]{1,0:T(8,128)(2,1)S(1)}) custom-call(s32[2]{0:T(128)S(1)} %pad_add_fusion.place_ref, bf16[64,24,128]{2,1,0:T(8,128)(2,1)S(1)} %all-to-all-done.got_ref, bf16[512,128]{1,0:T(8,128)(2,1)S(1)} %bitcast.41, bf16[512,128]{1,0:T(8,128)(2,1)S(1)} %bitcast.42, ...), custom_call_target="tpu_custom_call" | custom-call | tf_op jit(solution)/shard_map/values/pallas_call | solution.py:244
  30.9 2.0 %collective-permute-start.2 = (bf16[224,128]{1,0:T(8,128)(2,1)S(1)}, bf16[224,128]{1,0:T(8,128)(2,1)S(1)}, u32[]{:S(2)}, u32[]{:S(2)}) collective-permute-start(bf16[224,128]{1,0:T(8,128)(2,1)S(1)} %get-tuple-element.11), channel_id=1, source_target_pairs={{0,1},{1,0},{2,3},{3,2},{4,5},{5,4},{6,7},{7,6},{8,9},{9,8},{10,11... | collective-permute-start | bytes 172040 | tf_op jit(solution)/shard_map/ppermute | solution.py:23
  33.0 0.9 collective-permute-done.2.got_ref
  33.9 1.0 out_projection.1
  34.9 0.0 copy-start
  34.9 20.4 %all_to_all.20 = bf16[64,8,896]{2,1,0:T(8,128)(2,1)S(1)} all-to-all(bf16[64,8,896]{2,1,0:T(8,128)(2,1)S(1)} %bitcast.40), channel_id=1, replica_groups=mesh['x'=4,'z'=4,'y'=4,'core'=2] {'x','y','z'}, dimensions={0} | all-to-all | bytes 1835008 | tf_op jit(solution)/shard_map/all_to_all | solution.py:27
  55.3 0.2 convert_reduce_fusion.1
  55.5 0.1 broadcast_in_dim.4
  55.6 20.0 %all_to_all.21 = bf16[64,8,896]{2,1,0:T(8,128)(2,1)S(1)} all-to-all(bf16[64,8,896]{2,1,0:T(8,128)(2,1)S(1)} %broadcast_in_dim.4), channel_id=1, replica_groups=mesh['x'=4,'z'=4,'y'=4,'core'=2] {'x','y','z'}, dimensions={0} | all-to-all | bytes 1835008 | tf_op jit(solution)/shard_map/all_to_all | solution.py:27
  75.6 3.2 %collective-permute-start.3 = (bf16[64,8,896]{2,1,0:T(8,128)(2,1)S(1)}, bf16[64,8,896]{2,1,0:T(8,128)(2,1)S(1)}, u32[]{:S(2)}, u32[]{:S(2)}) collective-permute-start(bf16[64,8,896]{2,1,0:T(8,128)(2,1)S(1)} %all_to_all.21), channel_id=1, source_target_pairs={{0,1},{1,0},{2,3},{3,2},{4,5},{5,4},{6,7},{7,6},{8,9},{9,8},{10,11... | collective-permute-start | bytes 2752520 | tf_op jit(solution)/shard_map/ppermute | solution.py:23
  78.8 1.4 %gate_up_first.1 = (f32[128,128]{1,0:T(8,128)S(1)}, f32[3,128,256]{2,1,0:T(8,128)S(1)}) custom-call(s32[2]{0:T(128)S(1)} %pad_add_fusion.place_ref, bf16[16,4,8,896]{3,2,1,0:T(8,128)(2,1)S(1)} %bitcast.36, f32[1,7168]{1,0:T(1,128)S(1)} %bitcast.43, bf16[3,7168,128]{2,1,0:T(8,128)(2,1)S(1)} %bitcast.31, bf16[3,7168,128]{2,1,0:T(8,128)(2,1)S(1)} %copy-done), custom_call_target="tpu_custom_call" | custom-call | tf_op jit(solution)/shard_map/gate_up_first/pallas_call | solution.py:358
  80.2 0.6 collective-permute-done.3
  80.8 1.5 %gate_up_second.1.act_own_ref = bf16[128,384]{1,0:T(8,128)(2,1)S(1)} custom-call(s32[2]{0:T(128)S(1)} %pad_add_fusion.place_ref, bf16[16,4,8,896]{3,2,1,0:T(8,128)(2,1)S(1)} %bitcast.38, f32[1,7168]{1,0:T(1,128)S(1)} %bitcast.44, bf16[3,7168,128]{2,1,0:T(8,128)(2,1)S(1)} %bitcast.31, bf16[3,7168,128]{2,1,0:T(8,128)(2,1)S(1)} %copy-done, ...), custom_call_target="tpu_custom_call" | custom-call | tf_op jit(solution)/shard_map/gate_up_second/pallas_call | solution.py:369
  82.4 0.5 collective-permute-start.4
  82.8 0.9 collective-permute-done.4.act_other_ref
  83.8 0.0 collective-permute-done.5.other_ref
  83.8 4.8 %down.1 = bf16[64,56,128]{2,1,0:T(8,128)(2,1)} custom-call(s32[2]{0:T(128)S(1)} %pad_add_fusion.place_ref, bf16[128,384]{1,0:T(8,128)(2,1)S(1)} %gate_up_second.1.act_own_ref, bf16[128,384]{1,0:T(8,128)(2,1)S(1)} %collective-permute-done.4.act_other_ref, bf16[384,7168]{1,0:T(8,128)(2,1)S(1)} %bitcast.35, bf16[384,7168]{1,0:T(8,128)(2,1)} %collective-permute-done.5.other_ref), custom_call_target="tpu_custom_call" | custom-call | tf_op jit(solution)/shard_map/down/pallas_call | solution.py:407
  88.6 4.6 %all-to-all-start.3 = ((bf16[64,56,128]{2,1,0:T(8,128)(2,1)}), bf16[64,56,128]{2,1,0:T(8,128)(2,1)S(1)}, u32[]{:S(2)}, u32[]{:S(2)}) async-start(bf16[64,56,128]{2,1,0:T(8,128)(2,1)} %down.1), calls=%async_computation.3 | async-start | bytes 1835008 | tf_op jit(solution)/shard_map/all_to_all | solution.py:27
  93.4 15.8 %all-to-all-done.3 = bf16[64,56,128]{2,1,0:T(8,128)(2,1)S(1)} async-done(((bf16[64,56,128]{2,1,0:T(8,128)(2,1)}), bf16[64,56,128]{2,1,0:T(8,128)(2,1)S(1)}, u32[]{:S(2)}, u32[]{:S(2)}) %all-to-all-start.3) | async-done | bytes 917536 | tf_op jit(solution)/shard_map/all_to_all | solution.py:27
  109.2 0.2 convert_reduce_fusion
  109.4 2.3 %collective-permute-start.6 = (bf16[1,3584]{1,0:T(2,128)(2,1)S(1)}, bf16[1,3584]{1,0:T(2,128)(2,1)S(1)}, u32[]{:S(2)}, u32[]{:S(2)}) collective-permute-start(bf16[1,3584]{1,0:T(2,128)(2,1)S(1)} %get-tuple-element.19), channel_id=1, source_target_pairs={{0,1},{1,0},{2,3},{3,2},{4,5},{5,4},{6,7},{7,6},{8,9},{9,8},{10,11... | collective-permute-start | bytes 21512 | tf_op jit(solution)/shard_map/ppermute | solution.py:23
  111.7 0.7 broadcast_select_fusion.1
  112.4 0.2 collective-permute-done.6
  112.6 0.7 broadcast_select_fusion
  (24 shorter events, 0.2 us)
Async XLA Ops:
  0.6 27.8 %copy-start.1 = (bf16[128,7168]{1,0:T(8,128)(2,1)S(1)}, bf16[128,7168]{1,0:T(8,128)(2,1)}, u32[]{:S(2)}) copy-start(bf16[128,7168]{1,0:T(8,128)(2,1)} %out_own_hbm.1) | copy-start | bytes 5505028
  0.6 17.0 %copy-start.2 = (bf16[1,512,128]{2,1,0:T(8,128)(2,1)S(1)}, bf16[1,512,128]{2,1,0:T(8,128)(2,1)}, u32[]{:S(2)}) copy-start(bf16[1,512,128]{2,1,0:T(8,128)(2,1)} %param.18) | copy-start | bytes 393220
  0.7 83.1 %collective-permute-start.5 = (bf16[384,7168]{1,0:T(8,128)(2,1)}, bf16[384,7168]{1,0:T(8,128)(2,1)}, u32[]{:S(2)}, u32[]{:S(2)}) collective-permute-start(bf16[384,7168]{1,0:T(8,128)(2,1)} %bitcast.32), channel_id=1, source_target_pairs={{0,1},{1,0},{2,3},{3,2},{4,5},{5,4},{6,7},{7,6},{8,9},{9,8},{10,11... | collective-permute-start | bytes 16515080 | tf_op jit(solution)/shard_map/ppermute | solution.py:23
  2.1 26.3 %collective-permute-start.1 = (bf16[128,7168]{1,0:T(8,128)(2,1)}, bf16[128,7168]{1,0:T(8,128)(2,1)}, u32[]{:S(2)}, u32[]{:S(2)}) collective-permute-start(bf16[128,7168]{1,0:T(8,128)(2,1)} %out_own_hbm.1), channel_id=1, source_target_pairs={{0,1},{1,0},{2,3},{3,2},{4,5},{5,4},{6,7},{7,6},{8,9},{9,8},{10,11... | collective-permute-start | bytes 5505032 | tf_op jit(solution)/shard_map/ppermute | solution.py:23
  6.4 22.1 %all-to-all-start = ((bf16[64,24,128]{2,1,0:T(8,128)(2,1)}), bf16[64,24,128]{2,1,0:T(8,128)(2,1)S(1)}, u32[]{:S(2)}, u32[]{:S(2)}) async-start(bf16[64,24,128]{2,1,0:T(8,128)(2,1)} %attend.1), calls=%async_computation | async-start | bytes 786432 | tf_op jit(solution)/shard_map/all_to_all | solution.py:27
  17.7 1.8 %collective-permute-start = (bf16[1,512,128]{2,1,0:T(8,128)(2,1)S(1)}, bf16[1,512,128]{2,1,0:T(8,128)(2,1)S(1)}, u32[]{:S(2)}, u32[]{:S(2)}) collective-permute-start(bf16[1,512,128]{2,1,0:T(8,128)(2,1)S(1)} %copy-done.2), channel_id=1, source_target_pairs={{0,1},{1,0},{2,3},{3,2},{4,5},{5,4},{6,7},{7,6},{8,9},{9,8},{10,11... | collective-permute-start | bytes 393224 | tf_op jit(solution)/shard_map/ppermute | solution.py:23
  28.4 50.3 %slice-start = ((s8[5505024]{0:T(1024)(128)(4,1)}), s8[4194304]{0:T(1024)(128)(4,1)S(1)}, s32[]{:S(2)}) async-start(s8[5505024]{0:T(1024)(128)(4,1)} %bitcast.30), calls=%async_computation.4 | async-start | bytes 8388608
  30.9 2.9 %collective-permute-start.2 = (bf16[224,128]{1,0:T(8,128)(2,1)S(1)}, bf16[224,128]{1,0:T(8,128)(2,1)S(1)}, u32[]{:S(2)}, u32[]{:S(2)}) collective-permute-start(bf16[224,128]{1,0:T(8,128)(2,1)S(1)} %get-tuple-element.11), channel_id=1, source_target_pairs={{0,1},{1,0},{2,3},{3,2},{4,5},{5,4},{6,7},{7,6},{8,9},{9,8},{10,11... | collective-permute-start | bytes 172040 | tf_op jit(solution)/shard_map/ppermute | solution.py:23
  33.9 44.9 %slice-start.1 = ((s8[5505024]{0:T(1024)(128)(4,1)}), s8[1310720]{0:T(1024)(128)(4,1)S(1)}, s32[]{:S(2)}) async-start(s8[5505024]{0:T(1024)(128)(4,1)} %bitcast.30), calls=%async_computation.5 | async-start | bytes 2621440
  34.9 43.9 %copy-start = (bf16[3,7168,128]{2,1,0:T(8,128)(2,1)S(1)}, bf16[3,7168,128]{2,1,0:T(8,128)(2,1)}, u32[]{:S(2)}) copy-start(bf16[3,7168,128]{2,1,0:T(8,128)(2,1)} %up_ref.3) | copy-start | bytes 16515076
  55.3 23.4 %copy-start.3 = (f32[7168]{0:T(1024)S(1)}, f32[7168]{0:T(1024)}, u32[]{:S(2)}) copy-start(f32[7168]{0:T(1024)} %param.20) | copy-start | bytes 86020
  75.6 5.3 %collective-permute-start.3 = (bf16[64,8,896]{2,1,0:T(8,128)(2,1)S(1)}, bf16[64,8,896]{2,1,0:T(8,128)(2,1)S(1)}, u32[]{:S(2)}, u32[]{:S(2)}) collective-permute-start(bf16[64,8,896]{2,1,0:T(8,128)(2,1)S(1)} %all_to_all.21), channel_id=1, source_target_pairs={{0,1},{1,0},{2,3},{3,2},{4,5},{5,4},{6,7},{7,6},{8,9},{9,8},{10,11... | collective-permute-start | bytes 2752520 | tf_op jit(solution)/shard_map/ppermute | solution.py:23
  80.8 2.9 %slice-start.2 = ((s8[5505024]{0:T(1024)(128)(4,1)}), s8[4194304]{0:T(1024)(128)(4,1)S(1)}, s32[]{:S(2)}) async-start(s8[5505024]{0:T(1024)(128)(4,1)} %bitcast.33), calls=%async_computation.6 | async-start | bytes 8388608
  80.8 2.9 %slice-start.3 = ((s8[5505024]{0:T(1024)(128)(4,1)}), s8[1310720]{0:T(1024)(128)(4,1)S(1)}, s32[]{:S(2)}) async-start(s8[5505024]{0:T(1024)(128)(4,1)} %bitcast.33), calls=%async_computation.7 | async-start | bytes 2621440
  82.4 1.4 %collective-permute-start.4 = (bf16[128,384]{1,0:T(8,128)(2,1)S(1)}, bf16[128,384]{1,0:T(8,128)(2,1)S(1)}, u32[]{:S(2)}, u32[]{:S(2)}) collective-permute-start(bf16[128,384]{1,0:T(8,128)(2,1)S(1)} %gate_up_second.1.act_own_ref), channel_id=1, source_target_pairs={{0,1},{1,0},{2,3},{3,2},{4,5},{5,4},{6,7},{7,6},{8,9},{9,8},{10,11... | collective-permute-start | bytes 294920 | tf_op jit(solution)/shard_map/ppermute | solution.py:23
  88.6 20.6 %all-to-all-start.3 = ((bf16[64,56,128]{2,1,0:T(8,128)(2,1)}), bf16[64,56,128]{2,1,0:T(8,128)(2,1)S(1)}, u32[]{:S(2)}, u32[]{:S(2)}) async-start(bf16[64,56,128]{2,1,0:T(8,128)(2,1)} %down.1), calls=%async_computation.3 | async-start | bytes 1835008 | tf_op jit(solution)/shard_map/all_to_all | solution.py:27
  109.4 3.2 %collective-permute-start.6 = (bf16[1,3584]{1,0:T(2,128)(2,1)S(1)}, bf16[1,3584]{1,0:T(2,128)(2,1)S(1)}, u32[]{:S(2)}, u32[]{:S(2)}) collective-permute-start(bf16[1,3584]{1,0:T(2,128)(2,1)S(1)} %get-tuple-element.19), channel_id=1, source_target_pairs={{0,1},{1,0},{2,3},{3,2},{4,5},{5,4},{6,7},{7,6},{8,9},{9,8},{10,11... | collective-permute-start | bytes 21512 | tf_op jit(solution)/shard_map/ppermute | solution.py:23

commit v4 on v3

--- a/solution.py
+++ b/solution.py
@@ -9,10 +9,10 @@
 ROPE = 64
 VD = 128
 NX, NZ, NY = 4, 4, 4
-QUARTERS = NZ
+QUARTERS = NY
 CHIPS = NX * NZ * NY
 GROUPS = NX * NZ
-CHIP_AXES = ("x", "y", "z")
+CHIP_AXES = ("z", "x", "y")
 ALL_AXES = ("x", "z", "y", "core")
 SWAP = [(0, 1), (1, 0)]
 BF = jnp.bfloat16
@@ -34,6 +34,7 @@
 SENT_ROWS = 24
 ROUTE_ROW = 8
 STATE_ROW = 9
+CACHE_COPIES = 4
 
 
 def attend_kernel(
@@ -55,22 +56,20 @@
     pack_ref,
     done,
 ):
+    piece = cache_hbm.shape[0] // CACHE_COPIES
+    pairs = [
+        (cache_hbm.at[k * piece : (k + 1) * piece], cache_ref.at[k * piece : (k + 1) * piece])
+        for k in range(CACHE_COPIES)
+    ]
+    pairs += [(query_hbm, query_ref), (newest_hbm, newest_ref)]
+    early = [(states_hbm, states_ref), (ids_hbm, ids_ref), (score_hbm, score_ref)]
     copies = [
         pltpu.make_async_copy(source, target, done.at[index])
-        for index, (source, target) in enumerate(
-            (
-                (cache_hbm, cache_ref),
-                (query_hbm, query_ref),
-                (newest_hbm, newest_ref),
-                (states_hbm, states_ref),
-                (ids_hbm, ids_ref),
-                (score_hbm, score_ref),
-            )
-        )
+        for index, (source, target) in enumerate(pairs + early)
     ]
     for copy in copies:
         copy.start()
-    for copy in copies[3:]:
+    for copy in copies[len(pairs) :]:
         copy.wait()
     lanes = 128
     pieces = states_ref[...].astype(F32)
@@ -93,7 +92,7 @@
     ids = ids_ref[...]
     per_block = 3
     chip = lax.broadcasted_iota(jnp.int32, (CHIPS, lanes), 0)
-    block = chip // (NY * NZ) * NZ + chip % NZ
+    block = chip // NY % NX * NZ + chip // (NX * NY)
     lane = lax.broadcasted_iota(jnp.int32, (CHIPS, lanes), 1)
     expert = jnp.where(lane < per_block, block * per_block + lane, -1)
     dense = jnp.zeros((CHIPS, lanes), F32)
@@ -101,7 +100,7 @@
         dense = dense + jnp.where(expert == ids[:, k : k + 1], routes[:, k : k + 1], 0.0)
     pack_ref[pl.ds(ROUTE_ROW, CHIPS, stride=SENT_ROWS), :] = dense
 
-    for copy in copies[:3]:
+    for copy in copies[: len(pairs)]:
         copy.wait()
     heads = query_ref.shape[1]
     positions = cache_ref.shape[1]
@@ -132,13 +131,13 @@
         latent_ref[t] = blended[:, t * lanes : (t + 1) * lanes]
 
     for x in range(NX):
-        for y in range(NY):
-            head = 2 * (x * NZ * NY + y)
-            row = (x * NY + y) * NZ * SENT_ROWS
+        for z in range(NZ):
+            head = 2 * (x * NZ + z) * NY
+            row = (z * NX + x) * NY * SENT_ROWS
             for t in range(LAT // lanes):
                 for j in range(2):
-                    piece = latent_ref[t, pl.ds(head + j, NZ, stride=2 * NY), :]
-                    pack_ref[pl.ds(row + 2 * t + j, NZ, stride=SENT_ROWS), :] = piece
+                    piece = latent_ref[t, pl.ds(head + j, NY, stride=2), :]
+                    pack_ref[pl.ds(row + 2 * t + j, NY, stride=SENT_ROWS), :] = piece
     sent_ref[...] = pack_ref[...].astype(BF).reshape(sent_ref.shape)
 
 
@@ -155,7 +154,7 @@
         + [
             pltpu.VMEM((LAT // 128, queries.shape[1], 128), F32),
             pltpu.VMEM((CHIPS * SENT_ROWS, 128), F32),
-            pltpu.SemaphoreType.DMA((len(inputs),)),
+            pltpu.SemaphoreType.DMA((len(inputs) + CACHE_COPIES - 1,)),
         ],
         compiler_params=limit(62),
         name="attend",
@@ -165,39 +164,9 @@
 VALUE_ROWS = 3 * CHIPS + 32
 
 
-def value_kernel(
-    place_ref,
-    got_ref,
-    uv_own_hbm,
-    uv_other_hbm,
-    out_own_hbm,
-    out_other_hbm,
-    mine_ref,
-    send_ref,
-    weights_ref,
-    own_ref,
-    other_ref,
-    rows_ref,
-    state_ref,
-    done,
-):
+def value_kernel(place_ref, got_ref, uv_ref, after_ref, mine_ref, send_ref, rows_ref, state_ref):
+    del after_ref
     core = place_ref[0]
-    heads = out_own_hbm.shape[0]
-    half = weights_ref.shape[1]
-    columns = pl.ds(pl.multiple_of(core * half, 128), half)
-    copies = [
-        pltpu.make_async_copy(source, target, done.at[index])
-        for index, (source, target) in enumerate(
-            (
-                (uv_own_hbm, own_ref),
-                (uv_other_hbm, other_ref),
-                (out_own_hbm.at[:, columns], weights_ref.at[:heads]),
-                (out_other_hbm.at[:, columns], weights_ref.at[heads:]),
-            )
-        )
-    ]
-    for copy in copies:
-        copy.start()
     group = place_ref[1]
     lanes = 128
     rows_ref[...] = got_ref[...].astype(F32).reshape(rows_ref.shape)
@@ -211,10 +180,8 @@
     first, second = latent(0), latent(1)
     latent_own = jnp.where(core == 0, first, second)
     latent_other = jnp.where(core == 0, second, first)
-    copies[0].wait()
-    copies[1].wait()
-    value_own = jnp.dot(latent_own, own_ref[...], preferred_element_type=F32).astype(BF)
-    value_other = jnp.dot(latent_other, other_ref[...], preferred_element_type=F32).astype(BF)
+    value_own = jnp.dot(latent_own, uv_ref[0], preferred_element_type=F32).astype(BF)
+    value_other = jnp.dot(latent_other, uv_ref[1], preferred_element_type=F32).astype(BF)
     routes = rows_ref[pl.ds(ROUTE_ROW, CHIPS, stride=SENT_ROWS), :].astype(BF)
     base = pl.multiple_of(group * (NY * SENT_ROWS), 8)
     tiles = 7
@@ -232,30 +199,75 @@
         ref[2 * CHIPS : 3 * CHIPS, :] = routes
     mine_ref[3 * CHIPS :, :] = jnp.where(core == 0, low, high).astype(BF)
     send_ref[3 * CHIPS :, :] = jnp.where(core == 0, high, low).astype(BF)
-    copies[2].wait()
-    copies[3].wait()
-
-
-def project_values(place, got, uv_own, uv_other, out_own, out_other):
-    whole = pl.BlockSpec(memory_space=pltpu.VMEM)
-    outside = pl.BlockSpec(memory_space=pltpu.HBM)
+
+
+def project_values(place, got, uv, after):
+    whole = pl.BlockSpec(memory_space=pltpu.VMEM)
     out = jax.ShapeDtypeStruct((VALUE_ROWS, 128), BF)
-    heads, model = out_own.shape
     return pl.pallas_call(
         value_kernel,
-        in_specs=[pl.BlockSpec(memory_space=pltpu.SMEM), whole] + [outside] * 4,
-        out_specs=(whole, whole, whole),
-        out_shape=(out, out, jax.ShapeDtypeStruct((2 * heads, model // 2), BF)),
+        in_specs=[
+            pl.BlockSpec(memory_space=pltpu.SMEM),
+            whole,
+            whole,
+            pl.BlockSpec(memory_space=pl.ANY),
+        ],
+        out_specs=(whole, whole),
+        out_shape=(out, out),
         scratch_shapes=[
-            pltpu.VMEM(uv_own.shape, BF),
-            pltpu.VMEM(uv_own.shape, BF),
             pltpu.VMEM((CHIPS * SENT_ROWS, 128), F32),
             pltpu.VMEM((2, 32, 128), F32),
-            pltpu.SemaphoreType.DMA((4,)),
         ],
         compiler_params=limit(12),
         name="values",
-    )(place, got, uv_own, uv_other, out_own, out_other)
+    )(place, got, uv, after)
+
+
+def fetch_kernel(
+    place_ref,
+    uv_own_hbm,
+    uv_other_hbm,
+    own_hbm,
+    other_hbm,
+    uv_ref,
+    weights_ref,
+    done,
+):
+    heads = own_hbm.shape[0]
+    half = weights_ref.shape[1]
+    columns = pl.ds(pl.multiple_of(place_ref[0] * half, 128), half)
+    copies = [
+        pltpu.make_async_copy(source, target, done.at[index])
+        for index, (source, target) in enumerate(
+            (
+                (uv_own_hbm, uv_ref.at[0]),
+                (uv_other_hbm, uv_ref.at[1]),
+                (own_hbm.at[:, columns], weights_ref.at[:heads]),
+                (other_hbm.at[:, columns], weights_ref.at[heads:]),
+            )
+        )
+    ]
+    for copy in copies:
+        copy.start()
+    for copy in copies:
+        copy.wait()
+
+
+def fetch_halves(place, uv_own, uv_other, own, other):
+    whole = pl.BlockSpec(memory_space=pltpu.VMEM)
+    return pl.pallas_call(
+        fetch_kernel,
+        in_specs=[pl.BlockSpec(memory_space=pltpu.SMEM)]
+        + [pl.BlockSpec(memory_space=pl.ANY)] * 4,
+        out_specs=(whole, whole),
+        out_shape=(
+            jax.ShapeDtypeStruct((2,) + uv_own.shape, BF),
+            jax.ShapeDtypeStruct((2 * own.shape[0], own.shape[1] // 2), BF),
+        ),
+        scratch_shapes=[pltpu.SemaphoreType.DMA((4,))],
+        compiler_params=limit(4),
+        name="fetch",
+    )(place, uv_own, uv_other, own, other)
 
 
 def out_kernel(
@@ -327,11 +339,31 @@
     return total, sums
 
 
-def first_kernel(place_ref, rows_ref, gain_ref, gate_ref, up_ref, total_ref, sums_ref):
+COPIES = 6
+
+
+def first_kernel(
+    place_ref, rows_ref, gain_ref, gate_ref, up_ref, down_hbm, total_ref, sums_ref, down_ref, done
+):
+    half = down_ref.shape[1]
+    columns = pl.ds(pl.multiple_of(place_ref[0] * half, 128), half)
+    piece = down_ref.shape[0] // COPIES
+    copies = [
+        pltpu.make_async_copy(
+            down_hbm.at[index * piece : (index + 1) * piece, columns],
+            down_ref.at[index * piece : (index + 1) * piece],
+            done.at[index],
+        )
+        for index in range(COPIES)
+    ]
+    for copy in copies:
+        copy.start()
     total, sums = half_products(place_ref[0], rows_ref, gain_ref, gate_ref, up_ref)
     total_ref[...] = jnp.broadcast_to(total, total_ref.shape)
     for e, value in enumerate(sums):
         sums_ref[e] = value
+    for copy in copies:
+        copy.wait()
 
 
 def second_kernel(
@@ -349,24 +381,27 @@
         act_ref[:, e * hidden : (e + 1) * hidden] = active.astype(BF)
 
 
-def gate_up(place, own, other, gain, route, w_gate, w_up):
+def gate_up(place, own, other, gain, route, w_gate, w_up, down_other):
     groups, _, eight, wide = own.shape
     rows = groups * eight
     experts, model, hidden = w_gate.shape
     whole = pl.BlockSpec(memory_space=pltpu.VMEM)
     where = pl.BlockSpec(memory_space=pltpu.SMEM)
-    total, sums = pl.pallas_call(
+    down_rows, down_columns = down_other.shape
+    total, sums, down_half = pl.pallas_call(
         first_kernel,
-        in_specs=[where] + [whole] * 4,
-        out_specs=(whole, whole),
+        in_specs=[where] + [whole] * 4 + [pl.BlockSpec(memory_space=pltpu.HBM)],
+        out_specs=(whole, whole, whole),
         out_shape=(
             jax.ShapeDtypeStruct((rows, 128), F32),
             jax.ShapeDtypeStruct((experts, rows, 2 * hidden), F32),
+            jax.ShapeDtypeStruct((down_rows, down_columns // 2), BF),
         ),
+        scratch_shapes=[pltpu.SemaphoreType.DMA((COPIES,))],
         compiler_params=limit(12),
         name="gate_up_first",
-    )(place, own, gain[None], w_gate, w_up)
-    return pl.pallas_call(
+    )(place, own, gain[None], w_gate, w_up, down_other)
+    act = pl.pallas_call(
         second_kernel,
         in_specs=[where] + [whole] * 7,
         out_specs=whole,
@@ -374,6 +409,7 @@
         compiler_params=limit(12),
         name="gate_up_second",
     )(place, other, gain[None], w_gate, w_up, total, sums, route)
+    return act, down_half
 
 
 DOWN_COLUMNS = 512
@@ -388,7 +424,8 @@
     for step in range(half // DOWN_COLUMNS):
         slot = step % 2
         at = pl.ds(pl.multiple_of(core * half + step * DOWN_COLUMNS, 512), DOWN_COLUMNS)
-        weights = jnp.concatenate([own_ref[:, at], other_ref[:, at]], axis=0)
+        other = other_ref[:, step * DOWN_COLUMNS : (step + 1) * DOWN_COLUMNS]
+        weights = jnp.concatenate([own_ref[:, at], other], axis=0)
         product = jnp.dot(act, weights, preferred_element_type=F32)
         for t in range(tiles):
             sum_ref[slot, t] = product[:, t * lanes : (t + 1) * lanes]
@@ -416,6 +453,76 @@
         compiler_params=limit(8),
         name="down",
     )(place, act_own, act_other, own, other)
+
+
+def rows_kernel(place_ref, own_ref, other_ref, after_ref, residual_ref, rows_ref):
+    del after_ref
+    core = place_ref[0]
+    group = place_ref[1]
+    quarter = place_ref[2]
+    quarters, wide = own_ref.shape[1], own_ref.shape[3]
+    half = quarters * wide
+    place = lax.broadcasted_iota(jnp.int32, (8, wide), 0)
+    for q in range(quarters):
+        cols = slice(q * wide, (q + 1) * wide)
+
+        def row(ref, at):
+            block = ref[group, q].astype(F32)
+            return jnp.sum(jnp.where(place == at, block, 0.0), axis=0, keepdims=True)
+
+        first, second = row(own_ref, 2 * quarter), row(own_ref, 2 * quarter + 1)
+        rows_ref[0:1, cols] = first
+        rows_ref[1:2, cols] = second
+        at = pl.ds(pl.multiple_of(core * half + q * wide, 128), wide)
+        residual_ref[:, at] = jnp.where(core == 0, first, second).astype(BF)
+        at = pl.ds(pl.multiple_of((1 - core) * half + q * wide, 128), wide)
+        residual_ref[:, at] = row(other_ref, 2 * quarter + core).astype(BF)
+
+
+def take_rows(place, own, other, after):
+    half = own.shape[1] * own.shape[3]
+    whole = pl.BlockSpec(memory_space=pltpu.VMEM)
+    return pl.pallas_call(
+        rows_kernel,
+        in_specs=[
+            pl.BlockSpec(memory_space=pltpu.SMEM),
+            whole,
+            whole,
+            pl.BlockSpec(memory_space=pl.ANY),
+        ],
+        out_specs=(whole, whole),
+        out_shape=(
+            jax.ShapeDtypeStruct((1, 2 * half), BF),
+            jax.ShapeDtypeStruct((2, half), F32),
+        ),
+        compiler_params=limit(4),
+        name="take_rows",
+    )(place, own, other, after)
+
+
+def finish_kernel(place_ref, got_ref, rows_ref, mine_ref, send_ref, sum_ref):
+    core = place_ref[0]
+    lanes = 128
+    sum_ref[...] = jnp.sum(got_ref[...].astype(F32), axis=0)
+    for tile in range(rows_ref.shape[1] // lanes):
+        cols = slice(tile * lanes, (tile + 1) * lanes)
+        both = rows_ref[:, cols] + sum_ref[2 * tile : 2 * tile + 2, :]
+        mine_ref[:, cols] = jnp.where(core == 0, both[:1], both[1:]).astype(BF)
+        send_ref[:, cols] = jnp.where(core == 0, both[1:], both[:1]).astype(BF)
+
+
+def finish(place, got, rows):
+    whole = pl.BlockSpec(memory_space=pltpu.VMEM)
+    part = jax.ShapeDtypeStruct((1, rows.shape[1]), BF)
+    return pl.pallas_call(
+        finish_kernel,
+        in_specs=[pl.BlockSpec(memory_space=pltpu.SMEM)] + [whole] * 2,
+        out_specs=(whole, whole),
+        out_shape=(part, part),
+        scratch_shapes=[pltpu.VMEM(got.shape[1:], F32)],
+        compiler_params=limit(4),
+        name="finish",
+    )(place, got, rows)
 
 
 def body(
@@ -434,8 +541,8 @@
     w_down,
 ):
     core = lax.axis_index("core")
-    group = lax.axis_index("x") * NY + lax.axis_index("y")
-    quarter = lax.axis_index("z")
+    group = lax.axis_index("z") * NX + lax.axis_index("x")
+    quarter = lax.axis_index("y")
     model = states_in.shape[1]
     half = model // 2
     wide = half // QUARTERS
@@ -443,13 +550,14 @@
     uv_other = swap(w_uv)
     out_other = swap(w_out)
     down_other = swap(down_own)
-    place = jnp.stack([core, group])
+    place = jnp.stack([core, group, quarter])
 
     sent = attend_and_pack(
         lengths, queries, kv_cache, kv_new, states_in, expert_ids, route_scores
     )
     got = exchange(sent)
-    mine, send, weights = project_values(place, got, w_uv[0], uv_other[0], w_out, out_other)
+    uv, weights = fetch_halves(place, w_uv[0], uv_other[0], w_out, out_other)
+    mine, send = project_values(place, got, uv, weights)
     partial, route, my_states = out_projection(place, mine, swap(send), weights)
     partial = exchange(partial.reshape(CHIPS, 8, wide))
     attention = jnp.sum(partial.astype(F32), axis=0)
@@ -459,32 +567,17 @@
     rows_own = rows_own.reshape(GROUPS, NY, 8, wide)
     rows_other = rows_other.reshape(GROUPS, NY, 8, wide)
 
-    act = gate_up(place, rows_own, rows_other, norm_gain, route, w_gate, w_up)
-    act_other = swap(act)
-    output = down(place, act, act_other, down_own, down_other)
-    output = exchange(output)
-    expert_sum = jnp.sum(output.astype(F32), axis=0)
-    expert_sum = expert_sum.reshape(half // 128, 2, 128).transpose(1, 0, 2).reshape(2, half)
-
-    def chip_rows(rows):
-        mine = lax.dynamic_index_in_dim(rows, group, 0, keepdims=False)
-        mine = lax.dynamic_slice_in_dim(mine, 2 * quarter, 2, 1)
-        return mine.transpose(1, 0, 2).reshape(2, half)
-
-    residual_own = chip_rows(rows_own)
-    residual_other = chip_rows(rows_other)
-    layer_half = (residual_own.astype(F32) + expert_sum).astype(BF)
-    layer_mine = lax.dynamic_slice_in_dim(layer_half, core, 1, 0)
-    layer_got = swap(lax.dynamic_slice_in_dim(layer_half, 1 - core, 1, 0))
-    residual_mine = lax.dynamic_slice_in_dim(residual_own, core, 1, 0)
-    residual_got = lax.dynamic_slice_in_dim(residual_other, core, 1, 0)
-
-    def joined(mine, got):
-        return jnp.where(
-            core == 0, jnp.concatenate([mine, got], axis=1), jnp.concatenate([got, mine], axis=1)
-        )
-
-    return (joined(residual_mine, residual_got), joined(layer_mine, layer_got))
+    act, down_half = gate_up(
+        place, rows_own, rows_other, norm_gain, route, w_gate, w_up, down_other
+    )
+    residual, chip_rows = take_rows(place, rows_own, rows_other, act)
+    output = down(place, act, swap(act), down_own, down_half)
+    mine, send = finish(place, exchange(output), chip_rows)
+    got = swap(send)
+    layer_out = jnp.where(
+        core == 0, jnp.concatenate([mine, got], axis=1), jnp.concatenate([got, mine], axis=1)
+    )
+    return (residual, layer_out)
 
 
 def solution(mesh):

time: 114 us -> 114 us (level)
  waiting for transfers between devices: 28.3 us -> 22.1 us
  local copies, waits for them, and re-layouts: 0.23 us -> 5.26 us
  Pallas kernels: 14.8 us -> 16.5 us
    all_to_all x2, waiting for transfers between devices: 24.8 us -> 17.9 us  [exchange(): lax.all_to_all(value, CHIP_AXES, split_axis=0, concat_axis=0, tiled=True)]
    unnamed x16 -> x20, local copies, waits for them, and re-layouts: 0.03 us -> 5.19 us
    pallas_call x1 -> x4, Pallas kernels: 1.44 us -> 6.16 us  [the longest x1 3.06 us: gate_up(): pl.pallas_call(first_kernel, in_specs=[where] + [whole] * 4 + [pl.BlockSp...]
    pallas_call x1, Pallas kernels: 4.84 us -> 2.77 us  [down(): pl.pallas_call(down_kernel, in_specs=[pl.BlockSpec(memory_space=pltpu.SME...]
  transfers between devices with their start and end apart: 9 -> 9, of which waited for: 7 -> 6; matrix products, arithmetic and copies ran while one was open for 1% -> 0% of each run, Pallas kernels for 9% -> 10%
where the time goes in v4:
time: 114 us; the launch traced here: 113 us
  blocking collectives  41.5 us (36%)
  starting transfers between devices  25.8 us (23%)
  waiting for transfers between devices  22.1 us (19%)
  Pallas kernels  16.5 us (14%)
  local copies, waits for them, and re-layouts  5.26 us (5%)
  between operations  1.43 us (1%)
    all_to_all x2, blocking collectives, exchange(): lax.all_to_all(value, CHIP_AXES, split_axis=0, concat_axis=0, tiled=True)  41.5 us
    all_to_all x2, waiting for transfers between devices, exchange(): lax.all_to_all(value, CHIP_AXES, split_axis=0, concat_axis=0, tiled=True)  17.9 us
    all_to_all x2, starting transfers between devices, exchange(): lax.all_to_all(value, CHIP_AXES, split_axis=0, concat_axis=0, tiled=True)  16.1 us
    ppermute x7, starting transfers between devices, swap(): return lax.ppermute(value, 'core', SWAP)  9.63 us
    unnamed x20, local copies, waits for them, and re-layouts  5.19 us
    ppermute x7, waiting for transfers between devices, swap(): return lax.ppermute(value, 'core', SWAP)  4.14 us
    pallas_call x1, Pallas kernels, attend_and_pack(): pl.pallas_call(attend_kernel, in_specs=[pl.BlockSpec(memory_space=pltpu.S...  3.6 us
    pallas_call x1, Pallas kernels, gate_up(): pl.pallas_call(first_kernel, in_specs=[where] + [whole] * 4 + [pl.BlockSp...  3.06 us
  transfers between devices with their start and end apart: 9, of which 6 were waited for; matrix products, arithmetic and copies ran while one was open for 0% of the time, Pallas kernels for 10%

profile of v4, /device:TPU:1, one launch (start us, length us, event | category | flops | bytes accessed | tf_op | source)
XLA Modules:
  0.0 113.5 jit_solution(6808082593199194786)
XLA Ops:
  0.6 1.5 %collective-permute-start.4 = (bf16[384,7168]{1,0:T(8,128)(2,1)}, bf16[384,7168]{1,0:T(8,128)(2,1)}, u32[]{:S(2)}, u32[]{:S(2)}) collective-permute-start(bf16[384,7168]{1,0:T(8,128)(2,1)} %bitcast.20), channel_id=1, source_target_pairs={{0,1},{1,0},{2,3},{3,2},{4,5},{5,4},{6,7},{7,6},{8,9},{9,8},{10,11... | collective-permute-start | bytes 16515080 | tf_op jit(solution)/shard_map/ppermute | solution.py:23
  2.1 0.1 collective-permute-start.1
  2.8 3.6 %attend.1 = bf16[64,24,128]{2,1,0:T(8,128)(2,1)} custom-call(s32[1]{0:T(128)S(6)} %copy.15.length_ref, bf16[576,128]{1,0:T(8,128)(2,1)} %bitcast.32, bf16[576,1024]{1,0:T(8,128)(2,1)} %bitcast.31, bf16[1,576]{1,0:T(2,128)(2,1)} %newest_hbm.1, bf16[1,7168]{1,0:T(2,128)(2,1)} %states_hbm.1, s32[1,8]{1,0:T(1,128)} %ids_hbm.1, f32[1,8]{1,0:T(1,128)} %score_hbm.1), custom_call_target="tpu_custom_call" | custom-call | tf_op jit(solution)/shard_map/attend/pallas_call | solution.py:147
  6.4 11.5 %all-to-all-start = ((bf16[64,24,128]{2,1,0:T(8,128)(2,1)}), bf16[64,24,128]{2,1,0:T(8,128)(2,1)}, u32[]{:S(2)}, u32[]{:S(2)}) async-start(bf16[64,24,128]{2,1,0:T(8,128)(2,1)} %attend.1), calls=%async_computation | async-start | bytes 786432 | tf_op jit(solution)/shard_map/all_to_all | solution.py:27
  18.0 0.8 collective-permute-start
  18.8 1.1 collective-permute-done
  19.9 1.3 %copy-done.2 = bf16[128,7168]{1,0:T(8,128)(2,1)} copy-done((bf16[128,7168]{1,0:T(8,128)(2,1)}, bf16[128,7168]{1,0:T(8,128)(2,1)S(1)}, u32[]{:S(2)}) %copy-start.2) | copy-done | bytes 1835032
  21.2 1.5 %copy-done.1 = bf16[128,7168]{1,0:T(8,128)(2,1)S(1)} copy-done((bf16[128,7168]{1,0:T(8,128)(2,1)S(1)}, bf16[128,7168]{1,0:T(8,128)(2,1)}, u32[]{:S(2)}) %copy-start.1) | copy-done | bytes 1835032
  22.7 1.5 %copy-done.3 = bf16[128,7168]{1,0:T(8,128)(2,1)S(1)} copy-done((bf16[128,7168]{1,0:T(8,128)(2,1)S(1)}, bf16[128,7168]{1,0:T(8,128)(2,1)}, u32[]{:S(2)}) %copy-start.3) | copy-done | bytes 1835032
  24.2 0.9 copy-done.4
  25.1 1.1 fetch.1
  26.2 2.6 %all-to-all-done.got_ref = bf16[64,24,128]{2,1,0:T(8,128)(2,1)} async-done(((bf16[64,24,128]{2,1,0:T(8,128)(2,1)}), bf16[64,24,128]{2,1,0:T(8,128)(2,1)}, u32[]{:S(2)}, u32[]{:S(2)}) %all-to-all-start) | async-done | bytes 393248 | tf_op jit(solution)/shard_map/all_to_all | solution.py:27
  28.7 1.4 %values.1 = (bf16[224,128]{1,0:T(8,128)(2,1)S(1)}, bf16[224,128]{1,0:T(8,128)(2,1)S(1)}) custom-call(s32[3]{0:T(128)S(1)} %pad_add_fusion.place_ref, bf16[64,24,128]{2,1,0:T(8,128)(2,1)} %all-to-all-done.got_ref, bf16[2,512,128]{2,1,0:T(8,128)(2,1)S(1)} %get-tuple-element.16.uv_ref, bf16[256,3584]{1,0:T(8,128)(2,1)S(1)} %get-tuple-element.17.after_ref.weights_ref), custom_call_target="tpu_custom_call" | custom-call | tf_op jit(solution)/shard_map/values/pallas_call | solution.py:207
  30.1 2.0 %collective-permute-start.2 = (bf16[224,128]{1,0:T(8,128)(2,1)S(1)}, bf16[224,128]{1,0:T(8,128)(2,1)S(1)}, u32[]{:S(2)}, u32[]{:S(2)}) collective-permute-start(bf16[224,128]{1,0:T(8,128)(2,1)S(1)} %get-tuple-element.19), channel_id=1, source_target_pairs={{0,1},{1,0},{2,3},{3,2},{4,5},{5,4},{6,7},{7,6},{8,9},{9,8},{10,11... | collective-permute-start | bytes 172040 | tf_op jit(solution)/shard_map/ppermute | solution.py:23
  32.2 0.9 collective-permute-done.2.got_ref
  33.1 1.0 out_projection.1
  34.1 22.0 %all_to_all.20 = bf16[64,8,896]{2,1,0:T(8,128)(2,1)S(1)} all-to-all(bf16[64,8,896]{2,1,0:T(8,128)(2,1)S(1)} %bitcast.26), channel_id=1, replica_groups=mesh['x'=4,'z'=4,'y'=4,'core'=2] {'z','x','y'}, dimensions={0} | all-to-all | bytes 1835008 | tf_op jit(solution)/shard_map/all_to_all | solution.py:27
  56.1 0.2 convert_reduce_fusion
  56.4 19.5 %all_to_all.21 = bf16[64,8,896]{2,1,0:T(8,128)(2,1)S(1)} all-to-all(bf16[64,8,896]{2,1,0:T(8,128)(2,1)S(1)} %broadcast_in_dim.4), channel_id=1, replica_groups=mesh['x'=4,'z'=4,'y'=4,'core'=2] {'z','x','y'}, dimensions={0} | all-to-all | bytes 1835008 | tf_op jit(solution)/shard_map/all_to_all | solution.py:27
  75.9 3.4 %collective-permute-start.3 = (bf16[64,8,896]{2,1,0:T(8,128)(2,1)S(1)}, bf16[64,8,896]{2,1,0:T(8,128)(2,1)S(1)}, u32[]{:S(2)}, u32[]{:S(2)}) collective-permute-start(bf16[64,8,896]{2,1,0:T(8,128)(2,1)S(1)} %all_to_all.21), channel_id=1, source_target_pairs={{0,1},{1,0},{2,3},{3,2},{4,5},{5,4},{6,7},{7,6},{8,9},{9,8},{10,11... | collective-permute-start | bytes 2752520 | tf_op jit(solution)/shard_map/ppermute | solution.py:23
  79.4 3.1 %gate_up_first.1 = (f32[128,128]{1,0:T(8,128)S(1)}, f32[3,128,256]{2,1,0:T(8,128)S(1)}, bf16[384,3584]{1,0:T(8,128)(2,1)S(1)}) custom-call(s32[3]{0:T(128)S(1)} %pad_add_fusion.place_ref, bf16[16,4,8,896]{3,2,1,0:T(8,128)(2,1)S(1)} %bitcast.18, f32[1,7168]{1,0:T(1,128)S(1)} %bitcast.29, bf16[3,7168,128]{2,1,0:T(8,128)(2,1)S(1)} %bitcast.17, ...), custom_call_target="tpu_custom_call" | custom-call | tf_op jit(solution)/shard_map/gate_up_first/pallas_call | solution.py:391
  82.5 1.5 %gate_up_second.1.after_ref.act_own_ref = bf16[128,384]{1,0:T(8,128)(2,1)S(1)} custom-call(s32[3]{0:T(128)S(1)} %pad_add_fusion.place_ref, bf16[16,4,8,896]{3,2,1,0:T(8,128)(2,1)S(1)} %bitcast.24, f32[1,7168]{1,0:T(1,128)S(1)} %bitcast.30, bf16[3,7168,128]{2,1,0:T(8,128)(2,1)S(1)} %bitcast.17, bf16[3,7168,128]{2,1,0:T(8,128)(2,1)S(1)} %copy-done, ...), custom_call_target="tpu_custom_call" | custom-call | tf_op jit(solution)/shard_map/gate_up_second/pallas_call | solution.py:404
  84.0 0.1 collective-permute-start.5
  84.1 1.3 %collective-permute-done.5.act_other_ref = bf16[128,384]{1,0:T(8,128)(2,1)S(1)} collective-permute-done((bf16[128,384]{1,0:T(8,128)(2,1)S(1)}, bf16[128,384]{1,0:T(8,128)(2,1)S(1)}, u32[]{:S(2)}, u32[]{:S(2)}) %collective-permute-start.5) | collective-permute-done | bytes 98336 | tf_op jit(solution)/shard_map/ppermute | solution.py:23
  85.4 2.8 %down.1 = bf16[64,56,128]{2,1,0:T(8,128)(2,1)} custom-call(s32[3]{0:T(128)S(1)} %pad_add_fusion.place_ref, bf16[128,384]{1,0:T(8,128)(2,1)S(1)} %gate_up_second.1.after_ref.act_own_ref, bf16[128,384]{1,0:T(8,128)(2,1)S(1)} %collective-permute-done.5.act_other_ref, bf16[384,7168]{1,0:T(8,128)(2,1)S(1)} %bitcast.23, ...), custom_call_target="tpu_custom_call" | custom-call | tf_op jit(solution)/shard_map/down/pallas_call | solution.py:444
  88.2 4.6 %all-to-all-start.3 = ((bf16[64,56,128]{2,1,0:T(8,128)(2,1)}), bf16[64,56,128]{2,1,0:T(8,128)(2,1)S(1)}, u32[]{:S(2)}, u32[]{:S(2)}) async-start(bf16[64,56,128]{2,1,0:T(8,128)(2,1)} %down.1), calls=%async_computation.3 | async-start | bytes 1835008 | tf_op jit(solution)/shard_map/all_to_all | solution.py:27
  92.8 1.3 %take_rows.1 = (bf16[1,7168]{1,0:T(2,128)(2,1)}, f32[2,3584]{1,0:T(2,128)S(1)}) custom-call(s32[3]{0:T(128)S(1)} %pad_add_fusion.place_ref, bf16[16,4,8,896]{3,2,1,0:T(8,128)(2,1)S(1)} %bitcast.19, bf16[16,4,8,896]{3,2,1,0:T(8,128)(2,1)S(1)} %bitcast.25, bf16[128,384]{1,0:T(8,128)(2,1)S(1)} %gate_up_second.1.after_ref.act_own_ref), custom_call_target="tpu_custom_call" | custom-call | tf_op jit(solution)/shard_map/take_rows/pallas_call | solution.py:485
  94.1 15.4 %all-to-all-done.3.got_ref = bf16[64,56,128]{2,1,0:T(8,128)(2,1)S(1)} async-done(((bf16[64,56,128]{2,1,0:T(8,128)(2,1)}), bf16[64,56,128]{2,1,0:T(8,128)(2,1)S(1)}, u32[]{:S(2)}, u32[]{:S(2)}) %all-to-all-start.3) | async-done | bytes 917536 | tf_op jit(solution)/shard_map/all_to_all | solution.py:27
  109.5 0.8 finish.1
  110.2 1.7 %collective-permute-start.6 = (bf16[1,3584]{1,0:T(2,128)(2,1)S(1)}, bf16[1,3584]{1,0:T(2,128)(2,1)S(1)}, u32[]{:S(2)}, u32[]{:S(2)}) collective-permute-start(bf16[1,3584]{1,0:T(2,128)(2,1)S(1)} %get-tuple-element.29), channel_id=1, source_target_pairs={{0,1},{1,0},{2,3},{3,2},{4,5},{5,4},{6,7},{7,6},{8,9},{9,8},{10,11... | collective-permute-start | bytes 21512 | tf_op jit(solution)/shard_map/ppermute | solution.py:23
  112.0 0.8 collective-permute-done.6
  112.8 0.7 broadcast_select_fusion
  (24 shorter events, 0.2 us)
Async XLA Ops:
  0.6 78.7 %collective-permute-start.4 = (bf16[384,7168]{1,0:T(8,128)(2,1)}, bf16[384,7168]{1,0:T(8,128)(2,1)}, u32[]{:S(2)}, u32[]{:S(2)}) collective-permute-start(bf16[384,7168]{1,0:T(8,128)(2,1)} %bitcast.20), channel_id=1, source_target_pairs={{0,1},{1,0},{2,3},{3,2},{4,5},{5,4},{6,7},{7,6},{8,9},{9,8},{10,11... | collective-permute-start | bytes 16515080 | tf_op jit(solution)/shard_map/ppermute | solution.py:23
  2.1 17.8 %collective-permute-start.1 = (bf16[128,7168]{1,0:T(8,128)(2,1)}, bf16[128,7168]{1,0:T(8,128)(2,1)S(1)}, u32[]{:S(2)}, u32[]{:S(2)}) collective-permute-start(bf16[128,7168]{1,0:T(8,128)(2,1)} %own_hbm.1), channel_id=1, source_target_pairs={{0,1},{1,0},{2,3},{3,2},{4,5},{5,4},{6,7},{7,6},{8,9},{9,8},{10,11... | collective-permute-start | bytes 5505032 | tf_op jit(solution)/shard_map/ppermute | solution.py:23
  6.4 22.3 %all-to-all-start = ((bf16[64,24,128]{2,1,0:T(8,128)(2,1)}), bf16[64,24,128]{2,1,0:T(8,128)(2,1)}, u32[]{:S(2)}, u32[]{:S(2)}) async-start(bf16[64,24,128]{2,1,0:T(8,128)(2,1)} %attend.1), calls=%async_computation | async-start | bytes 786432 | tf_op jit(solution)/shard_map/all_to_all | solution.py:27
  18.0 2.0 %collective-permute-start = (bf16[1,512,128]{2,1,0:T(8,128)(2,1)}, bf16[1,512,128]{2,1,0:T(8,128)(2,1)S(1)}, u32[]{:S(2)}, u32[]{:S(2)}) collective-permute-start(bf16[1,512,128]{2,1,0:T(8,128)(2,1)} %param.18), channel_id=1, source_target_pairs={{0,1},{1,0},{2,3},{3,2},{4,5},{5,4},{6,7},{7,6},{8,9},{9,8},{10,11... | collective-permute-start | bytes 393224 | tf_op jit(solution)/shard_map/ppermute | solution.py:23
  19.9 1.3 %copy-start.2 = (bf16[128,7168]{1,0:T(8,128)(2,1)}, bf16[128,7168]{1,0:T(8,128)(2,1)S(1)}, u32[]{:S(2)}) copy-start(bf16[128,7168]{1,0:T(8,128)(2,1)S(1)} %collective-permute-done.1.other_hbm) | copy-start | bytes 5505028
  21.2 1.5 %copy-start.1 = (bf16[128,7168]{1,0:T(8,128)(2,1)S(1)}, bf16[128,7168]{1,0:T(8,128)(2,1)}, u32[]{:S(2)}) copy-start(bf16[128,7168]{1,0:T(8,128)(2,1)} %own_hbm.1) | copy-start | bytes 5505028
  22.7 1.5 %copy-start.3 = (bf16[128,7168]{1,0:T(8,128)(2,1)S(1)}, bf16[128,7168]{1,0:T(8,128)(2,1)}, u32[]{:S(2)}) copy-start(bf16[128,7168]{1,0:T(8,128)(2,1)} %copy-done.2) | copy-start | bytes 5505028
  24.2 0.9 copy-start.4
  25.1 54.3 %slice-start = ((s8[5505024]{0:T(1024)(128)(4,1)}), s8[1310720]{0:T(1024)(128)(4,1)S(1)}, s32[]{:S(2)}) async-start(s8[5505024]{0:T(1024)(128)(4,1)} %bitcast.16), calls=%async_computation.4 | async-start | bytes 2621440
  28.7 50.6 %copy-start = (bf16[3,7168,128]{2,1,0:T(8,128)(2,1)S(1)}, bf16[3,7168,128]{2,1,0:T(8,128)(2,1)}, u32[]{:S(2)}) copy-start(bf16[3,7168,128]{2,1,0:T(8,128)(2,1)} %up_ref.3) | copy-start | bytes 16515076
  30.1 2.9 %collective-permute-start.2 = (bf16[224,128]{1,0:T(8,128)(2,1)S(1)}, bf16[224,128]{1,0:T(8,128)(2,1)S(1)}, u32[]{:S(2)}, u32[]{:S(2)}) collective-permute-start(bf16[224,128]{1,0:T(8,128)(2,1)S(1)} %get-tuple-element.19), channel_id=1, source_target_pairs={{0,1},{1,0},{2,3},{3,2},{4,5},{5,4},{6,7},{7,6},{8,9},{9,8},{10,11... | collective-permute-start | bytes 172040 | tf_op jit(solution)/shard_map/ppermute | solution.py:23
  33.1 46.3 %slice-start.1 = ((s8[5505024]{0:T(1024)(128)(4,1)}), s8[4194304]{0:T(1024)(128)(4,1)S(1)}, s32[]{:S(2)}) async-start(s8[5505024]{0:T(1024)(128)(4,1)} %bitcast.16), calls=%async_computation.5 | async-start | bytes 8388608
  34.1 45.3 %copy-start.5 = (f32[7168]{0:T(1024)S(1)}, f32[7168]{0:T(1024)}, u32[]{:S(2)}) copy-start(f32[7168]{0:T(1024)} %param.20) | copy-start | bytes 86020
  75.9 6.5 %collective-permute-start.3 = (bf16[64,8,896]{2,1,0:T(8,128)(2,1)S(1)}, bf16[64,8,896]{2,1,0:T(8,128)(2,1)S(1)}, u32[]{:S(2)}, u32[]{:S(2)}) collective-permute-start(bf16[64,8,896]{2,1,0:T(8,128)(2,1)S(1)} %all_to_all.21), channel_id=1, source_target_pairs={{0,1},{1,0},{2,3},{3,2},{4,5},{5,4},{6,7},{7,6},{8,9},{9,8},{10,11... | collective-permute-start | bytes 2752520 | tf_op jit(solution)/shard_map/ppermute | solution.py:23
  82.4 2.9 %slice-start.2 = ((s8[5505024]{0:T(1024)(128)(4,1)}), s8[4194304]{0:T(1024)(128)(4,1)S(1)}, s32[]{:S(2)}) async-start(s8[5505024]{0:T(1024)(128)(4,1)} %bitcast.21), calls=%async_computation.6 | async-start | bytes 8388608
  82.5 2.9 %slice-start.3 = ((s8[5505024]{0:T(1024)(128)(4,1)}), s8[1310720]{0:T(1024)(128)(4,1)S(1)}, s32[]{:S(2)}) async-start(s8[5505024]{0:T(1024)(128)(4,1)} %bitcast.21), calls=%async_computation.7 | async-start | bytes 2621440
  84.0 1.4 %collective-permute-start.5 = (bf16[128,384]{1,0:T(8,128)(2,1)S(1)}, bf16[128,384]{1,0:T(8,128)(2,1)S(1)}, u32[]{:S(2)}, u32[]{:S(2)}) collective-permute-start(bf16[128,384]{1,0:T(8,128)(2,1)S(1)} %gate_up_second.1.after_ref.act_own_ref), channel_id=1, source_target_pairs={{0,1},{1,0},{2,3},{3,2},{4,5},{5,4},{6,7},{7,6},{8,9},{9,8},{10,11... | collective-permute-start | bytes 294920 | tf_op jit(solution)/shard_map/ppermute | solution.py:23
  88.2 21.3 %all-to-all-start.3 = ((bf16[64,56,128]{2,1,0:T(8,128)(2,1)}), bf16[64,56,128]{2,1,0:T(8,128)(2,1)S(1)}, u32[]{:S(2)}, u32[]{:S(2)}) async-start(bf16[64,56,128]{2,1,0:T(8,128)(2,1)} %down.1), calls=%async_computation.3 | async-start | bytes 1835008 | tf_op jit(solution)/shard_map/all_to_all | solution.py:27
  110.2 2.6 %collective-permute-start.6 = (bf16[1,3584]{1,0:T(2,128)(2,1)S(1)}, bf16[1,3584]{1,0:T(2,128)(2,1)S(1)}, u32[]{:S(2)}, u32[]{:S(2)}) collective-permute-start(bf16[1,3584]{1,0:T(2,128)(2,1)S(1)} %get-tuple-element.29), channel_id=1, source_target_pairs={{0,1},{1,0},{2,3},{3,2},{4,5},{5,4},{6,7},{7,6},{8,9},{9,8},{10,11... | collective-permute-start | bytes 21512 | tf_op jit(solution)/shard_map/ppermute | solution.py:23

commit v5 on v4

--- a/solution.py
+++ b/solution.py
@@ -415,7 +415,18 @@
 DOWN_COLUMNS = 512
 
 
-def down_kernel(place_ref, act_own_ref, act_other_ref, own_ref, other_ref, out_ref, sum_ref, pack_ref):
+def down_kernel(
+    place_ref,
+    act_own_ref,
+    act_other_ref,
+    own_ref,
+    other_ref,
+    after_ref,
+    out_ref,
+    sum_ref,
+    pack_ref,
+):
+    del after_ref
     core = place_ref[0]
     lanes = 128
     half = own_ref.shape[1] // 2
@@ -436,14 +447,16 @@
         out_ref[:, rows, :] = pack_ref[slot].astype(BF).reshape(CHIPS, 2 * tiles, lanes)
 
 
-def down(place, act_own, act_other, own, other):
+def down(place, act_own, act_other, own, other, after):
     rows = act_own.shape[0]
     out_rows = own.shape[1] // 128
     tiles = DOWN_COLUMNS // 128
     whole = pl.BlockSpec(memory_space=pltpu.VMEM)
     return pl.pallas_call(
         down_kernel,
-        in_specs=[pl.BlockSpec(memory_space=pltpu.SMEM)] + [whole] * 4,
+        in_specs=[pl.BlockSpec(memory_space=pltpu.SMEM)]
+        + [whole] * 4
+        + [pl.BlockSpec(memory_space=pl.ANY)],
         out_specs=whole,
         out_shape=jax.ShapeDtypeStruct((CHIPS, out_rows, 128), BF),
         scratch_shapes=[
@@ -452,7 +465,7 @@
         ],
         compiler_params=limit(8),
         name="down",
-    )(place, act_own, act_other, own, other)
+    )(place, act_own, act_other, own, other, after)
 
 
 def rows_kernel(place_ref, own_ref, other_ref, after_ref, residual_ref, rows_ref):
@@ -571,7 +584,7 @@
         place, rows_own, rows_other, norm_gain, route, w_gate, w_up, down_other
     )
     residual, chip_rows = take_rows(place, rows_own, rows_other, act)
-    output = down(place, act, swap(act), down_own, down_half)
+    output = down(place, act, swap(act), down_own, down_half, chip_rows)
     mine, send = finish(place, exchange(output), chip_rows)
     got = swap(send)
     layer_out = jnp.where(

time: 114 us -> 113 us (level)
  blocking collectives: 41.5 us -> 62 us
  waiting for transfers between devices: 22.1 us -> 5.45 us
  starting transfers between devices: 25.8 us -> 21.6 us
    all_to_all x2 -> x3, blocking collectives: 41.5 us -> 62 us  [exchange(): lax.all_to_all(value, CHIP_AXES, split_axis=0, concat_axis=0, tiled=True)]
    all_to_all x2 -> x1, waiting for transfers between devices: 17.9 us -> 2.58 us  [exchange(): lax.all_to_all(value, CHIP_AXES, split_axis=0, concat_axis=0, tiled=True)]
    all_to_all x2 -> x1, starting transfers between devices: 16.1 us -> 11.5 us  [exchange(): lax.all_to_all(value, CHIP_AXES, split_axis=0, concat_axis=0, tiled=True)]
    ppermute x7, waiting for transfers between devices: 4.14 us -> 2.87 us  [swap(): return lax.ppermute(value, 'core', SWAP)]
  transfers between devices with their start and end apart: 9 -> 8, of which waited for: 6 -> 4; matrix products, arithmetic and copies ran while one was open for 0% -> 0% of each run, Pallas kernels for 10% -> 10%
where the time goes in v5:
time: 113 us; the launch traced here: 112 us
  blocking collectives  62 us (55%)
  starting transfers between devices  21.6 us (19%)
  Pallas kernels  15.5 us (14%)
  waiting for transfers between devices  5.45 us (5%)
  local copies, waits for them, and re-layouts  5.25 us (5%)
  between operations  1.43 us (1%)
    all_to_all x3, blocking collectives, exchange(): lax.all_to_all(value, CHIP_AXES, split_axis=0, concat_axis=0, tiled=True)  62 us
    all_to_all x1, starting transfers between devices, exchange(): lax.all_to_all(value, CHIP_AXES, split_axis=0, concat_axis=0, tiled=True)  11.5 us
    ppermute x7, starting transfers between devices, swap(): return lax.ppermute(value, 'core', SWAP)  10.1 us
    unnamed x20, local copies, waits for them, and re-layouts  5.18 us
    pallas_call x1, Pallas kernels, attend_and_pack(): pl.pallas_call(attend_kernel, in_specs=[pl.BlockSpec(memory_space=pltpu.S...  3.61 us
    pallas_call x1, Pallas kernels, gate_up(): pl.pallas_call(first_kernel, in_specs=[where] + [whole] * 4 + [pl.BlockSp...  3.06 us
    ppermute x7, waiting for transfers between devices, swap(): return lax.ppermute(value, 'core', SWAP)  2.87 us
    all_to_all x1, waiting for transfers between devices, exchange(): lax.all_to_all(value, CHIP_AXES, split_axis=0, concat_axis=0, tiled=True)  2.58 us
  transfers between devices with their start and end apart: 8, of which 4 were waited for; matrix products, arithmetic and copies ran while one was open for 0% of the time, Pallas kernels for 10%

profile of v5, /device:TPU:1, one launch (start us, length us, event | category | flops | bytes accessed | tf_op | source)
XLA Modules:
  0.0 112.1 jit_solution(4207158719562492052)
XLA Ops:
  0.6 1.5 %collective-permute-start.4 = (bf16[384,7168]{1,0:T(8,128)(2,1)}, bf16[384,7168]{1,0:T(8,128)(2,1)}, u32[]{:S(2)}, u32[]{:S(2)}) collective-permute-start(bf16[384,7168]{1,0:T(8,128)(2,1)} %bitcast.20), channel_id=1, source_target_pairs={{0,1},{1,0},{2,3},{3,2},{4,5},{5,4},{6,7},{7,6},{8,9},{9,8},{10,11... | collective-permute-start | bytes 16515080 | tf_op jit(solution)/shard_map/ppermute | solution.py:23
  2.1 0.1 collective-permute-start.1
  2.8 3.6 %attend.1 = bf16[64,24,128]{2,1,0:T(8,128)(2,1)} custom-call(s32[1]{0:T(128)S(6)} %copy.15.length_ref, bf16[576,128]{1,0:T(8,128)(2,1)} %bitcast.32, bf16[576,1024]{1,0:T(8,128)(2,1)} %bitcast.31, bf16[1,576]{1,0:T(2,128)(2,1)} %newest_hbm.1, bf16[1,7168]{1,0:T(2,128)(2,1)} %states_hbm.1, s32[1,8]{1,0:T(1,128)} %ids_hbm.1, f32[1,8]{1,0:T(1,128)} %score_hbm.1), custom_call_target="tpu_custom_call" | custom-call | tf_op jit(solution)/shard_map/attend/pallas_call | solution.py:147
  6.5 11.5 %all-to-all-start = ((bf16[64,24,128]{2,1,0:T(8,128)(2,1)}), bf16[64,24,128]{2,1,0:T(8,128)(2,1)}, u32[]{:S(2)}, u32[]{:S(2)}) async-start(bf16[64,24,128]{2,1,0:T(8,128)(2,1)} %attend.1), calls=%async_computation | async-start | bytes 786432 | tf_op jit(solution)/shard_map/all_to_all | solution.py:27
  18.0 0.8 collective-permute-start
  18.7 0.1 pad_add_fusion.place_ref
  18.8 1.1 collective-permute-done
  19.9 1.2 %copy-done.2 = bf16[128,7168]{1,0:T(8,128)(2,1)} copy-done((bf16[128,7168]{1,0:T(8,128)(2,1)}, bf16[128,7168]{1,0:T(8,128)(2,1)S(1)}, u32[]{:S(2)}) %copy-start.2) | copy-done | bytes 1835032
  21.2 1.5 %copy-done.1 = bf16[128,7168]{1,0:T(8,128)(2,1)S(1)} copy-done((bf16[128,7168]{1,0:T(8,128)(2,1)S(1)}, bf16[128,7168]{1,0:T(8,128)(2,1)}, u32[]{:S(2)}) %copy-start.1) | copy-done | bytes 1835032
  22.7 1.5 %copy-done.3 = bf16[128,7168]{1,0:T(8,128)(2,1)S(1)} copy-done((bf16[128,7168]{1,0:T(8,128)(2,1)S(1)}, bf16[128,7168]{1,0:T(8,128)(2,1)}, u32[]{:S(2)}) %copy-start.3) | copy-done | bytes 1835032
  24.2 0.9 copy-done.4
  25.1 1.1 fetch.1
  26.2 2.6 %all-to-all-done.got_ref = bf16[64,24,128]{2,1,0:T(8,128)(2,1)} async-done(((bf16[64,24,128]{2,1,0:T(8,128)(2,1)}), bf16[64,24,128]{2,1,0:T(8,128)(2,1)}, u32[]{:S(2)}, u32[]{:S(2)}) %all-to-all-start) | async-done | bytes 393248 | tf_op jit(solution)/shard_map/all_to_all | solution.py:27
  28.7 1.4 %values.1 = (bf16[224,128]{1,0:T(8,128)(2,1)S(1)}, bf16[224,128]{1,0:T(8,128)(2,1)S(1)}) custom-call(s32[3]{0:T(128)S(1)} %pad_add_fusion.place_ref, bf16[64,24,128]{2,1,0:T(8,128)(2,1)} %all-to-all-done.got_ref, bf16[2,512,128]{2,1,0:T(8,128)(2,1)S(1)} %get-tuple-element.16.uv_ref, bf16[256,3584]{1,0:T(8,128)(2,1)S(1)} %get-tuple-element.17.after_ref.weights_ref), custom_call_target="tpu_custom_call" | custom-call | tf_op jit(solution)/shard_map/values/pallas_call | solution.py:207
  30.1 2.0 %collective-permute-start.2 = (bf16[224,128]{1,0:T(8,128)(2,1)S(1)}, bf16[224,128]{1,0:T(8,128)(2,1)S(1)}, u32[]{:S(2)}, u32[]{:S(2)}) collective-permute-start(bf16[224,128]{1,0:T(8,128)(2,1)S(1)} %get-tuple-element.19), channel_id=1, source_target_pairs={{0,1},{1,0},{2,3},{3,2},{4,5},{5,4},{6,7},{7,6},{8,9},{9,8},{10,11... | collective-permute-start | bytes 172040 | tf_op jit(solution)/shard_map/ppermute | solution.py:23
  32.2 0.9 collective-permute-done.2.got_ref
  33.1 1.0 out_projection.1
  34.1 22.0 %all_to_all.20 = bf16[64,8,896]{2,1,0:T(8,128)(2,1)S(1)} all-to-all(bf16[64,8,896]{2,1,0:T(8,128)(2,1)S(1)} %bitcast.26), channel_id=1, replica_groups=mesh['x'=4,'z'=4,'y'=4,'core'=2] {'z','x','y'}, dimensions={0} | all-to-all | bytes 1835008 | tf_op jit(solution)/shard_map/all_to_all | solution.py:27
  56.1 0.2 convert_reduce_fusion
  56.3 0.1 broadcast_in_dim.4
  56.4 19.5 %all_to_all.21 = bf16[64,8,896]{2,1,0:T(8,128)(2,1)S(1)} all-to-all(bf16[64,8,896]{2,1,0:T(8,128)(2,1)S(1)} %broadcast_in_dim.4), channel_id=1, replica_groups=mesh['x'=4,'z'=4,'y'=4,'core'=2] {'z','x','y'}, dimensions={0} | all-to-all | bytes 1835008 | tf_op jit(solution)/shard_map/all_to_all | solution.py:27
  75.9 3.4 %collective-permute-start.3 = (bf16[64,8,896]{2,1,0:T(8,128)(2,1)S(1)}, bf16[64,8,896]{2,1,0:T(8,128)(2,1)S(1)}, u32[]{:S(2)}, u32[]{:S(2)}) collective-permute-start(bf16[64,8,896]{2,1,0:T(8,128)(2,1)S(1)} %all_to_all.21), channel_id=1, source_target_pairs={{0,1},{1,0},{2,3},{3,2},{4,5},{5,4},{6,7},{7,6},{8,9},{9,8},{10,11... | collective-permute-start | bytes 2752520 | tf_op jit(solution)/shard_map/ppermute | solution.py:23
  79.4 3.1 %gate_up_first.1 = (f32[128,128]{1,0:T(8,128)S(1)}, f32[3,128,256]{2,1,0:T(8,128)S(1)}, bf16[384,3584]{1,0:T(8,128)(2,1)S(1)}) custom-call(s32[3]{0:T(128)S(1)} %pad_add_fusion.place_ref, bf16[16,4,8,896]{3,2,1,0:T(8,128)(2,1)S(1)} %bitcast.18, f32[1,7168]{1,0:T(1,128)S(1)} %bitcast.29, bf16[3,7168,128]{2,1,0:T(8,128)(2,1)S(1)} %bitcast.17, ...), custom_call_target="tpu_custom_call" | custom-call | tf_op jit(solution)/shard_map/gate_up_first/pallas_call | solution.py:391
  82.5 1.5 %gate_up_second.1.after_ref.act_own_ref = bf16[128,384]{1,0:T(8,128)(2,1)S(1)} custom-call(s32[3]{0:T(128)S(1)} %pad_add_fusion.place_ref, bf16[16,4,8,896]{3,2,1,0:T(8,128)(2,1)S(1)} %bitcast.24, f32[1,7168]{1,0:T(1,128)S(1)} %bitcast.30, bf16[3,7168,128]{2,1,0:T(8,128)(2,1)S(1)} %bitcast.17, bf16[3,7168,128]{2,1,0:T(8,128)(2,1)S(1)} %copy-done, ...), custom_call_target="tpu_custom_call" | custom-call | tf_op jit(solution)/shard_map/gate_up_second/pallas_call | solution.py:404
  84.0 0.1 collective-permute-start.5
  84.1 1.3 %take_rows.1 = (bf16[1,7168]{1,0:T(2,128)(2,1)}, f32[2,3584]{1,0:T(2,128)S(1)}) custom-call(s32[3]{0:T(128)S(1)} %pad_add_fusion.place_ref, bf16[16,4,8,896]{3,2,1,0:T(8,128)(2,1)S(1)} %bitcast.19, bf16[16,4,8,896]{3,2,1,0:T(8,128)(2,1)S(1)} %bitcast.25, bf16[128,384]{1,0:T(8,128)(2,1)S(1)} %gate_up_second.1.after_ref.act_own_ref), custom_call_target="tpu_custom_call" | custom-call | tf_op jit(solution)/shard_map/take_rows/pallas_call | solution.py:498
  85.4 1.8 %down.1 = bf16[64,56,128]{2,1,0:T(8,128)(2,1)S(1)} custom-call(s32[3]{0:T(128)S(1)} %pad_add_fusion.place_ref, bf16[128,384]{1,0:T(8,128)(2,1)S(1)} %gate_up_second.1.after_ref.act_own_ref, bf16[128,384]{1,0:T(8,128)(2,1)S(1)} %collective-permute-done.5.act_other_ref, bf16[384,7168]{1,0:T(8,128)(2,1)S(1)} %bitcast.23, ...), custom_call_target="tpu_custom_call" | custom-call | tf_op jit(solution)/shard_map/down/pallas_call | solution.py:455
  87.2 20.5 %all_to_all.22.got_ref = bf16[64,56,128]{2,1,0:T(8,128)(2,1)S(1)} all-to-all(bf16[64,56,128]{2,1,0:T(8,128)(2,1)S(1)} %down.1), channel_id=1, replica_groups=mesh['x'=4,'z'=4,'y'=4,'core'=2] {'z','x','y'}, dimensions={0} | all-to-all | bytes 1835008 | tf_op jit(solution)/shard_map/all_to_all | solution.py:27
  107.7 0.8 finish.1
  108.4 2.2 %collective-permute-start.6 = (bf16[1,3584]{1,0:T(2,128)(2,1)S(1)}, bf16[1,3584]{1,0:T(2,128)(2,1)S(1)}, u32[]{:S(2)}, u32[]{:S(2)}) collective-permute-start(bf16[1,3584]{1,0:T(2,128)(2,1)S(1)} %get-tuple-element.29), channel_id=1, source_target_pairs={{0,1},{1,0},{2,3},{3,2},{4,5},{5,4},{6,7},{7,6},{8,9},{9,8},{10,11... | collective-permute-start | bytes 21512 | tf_op jit(solution)/shard_map/ppermute | solution.py:23
  110.6 0.8 collective-permute-done.6
  111.5 0.7 broadcast_select_fusion
  (23 shorter events, 0.1 us)
Async XLA Ops:
  0.6 78.7 %collective-permute-start.4 = (bf16[384,7168]{1,0:T(8,128)(2,1)}, bf16[384,7168]{1,0:T(8,128)(2,1)}, u32[]{:S(2)}, u32[]{:S(2)}) collective-permute-start(bf16[384,7168]{1,0:T(8,128)(2,1)} %bitcast.20), channel_id=1, source_target_pairs={{0,1},{1,0},{2,3},{3,2},{4,5},{5,4},{6,7},{7,6},{8,9},{9,8},{10,11... | collective-permute-start | bytes 16515080 | tf_op jit(solution)/shard_map/ppermute | solution.py:23
  2.1 17.8 %collective-permute-start.1 = (bf16[128,7168]{1,0:T(8,128)(2,1)}, bf16[128,7168]{1,0:T(8,128)(2,1)S(1)}, u32[]{:S(2)}, u32[]{:S(2)}) collective-permute-start(bf16[128,7168]{1,0:T(8,128)(2,1)} %own_hbm.1), channel_id=1, source_target_pairs={{0,1},{1,0},{2,3},{3,2},{4,5},{5,4},{6,7},{7,6},{8,9},{9,8},{10,11... | collective-permute-start | bytes 5505032 | tf_op jit(solution)/shard_map/ppermute | solution.py:23
  6.5 22.3 %all-to-all-start = ((bf16[64,24,128]{2,1,0:T(8,128)(2,1)}), bf16[64,24,128]{2,1,0:T(8,128)(2,1)}, u32[]{:S(2)}, u32[]{:S(2)}) async-start(bf16[64,24,128]{2,1,0:T(8,128)(2,1)} %attend.1), calls=%async_computation | async-start | bytes 786432 | tf_op jit(solution)/shard_map/all_to_all | solution.py:27
  18.0 2.0 %collective-permute-start = (bf16[1,512,128]{2,1,0:T(8,128)(2,1)}, bf16[1,512,128]{2,1,0:T(8,128)(2,1)S(1)}, u32[]{:S(2)}, u32[]{:S(2)}) collective-permute-start(bf16[1,512,128]{2,1,0:T(8,128)(2,1)} %param.18), channel_id=1, source_target_pairs={{0,1},{1,0},{2,3},{3,2},{4,5},{5,4},{6,7},{7,6},{8,9},{9,8},{10,11... | collective-permute-start | bytes 393224 | tf_op jit(solution)/shard_map/ppermute | solution.py:23
  19.9 1.2 %copy-start.2 = (bf16[128,7168]{1,0:T(8,128)(2,1)}, bf16[128,7168]{1,0:T(8,128)(2,1)S(1)}, u32[]{:S(2)}) copy-start(bf16[128,7168]{1,0:T(8,128)(2,1)S(1)} %collective-permute-done.1.other_hbm) | copy-start | bytes 5505028
  21.2 1.5 %copy-start.1 = (bf16[128,7168]{1,0:T(8,128)(2,1)S(1)}, bf16[128,7168]{1,0:T(8,128)(2,1)}, u32[]{:S(2)}) copy-start(bf16[128,7168]{1,0:T(8,128)(2,1)} %own_hbm.1) | copy-start | bytes 5505028
  22.7 1.5 %copy-start.3 = (bf16[128,7168]{1,0:T(8,128)(2,1)S(1)}, bf16[128,7168]{1,0:T(8,128)(2,1)}, u32[]{:S(2)}) copy-start(bf16[128,7168]{1,0:T(8,128)(2,1)} %copy-done.2) | copy-start | bytes 5505028
  24.2 0.9 copy-start.4
  25.1 54.3 %slice-start = ((s8[5505024]{0:T(1024)(128)(4,1)}), s8[1310720]{0:T(1024)(128)(4,1)S(1)}, s32[]{:S(2)}) async-start(s8[5505024]{0:T(1024)(128)(4,1)} %bitcast.16), calls=%async_computation.4 | async-start | bytes 2621440
  28.7 50.6 %copy-start = (bf16[3,7168,128]{2,1,0:T(8,128)(2,1)S(1)}, bf16[3,7168,128]{2,1,0:T(8,128)(2,1)}, u32[]{:S(2)}) copy-start(bf16[3,7168,128]{2,1,0:T(8,128)(2,1)} %up_ref.3) | copy-start | bytes 16515076
  30.1 2.9 %collective-permute-start.2 = (bf16[224,128]{1,0:T(8,128)(2,1)S(1)}, bf16[224,128]{1,0:T(8,128)(2,1)S(1)}, u32[]{:S(2)}, u32[]{:S(2)}) collective-permute-start(bf16[224,128]{1,0:T(8,128)(2,1)S(1)} %get-tuple-element.19), channel_id=1, source_target_pairs={{0,1},{1,0},{2,3},{3,2},{4,5},{5,4},{6,7},{7,6},{8,9},{9,8},{10,11... | collective-permute-start | bytes 172040 | tf_op jit(solution)/shard_map/ppermute | solution.py:23
  33.1 46.3 %slice-start.1 = ((s8[5505024]{0:T(1024)(128)(4,1)}), s8[4194304]{0:T(1024)(128)(4,1)S(1)}, s32[]{:S(2)}) async-start(s8[5505024]{0:T(1024)(128)(4,1)} %bitcast.16), calls=%async_computation.5 | async-start | bytes 8388608
  34.1 45.3 %copy-start.5 = (f32[7168]{0:T(1024)S(1)}, f32[7168]{0:T(1024)}, u32[]{:S(2)}) copy-start(f32[7168]{0:T(1024)} %param.20) | copy-start | bytes 86020
  75.9 6.5 %collective-permute-start.3 = (bf16[64,8,896]{2,1,0:T(8,128)(2,1)S(1)}, bf16[64,8,896]{2,1,0:T(8,128)(2,1)S(1)}, u32[]{:S(2)}, u32[]{:S(2)}) collective-permute-start(bf16[64,8,896]{2,1,0:T(8,128)(2,1)S(1)} %all_to_all.21), channel_id=1, source_target_pairs={{0,1},{1,0},{2,3},{3,2},{4,5},{5,4},{6,7},{7,6},{8,9},{9,8},{10,11... | collective-permute-start | bytes 2752520 | tf_op jit(solution)/shard_map/ppermute | solution.py:23
  82.4 2.9 %slice-start.2 = ((s8[5505024]{0:T(1024)(128)(4,1)}), s8[4194304]{0:T(1024)(128)(4,1)S(1)}, s32[]{:S(2)}) async-start(s8[5505024]{0:T(1024)(128)(4,1)} %bitcast.21), calls=%async_computation.6 | async-start | bytes 8388608
  82.5 2.9 %slice-start.3 = ((s8[5505024]{0:T(1024)(128)(4,1)}), s8[1310720]{0:T(1024)(128)(4,1)S(1)}, s32[]{:S(2)}) async-start(s8[5505024]{0:T(1024)(128)(4,1)} %bitcast.21), calls=%async_computation.7 | async-start | bytes 2621440
  84.0 1.4 %collective-permute-start.5 = (bf16[128,384]{1,0:T(8,128)(2,1)S(1)}, bf16[128,384]{1,0:T(8,128)(2,1)S(1)}, u32[]{:S(2)}, u32[]{:S(2)}) collective-permute-start(bf16[128,384]{1,0:T(8,128)(2,1)S(1)} %gate_up_second.1.after_ref.act_own_ref), channel_id=1, source_target_pairs={{0,1},{1,0},{2,3},{3,2},{4,5},{5,4},{6,7},{7,6},{8,9},{9,8},{10,11... | collective-permute-start | bytes 294920 | tf_op jit(solution)/shard_map/ppermute | solution.py:23
  108.4 3.1 %collective-permute-start.6 = (bf16[1,3584]{1,0:T(2,128)(2,1)S(1)}, bf16[1,3584]{1,0:T(2,128)(2,1)S(1)}, u32[]{:S(2)}, u32[]{:S(2)}) collective-permute-start(bf16[1,3584]{1,0:T(2,128)(2,1)S(1)} %get-tuple-element.29), channel_id=1, source_target_pairs={{0,1},{1,0},{2,3},{3,2},{4,5},{5,4},{6,7},{7,6},{8,9},{9,8},{10,11... | collective-permute-start | bytes 21512 | tf_op jit(solution)/shard_map/ppermute | solution.py:23

commit v6 on v5

--- a/solution.py
+++ b/solution.py
@@ -339,31 +339,11 @@
     return total, sums
 
 
-COPIES = 6
-
-
-def first_kernel(
-    place_ref, rows_ref, gain_ref, gate_ref, up_ref, down_hbm, total_ref, sums_ref, down_ref, done
-):
-    half = down_ref.shape[1]
-    columns = pl.ds(pl.multiple_of(place_ref[0] * half, 128), half)
-    piece = down_ref.shape[0] // COPIES
-    copies = [
-        pltpu.make_async_copy(
-            down_hbm.at[index * piece : (index + 1) * piece, columns],
-            down_ref.at[index * piece : (index + 1) * piece],
-            done.at[index],
-        )
-        for index in range(COPIES)
-    ]
-    for copy in copies:
-        copy.start()
+def first_kernel(place_ref, rows_ref, gain_ref, gate_ref, up_ref, total_ref, sums_ref):
     total, sums = half_products(place_ref[0], rows_ref, gain_ref, gate_ref, up_ref)
     total_ref[...] = jnp.broadcast_to(total, total_ref.shape)
     for e, value in enumerate(sums):
         sums_ref[e] = value
-    for copy in copies:
-        copy.wait()
 
 
 def second_kernel(
@@ -381,26 +361,23 @@
         act_ref[:, e * hidden : (e + 1) * hidden] = active.astype(BF)
 
 
-def gate_up(place, own, other, gain, route, w_gate, w_up, down_other):
+def gate_up(place, own, other, gain, route, w_gate, w_up):
     groups, _, eight, wide = own.shape
     rows = groups * eight
     experts, model, hidden = w_gate.shape
     whole = pl.BlockSpec(memory_space=pltpu.VMEM)
     where = pl.BlockSpec(memory_space=pltpu.SMEM)
-    down_rows, down_columns = down_other.shape
-    total, sums, down_half = pl.pallas_call(
+    total, sums = pl.pallas_call(
         first_kernel,
-        in_specs=[where] + [whole] * 4 + [pl.BlockSpec(memory_space=pltpu.HBM)],
-        out_specs=(whole, whole, whole),
+        in_specs=[where] + [whole] * 4,
+        out_specs=(whole, whole),
         out_shape=(
             jax.ShapeDtypeStruct((rows, 128), F32),
             jax.ShapeDtypeStruct((experts, rows, 2 * hidden), F32),
-            jax.ShapeDtypeStruct((down_rows, down_columns // 2), BF),
         ),
-        scratch_shapes=[pltpu.SemaphoreType.DMA((COPIES,))],
         compiler_params=limit(12),
         name="gate_up_first",
-    )(place, own, gain[None], w_gate, w_up, down_other)
+    )(place, own, gain[None], w_gate, w_up)
     act = pl.pallas_call(
         second_kernel,
         in_specs=[where] + [whole] * 7,
@@ -409,7 +386,7 @@
         compiler_params=limit(12),
         name="gate_up_second",
     )(place, other, gain[None], w_gate, w_up, total, sums, route)
-    return act, down_half
+    return act
 
 
 DOWN_COLUMNS = 512
@@ -420,7 +397,7 @@
     act_own_ref,
     act_other_ref,
     own_ref,
-    other_ref,
+    other_refs,
     after_ref,
     out_ref,
     sum_ref,
@@ -435,8 +412,7 @@
     for step in range(half // DOWN_COLUMNS):
         slot = step % 2
         at = pl.ds(pl.multiple_of(core * half + step * DOWN_COLUMNS, 512), DOWN_COLUMNS)
-        other = other_ref[:, step * DOWN_COLUMNS : (step + 1) * DOWN_COLUMNS]
-        weights = jnp.concatenate([own_ref[:, at], other], axis=0)
+        weights = jnp.concatenate([own_ref[:, at]] + [ref[:, at] for ref in other_refs], axis=0)
         product = jnp.dot(act, weights, preferred_element_type=F32)
         for t in range(tiles):
             sum_ref[slot, t] = product[:, t * lanes : (t + 1) * lanes]
@@ -454,9 +430,14 @@
     whole = pl.BlockSpec(memory_space=pltpu.VMEM)
     return pl.pallas_call(
         down_kernel,
-        in_specs=[pl.BlockSpec(memory_space=pltpu.SMEM)]
-        + [whole] * 4
-        + [pl.BlockSpec(memory_space=pl.ANY)],
+        in_specs=[
+            pl.BlockSpec(memory_space=pltpu.SMEM),
+            whole,
+            whole,
+            whole,
+            [whole] * len(other),
+            pl.BlockSpec(memory_space=pl.ANY),
+        ],
         out_specs=whole,
         out_shape=jax.ShapeDtypeStruct((CHIPS, out_rows, 128), BF),
         scratch_shapes=[
@@ -562,7 +543,6 @@
     down_own = w_down.reshape(-1, model)
     uv_other = swap(w_uv)
     out_other = swap(w_out)
-    down_other = swap(down_own)
     place = jnp.stack([core, group, quarter])
 
     sent = attend_and_pack(
@@ -572,6 +552,8 @@
     uv, weights = fetch_halves(place, w_uv[0], uv_other[0], w_out, out_other)
     mine, send = project_values(place, got, uv, weights)
     partial, route, my_states = out_projection(place, mine, swap(send), weights)
+    partial, down_sent = lax.optimization_barrier((partial, down_own))
+    down_other = [swap(down_sent)]
     partial = exchange(partial.reshape(CHIPS, 8, wide))
     attention = jnp.sum(partial.astype(F32), axis=0)
     residual_part = (my_states + attention).astype(BF)
@@ -580,11 +562,9 @@
     rows_own = rows_own.reshape(GROUPS, NY, 8, wide)
     rows_other = rows_other.reshape(GROUPS, NY, 8, wide)
 
-    act, down_half = gate_up(
-        place, rows_own, rows_other, norm_gain, route, w_gate, w_up, down_other
-    )
+    act = gate_up(place, rows_own, rows_other, norm_gain, route, w_gate, w_up)
     residual, chip_rows = take_rows(place, rows_own, rows_other, act)
-    output = down(place, act, swap(act), down_own, down_half, chip_rows)
+    output = down(place, act, swap(act), down_own, down_other, chip_rows)
     mine, send = finish(place, exchange(output), chip_rows)
     got = swap(send)
     layer_out = jnp.where(

time: 113 us -> 112 us (level)
  Pallas kernels: 15.5 us -> 13.8 us
    pallas_call x1, Pallas kernels: 3.06 us -> 1.44 us  [gate_up(): pl.pallas_call(first_kernel, in_specs=[where] + [whole] * 4, out_specs=(w...]
    unnamed x20 -> x24, local copies, waits for them, and re-layouts: 5.18 us -> 5.84 us
  transfers between devices with their start and end apart: 8 -> 8, of which waited for: 4 -> 5; matrix products, arithmetic and copies ran while one was open for 0% -> 0% of each run, Pallas kernels for 10% -> 8%
where the time goes in v6:
time: 112 us
  blocking collectives  62.5 us (56%)
  starting transfers between devices  21 us (19%)
  Pallas kernels  13.8 us (12%)
  waiting for transfers between devices  6.18 us (6%)
  local copies, waits for them, and re-layouts  5.91 us (5%)
  between operations  1.41 us (1%)
    all_to_all x3, blocking collectives, exchange(): lax.all_to_all(value, CHIP_AXES, split_axis=0, concat_axis=0, tiled=True)  62.5 us
    all_to_all x1, starting transfers between devices, exchange(): lax.all_to_all(value, CHIP_AXES, split_axis=0, concat_axis=0, tiled=True)  11.5 us
    ppermute x7, starting transfers between devices, swap(): return lax.ppermute(value, 'core', SWAP)  9.55 us
    unnamed x24, local copies, waits for them, and re-layouts  5.84 us
    pallas_call x1, Pallas kernels, attend_and_pack(): pl.pallas_call(attend_kernel, in_specs=[pl.BlockSpec(memory_space=pltpu.S...  3.54 us
    ppermute x7, waiting for transfers between devices, swap(): return lax.ppermute(value, 'core', SWAP)  3.36 us
    all_to_all x1, waiting for transfers between devices, exchange(): lax.all_to_all(value, CHIP_AXES, split_axis=0, concat_axis=0, tiled=True)  2.83 us
  transfers between devices with their start and end apart: 8, of which 5 were waited for; matrix products, arithmetic and copies ran while one was open for 0% of the time, Pallas kernels for 8%

profile of v6, /device:TPU:1, one launch (start us, length us, event | category | flops | bytes accessed | tf_op | source)
XLA Modules:
  0.0 111.8 jit_solution(8551115386540575371)
XLA Ops:
  0.6 1.5 %collective-permute-start.1 = (bf16[128,7168]{1,0:T(8,128)(2,1)}, bf16[128,7168]{1,0:T(8,128)(2,1)S(1)}, u32[]{:S(2)}, u32[]{:S(2)}) collective-permute-start(bf16[128,7168]{1,0:T(8,128)(2,1)} %own_hbm.1), channel_id=1, source_target_pairs={{0,1},{1,0},{2,3},{3,2},{4,5},{5,4},{6,7},{7,6},{8,9},{9,8},{10,11... | collective-permute-start | bytes 5505032 | tf_op jit(solution)/shard_map/ppermute | solution.py:23
  2.8 3.5 %attend.1 = bf16[64,24,128]{2,1,0:T(8,128)(2,1)} custom-call(s32[1]{0:T(128)S(6)} %copy.15.length_ref, bf16[576,128]{1,0:T(8,128)(2,1)} %bitcast.32, bf16[576,1024]{1,0:T(8,128)(2,1)} %bitcast.31, bf16[1,576]{1,0:T(2,128)(2,1)} %newest_hbm.1, bf16[1,7168]{1,0:T(2,128)(2,1)} %states_hbm.1, s32[1,8]{1,0:T(1,128)} %ids_hbm.1, f32[1,8]{1,0:T(1,128)} %score_hbm.1), custom_call_target="tpu_custom_call" | custom-call | tf_op jit(solution)/shard_map/attend/pallas_call | solution.py:147
  6.3 11.5 %all-to-all-start = ((bf16[64,24,128]{2,1,0:T(8,128)(2,1)}), bf16[64,24,128]{2,1,0:T(8,128)(2,1)}, u32[]{:S(2)}, u32[]{:S(2)}) async-start(bf16[64,24,128]{2,1,0:T(8,128)(2,1)} %attend.1), calls=%async_computation | async-start | bytes 786432 | tf_op jit(solution)/shard_map/all_to_all | solution.py:27
  17.8 0.4 collective-permute-start
  18.3 1.0 collective-permute-done
  19.2 0.7 copy-done.5
  19.9 1.3 %copy-done.2 = bf16[128,7168]{1,0:T(8,128)(2,1)} copy-done((bf16[128,7168]{1,0:T(8,128)(2,1)}, bf16[128,7168]{1,0:T(8,128)(2,1)S(1)}, u32[]{:S(2)}) %copy-start.2) | copy-done | bytes 1835032
  21.2 1.5 %copy-done.1 = bf16[128,7168]{1,0:T(8,128)(2,1)S(1)} copy-done((bf16[128,7168]{1,0:T(8,128)(2,1)S(1)}, bf16[128,7168]{1,0:T(8,128)(2,1)}, u32[]{:S(2)}) %copy-start.1) | copy-done | bytes 1835032
  22.7 1.5 %copy-done.3 = bf16[128,7168]{1,0:T(8,128)(2,1)S(1)} copy-done((bf16[128,7168]{1,0:T(8,128)(2,1)S(1)}, bf16[128,7168]{1,0:T(8,128)(2,1)}, u32[]{:S(2)}) %copy-start.3) | copy-done | bytes 1835032
  24.2 0.9 copy-done.6
  25.1 1.1 fetch.1
  26.1 2.8 %all-to-all-done.got_ref = bf16[64,24,128]{2,1,0:T(8,128)(2,1)} async-done(((bf16[64,24,128]{2,1,0:T(8,128)(2,1)}), bf16[64,24,128]{2,1,0:T(8,128)(2,1)}, u32[]{:S(2)}, u32[]{:S(2)}) %all-to-all-start) | async-done | bytes 393248 | tf_op jit(solution)/shard_map/all_to_all | solution.py:27
  29.0 1.4 %values.1 = (bf16[224,128]{1,0:T(8,128)(2,1)S(1)}, bf16[224,128]{1,0:T(8,128)(2,1)S(1)}) custom-call(s32[3]{0:T(128)S(1)} %pad_add_fusion.place_ref, bf16[64,24,128]{2,1,0:T(8,128)(2,1)} %all-to-all-done.got_ref, bf16[2,512,128]{2,1,0:T(8,128)(2,1)S(1)} %get-tuple-element.17.uv_ref, bf16[256,3584]{1,0:T(8,128)(2,1)S(1)} %get-tuple-element.18.after_ref.weights_ref), custom_call_target="tpu_custom_call" | custom-call | tf_op jit(solution)/shard_map/values/pallas_call | solution.py:207
  30.4 1.6 %collective-permute-start.2 = (bf16[224,128]{1,0:T(8,128)(2,1)S(1)}, bf16[224,128]{1,0:T(8,128)(2,1)S(1)}, u32[]{:S(2)}, u32[]{:S(2)}) collective-permute-start(bf16[224,128]{1,0:T(8,128)(2,1)S(1)} %get-tuple-element.20), channel_id=1, source_target_pairs={{0,1},{1,0},{2,3},{3,2},{4,5},{5,4},{6,7},{7,6},{8,9},{9,8},{10,11... | collective-permute-start | bytes 172040 | tf_op jit(solution)/shard_map/ppermute | solution.py:23
  32.0 0.9 collective-permute-done.2.got_ref
  32.9 1.0 out_projection.1
  33.9 0.4 collective-permute-start.5
  34.4 22.2 %all_to_all.20 = bf16[64,8,896]{2,1,0:T(8,128)(2,1)S(1)} all-to-all(bf16[64,8,896]{2,1,0:T(8,128)(2,1)S(1)} %bitcast.26), channel_id=1, replica_groups=mesh['x'=4,'z'=4,'y'=4,'core'=2] {'z','x','y'}, dimensions={0} | all-to-all | bytes 1835008 | tf_op jit(solution)/shard_map/all_to_all | solution.py:27
  56.6 0.2 convert_reduce_fusion
  56.8 19.4 %all_to_all.21 = bf16[64,8,896]{2,1,0:T(8,128)(2,1)S(1)} all-to-all(bf16[64,8,896]{2,1,0:T(8,128)(2,1)S(1)} %broadcast_in_dim.4), channel_id=1, replica_groups=mesh['x'=4,'z'=4,'y'=4,'core'=2] {'z','x','y'}, dimensions={0} | all-to-all | bytes 1835008 | tf_op jit(solution)/shard_map/all_to_all | solution.py:27
  76.2 3.4 %collective-permute-start.3 = (bf16[64,8,896]{2,1,0:T(8,128)(2,1)S(1)}, bf16[64,8,896]{2,1,0:T(8,128)(2,1)S(1)}, u32[]{:S(2)}, u32[]{:S(2)}) collective-permute-start(bf16[64,8,896]{2,1,0:T(8,128)(2,1)S(1)} %all_to_all.21), channel_id=1, source_target_pairs={{0,1},{1,0},{2,3},{3,2},{4,5},{5,4},{6,7},{7,6},{8,9},{9,8},{10,11... | collective-permute-start | bytes 2752520 | tf_op jit(solution)/shard_map/ppermute | solution.py:23
  79.6 1.4 %gate_up_first.1 = (f32[128,128]{1,0:T(8,128)S(1)}, f32[3,128,256]{2,1,0:T(8,128)S(1)}) custom-call(s32[3]{0:T(128)S(1)} %pad_add_fusion.place_ref, bf16[16,4,8,896]{3,2,1,0:T(8,128)(2,1)S(1)} %bitcast.18, f32[1,7168]{1,0:T(1,128)S(1)} %bitcast.29, bf16[3,7168,128]{2,1,0:T(8,128)(2,1)S(1)} %bitcast.17, bf16[3,7168,128]{2,1,0:T(8,128)(2,1)S(1)} %copy-done), custom_call_target="tpu_custom_call" | custom-call | tf_op jit(solution)/shard_map/gate_up_first/pallas_call | solution.py:370
  81.1 0.6 collective-permute-done.3
  81.7 1.5 %gate_up_second.1.after_ref.act_own_ref = bf16[128,384]{1,0:T(8,128)(2,1)S(1)} custom-call(s32[3]{0:T(128)S(1)} %pad_add_fusion.place_ref, bf16[16,4,8,896]{3,2,1,0:T(8,128)(2,1)S(1)} %bitcast.24, f32[1,7168]{1,0:T(1,128)S(1)} %bitcast.30, bf16[3,7168,128]{2,1,0:T(8,128)(2,1)S(1)} %bitcast.17, bf16[3,7168,128]{2,1,0:T(8,128)(2,1)S(1)} %copy-done, ...), custom_call_target="tpu_custom_call" | custom-call | tf_op jit(solution)/shard_map/gate_up_second/pallas_call | solution.py:381
  83.2 0.5 collective-permute-start.4
  83.7 1.3 %take_rows.1 = (bf16[1,7168]{1,0:T(2,128)(2,1)}, f32[2,3584]{1,0:T(2,128)S(1)}) custom-call(s32[3]{0:T(128)S(1)} %pad_add_fusion.place_ref, bf16[16,4,8,896]{3,2,1,0:T(8,128)(2,1)S(1)} %bitcast.19, bf16[16,4,8,896]{3,2,1,0:T(8,128)(2,1)S(1)} %bitcast.25, bf16[128,384]{1,0:T(8,128)(2,1)S(1)} %gate_up_second.1.after_ref.act_own_ref), custom_call_target="tpu_custom_call" | custom-call | tf_op jit(solution)/shard_map/take_rows/pallas_call | solution.py:479
  85.0 1.8 %down.1 = bf16[64,56,128]{2,1,0:T(8,128)(2,1)S(1)} custom-call(s32[3]{0:T(128)S(1)} %pad_add_fusion.place_ref, bf16[128,384]{1,0:T(8,128)(2,1)S(1)} %gate_up_second.1.after_ref.act_own_ref, bf16[128,384]{1,0:T(8,128)(2,1)S(1)} %collective-permute-done.4.act_other_ref, bf16[384,7168]{1,0:T(8,128)(2,1)S(1)} %bitcast.23, ...), custom_call_target="tpu_custom_call" | custom-call | tf_op jit(solution)/shard_map/down/pallas_call | solution.py:431
  86.8 20.9 %all_to_all.22.got_ref = bf16[64,56,128]{2,1,0:T(8,128)(2,1)S(1)} all-to-all(bf16[64,56,128]{2,1,0:T(8,128)(2,1)S(1)} %down.1), channel_id=1, replica_groups=mesh['x'=4,'z'=4,'y'=4,'core'=2] {'z','x','y'}, dimensions={0} | all-to-all | bytes 1835008 | tf_op jit(solution)/shard_map/all_to_all | solution.py:27
  107.7 0.8 finish.1
  108.5 1.8 %collective-permute-start.6 = (bf16[1,3584]{1,0:T(2,128)(2,1)S(1)}, bf16[1,3584]{1,0:T(2,128)(2,1)S(1)}, u32[]{:S(2)}, u32[]{:S(2)}) collective-permute-start(bf16[1,3584]{1,0:T(2,128)(2,1)S(1)} %get-tuple-element.31), channel_id=1, source_target_pairs={{0,1},{1,0},{2,3},{3,2},{4,5},{5,4},{6,7},{7,6},{8,9},{9,8},{10,11... | collective-permute-start | bytes 21512 | tf_op jit(solution)/shard_map/ppermute | solution.py:23
  110.3 0.8 collective-permute-done.6
  111.1 0.7 broadcast_select_fusion
  (27 shorter events, 0.2 us)
Async XLA Ops:
  0.6 17.2 %copy-start.4 = (bf16[1,512,128]{2,1,0:T(8,128)(2,1)S(1)}, bf16[1,512,128]{2,1,0:T(8,128)(2,1)}, u32[]{:S(2)}) copy-start(bf16[1,512,128]{2,1,0:T(8,128)(2,1)} %param.18) | copy-start | bytes 393220
  0.6 19.3 %collective-permute-start.1 = (bf16[128,7168]{1,0:T(8,128)(2,1)}, bf16[128,7168]{1,0:T(8,128)(2,1)S(1)}, u32[]{:S(2)}, u32[]{:S(2)}) collective-permute-start(bf16[128,7168]{1,0:T(8,128)(2,1)} %own_hbm.1), channel_id=1, source_target_pairs={{0,1},{1,0},{2,3},{3,2},{4,5},{5,4},{6,7},{7,6},{8,9},{9,8},{10,11... | collective-permute-start | bytes 5505032 | tf_op jit(solution)/shard_map/ppermute | solution.py:23
  6.3 22.7 %all-to-all-start = ((bf16[64,24,128]{2,1,0:T(8,128)(2,1)}), bf16[64,24,128]{2,1,0:T(8,128)(2,1)}, u32[]{:S(2)}, u32[]{:S(2)}) async-start(bf16[64,24,128]{2,1,0:T(8,128)(2,1)} %attend.1), calls=%async_computation | async-start | bytes 786432 | tf_op jit(solution)/shard_map/all_to_all | solution.py:27
  17.8 1.4 %collective-permute-start = (bf16[1,512,128]{2,1,0:T(8,128)(2,1)S(1)}, bf16[1,512,128]{2,1,0:T(8,128)(2,1)S(1)}, u32[]{:S(2)}, u32[]{:S(2)}) collective-permute-start(bf16[1,512,128]{2,1,0:T(8,128)(2,1)S(1)} %copy-done.4), channel_id=1, source_target_pairs={{0,1},{1,0},{2,3},{3,2},{4,5},{5,4},{6,7},{7,6},{8,9},{9,8},{10,11... | collective-permute-start | bytes 393224 | tf_op jit(solution)/shard_map/ppermute | solution.py:23
  19.2 0.7 copy-start.5
  19.9 1.3 %copy-start.2 = (bf16[128,7168]{1,0:T(8,128)(2,1)}, bf16[128,7168]{1,0:T(8,128)(2,1)S(1)}, u32[]{:S(2)}) copy-start(bf16[128,7168]{1,0:T(8,128)(2,1)S(1)} %collective-permute-done.1.other_hbm) | copy-start | bytes 5505028
  21.2 1.5 %copy-start.1 = (bf16[128,7168]{1,0:T(8,128)(2,1)S(1)}, bf16[128,7168]{1,0:T(8,128)(2,1)}, u32[]{:S(2)}) copy-start(bf16[128,7168]{1,0:T(8,128)(2,1)} %own_hbm.1) | copy-start | bytes 5505028
  22.7 1.5 %copy-start.3 = (bf16[128,7168]{1,0:T(8,128)(2,1)S(1)}, bf16[128,7168]{1,0:T(8,128)(2,1)}, u32[]{:S(2)}) copy-start(bf16[128,7168]{1,0:T(8,128)(2,1)} %copy-done.2) | copy-start | bytes 5505028
  24.2 0.9 copy-start.6
  25.1 54.6 %slice-start = ((s8[5505024]{0:T(1024)(128)(4,1)}), s8[1310720]{0:T(1024)(128)(4,1)S(1)}, s32[]{:S(2)}) async-start(s8[5505024]{0:T(1024)(128)(4,1)} %bitcast.16), calls=%async_computation.4 | async-start | bytes 2621440
  29.0 50.6 %copy-start = (bf16[3,7168,128]{2,1,0:T(8,128)(2,1)S(1)}, bf16[3,7168,128]{2,1,0:T(8,128)(2,1)}, u32[]{:S(2)}) copy-start(bf16[3,7168,128]{2,1,0:T(8,128)(2,1)} %up_ref.3) | copy-start | bytes 16515076
  30.4 2.5 %collective-permute-start.2 = (bf16[224,128]{1,0:T(8,128)(2,1)S(1)}, bf16[224,128]{1,0:T(8,128)(2,1)S(1)}, u32[]{:S(2)}, u32[]{:S(2)}) collective-permute-start(bf16[224,128]{1,0:T(8,128)(2,1)S(1)} %get-tuple-element.20), channel_id=1, source_target_pairs={{0,1},{1,0},{2,3},{3,2},{4,5},{5,4},{6,7},{7,6},{8,9},{9,8},{10,11... | collective-permute-start | bytes 172040 | tf_op jit(solution)/shard_map/ppermute | solution.py:23
  32.9 46.7 %slice-start.1 = ((s8[5505024]{0:T(1024)(128)(4,1)}), s8[4194304]{0:T(1024)(128)(4,1)S(1)}, s32[]{:S(2)}) async-start(s8[5505024]{0:T(1024)(128)(4,1)} %bitcast.16), calls=%async_computation.5 | async-start | bytes 8388608
  33.9 51.0 %collective-permute-start.5 = (bf16[384,7168]{1,0:T(8,128)(2,1)}, bf16[384,7168]{1,0:T(8,128)(2,1)S(1)}, u32[]{:S(2)}, u32[]{:S(2)}) collective-permute-start(bf16[384,7168]{1,0:T(8,128)(2,1)} %bitcast.20), channel_id=1, source_target_pairs={{0,1},{1,0},{2,3},{3,2},{4,5},{5,4},{6,7},{7,6},{8,9},{9,8},{10,11... | collective-permute-start | bytes 16515080 | tf_op jit(solution)/shard_map/ppermute | solution.py:23
  56.6 23.0 %copy-start.7 = (f32[7168]{0:T(1024)S(1)}, f32[7168]{0:T(1024)}, u32[]{:S(2)}) copy-start(f32[7168]{0:T(1024)} %param.20) | copy-start | bytes 86020
  76.2 5.5 %collective-permute-start.3 = (bf16[64,8,896]{2,1,0:T(8,128)(2,1)S(1)}, bf16[64,8,896]{2,1,0:T(8,128)(2,1)S(1)}, u32[]{:S(2)}, u32[]{:S(2)}) collective-permute-start(bf16[64,8,896]{2,1,0:T(8,128)(2,1)S(1)} %all_to_all.21), channel_id=1, source_target_pairs={{0,1},{1,0},{2,3},{3,2},{4,5},{5,4},{6,7},{7,6},{8,9},{9,8},{10,11... | collective-permute-start | bytes 2752520 | tf_op jit(solution)/shard_map/ppermute | solution.py:23
  81.7 3.3 %slice-start.2 = ((s8[5505024]{0:T(1024)(128)(4,1)}), s8[4194304]{0:T(1024)(128)(4,1)S(1)}, s32[]{:S(2)}) async-start(s8[5505024]{0:T(1024)(128)(4,1)} %bitcast.21), calls=%async_computation.6 | async-start | bytes 8388608
  81.7 3.3 %slice-start.3 = ((s8[5505024]{0:T(1024)(128)(4,1)}), s8[1310720]{0:T(1024)(128)(4,1)S(1)}, s32[]{:S(2)}) async-start(s8[5505024]{0:T(1024)(128)(4,1)} %bitcast.21), calls=%async_computation.7 | async-start | bytes 2621440
  83.2 1.7 %collective-permute-start.4 = (bf16[128,384]{1,0:T(8,128)(2,1)S(1)}, bf16[128,384]{1,0:T(8,128)(2,1)S(1)}, u32[]{:S(2)}, u32[]{:S(2)}) collective-permute-start(bf16[128,384]{1,0:T(8,128)(2,1)S(1)} %gate_up_second.1.after_ref.act_own_ref), channel_id=1, source_target_pairs={{0,1},{1,0},{2,3},{3,2},{4,5},{5,4},{6,7},{7,6},{8,9},{9,8},{10,11... | collective-permute-start | bytes 294920 | tf_op jit(solution)/shard_map/ppermute | solution.py:23
  108.5 2.6 %collective-permute-start.6 = (bf16[1,3584]{1,0:T(2,128)(2,1)S(1)}, bf16[1,3584]{1,0:T(2,128)(2,1)S(1)}, u32[]{:S(2)}, u32[]{:S(2)}) collective-permute-start(bf16[1,3584]{1,0:T(2,128)(2,1)S(1)} %get-tuple-element.31), channel_id=1, source_target_pairs={{0,1},{1,0},{2,3},{3,2},{4,5},{5,4},{6,7},{7,6},{8,9},{9,8},{10,11... | collective-permute-start | bytes 21512 | tf_op jit(solution)/shard_map/ppermute | solution.py:23

commit v7 on v6

--- a/solution.py
+++ b/solution.py
@@ -324,18 +324,15 @@
     groups, quarters, eight, wide = rows_ref.shape
     rows = groups * eight
     experts = gate_ref.shape[0]
-    total = jnp.zeros((rows, 1), F32)
-    sums = [None] * experts
-    for pair in range(quarters // 2):
-        pieces = [rows_ref[:, q].reshape(rows, wide) for q in (2 * pair, 2 * pair + 1)]
-        piece = jnp.concatenate(pieces, axis=1).astype(F32)
-        total = total + jnp.sum(piece * piece, axis=1, keepdims=True)
-        at = pl.ds(pl.multiple_of(half * (quarters * wide) + pair * (2 * wide), 256), 2 * wide)
-        scaled = (piece * gain_ref[:, at]).astype(BF)
-        for e in range(experts):
-            weights = jnp.concatenate([gate_ref[e, at, :], up_ref[e, at, :]], axis=1)
-            product = jnp.dot(scaled, weights, preferred_element_type=F32)
-            sums[e] = product if sums[e] is None else sums[e] + product
+    pieces = [rows_ref[:, q].reshape(rows, wide) for q in range(quarters)]
+    piece = jnp.concatenate(pieces, axis=1).astype(F32)
+    total = jnp.sum(piece * piece, axis=1, keepdims=True)
+    at = pl.ds(pl.multiple_of(half * (quarters * wide), 256), quarters * wide)
+    scaled = (piece * gain_ref[:, at]).astype(BF)
+    sums = []
+    for e in range(experts):
+        weights = jnp.concatenate([gate_ref[e, at, :], up_ref[e, at, :]], axis=1)
+        sums.append(jnp.dot(scaled, weights, preferred_element_type=F32))
     return total, sums
 
 

time: 112 us -> 112 us (level)
  no operation moved by 1% of the time
where the time goes in v7:
time: 112 us
  blocking collectives  62.5 us (56%)
  starting transfers between devices  21 us (19%)
  Pallas kernels  13.9 us (12%)
  waiting for transfers between devices  6.18 us (6%)
  local copies, waits for them, and re-layouts  5.91 us (5%)
  between operations  1.41 us (1%)
    all_to_all x3, blocking collectives, exchange(): lax.all_to_all(value, CHIP_AXES, split_axis=0, concat_axis=0, tiled=True)  62.5 us
    all_to_all x1, starting transfers between devices, exchange(): lax.all_to_all(value, CHIP_AXES, split_axis=0, concat_axis=0, tiled=True)  11.5 us
    ppermute x7, starting transfers between devices, swap(): return lax.ppermute(value, 'core', SWAP)  9.56 us
    unnamed x24, local copies, waits for them, and re-layouts  5.84 us
    pallas_call x1, Pallas kernels, attend_and_pack(): pl.pallas_call(attend_kernel, in_specs=[pl.BlockSpec(memory_space=pltpu.S...  3.54 us
    ppermute x7, waiting for transfers between devices, swap(): return lax.ppermute(value, 'core', SWAP)  3.35 us
    all_to_all x1, waiting for transfers between devices, exchange(): lax.all_to_all(value, CHIP_AXES, split_axis=0, concat_axis=0, tiled=True)  2.83 us
  transfers between devices with their start and end apart: 8, of which 5 were waited for; matrix products, arithmetic and copies ran while one was open for 0% of the time, Pallas kernels for 8%

profile of v7, /device:TPU:1, one launch (start us, length us, event | category | flops | bytes accessed | tf_op | source)
XLA Modules:
  0.0 111.8 jit_solution(81647260904034818)
XLA Ops:
  0.6 1.5 %collective-permute-start.1 = (bf16[128,7168]{1,0:T(8,128)(2,1)}, bf16[128,7168]{1,0:T(8,128)(2,1)S(1)}, u32[]{:S(2)}, u32[]{:S(2)}) collective-permute-start(bf16[128,7168]{1,0:T(8,128)(2,1)} %own_hbm.1), channel_id=1, source_target_pairs={{0,1},{1,0},{2,3},{3,2},{4,5},{5,4},{6,7},{7,6},{8,9},{9,8},{10,11... | collective-permute-start | bytes 5505032 | tf_op jit(solution)/shard_map/ppermute | solution.py:23
  2.8 3.5 %attend.1 = bf16[64,24,128]{2,1,0:T(8,128)(2,1)} custom-call(s32[1]{0:T(128)S(6)} %copy.15.length_ref, bf16[576,128]{1,0:T(8,128)(2,1)} %bitcast.32, bf16[576,1024]{1,0:T(8,128)(2,1)} %bitcast.31, bf16[1,576]{1,0:T(2,128)(2,1)} %newest_hbm.1, bf16[1,7168]{1,0:T(2,128)(2,1)} %states_hbm.1, s32[1,8]{1,0:T(1,128)} %ids_hbm.1, f32[1,8]{1,0:T(1,128)} %score_hbm.1), custom_call_target="tpu_custom_call" | custom-call | tf_op jit(solution)/shard_map/attend/pallas_call | solution.py:147
  6.3 11.5 %all-to-all-start = ((bf16[64,24,128]{2,1,0:T(8,128)(2,1)}), bf16[64,24,128]{2,1,0:T(8,128)(2,1)}, u32[]{:S(2)}, u32[]{:S(2)}) async-start(bf16[64,24,128]{2,1,0:T(8,128)(2,1)} %attend.1), calls=%async_computation | async-start | bytes 786432 | tf_op jit(solution)/shard_map/all_to_all | solution.py:27
  17.8 0.4 collective-permute-start
  18.3 1.0 collective-permute-done
  19.2 0.7 copy-done.5
  19.9 1.3 %copy-done.2 = bf16[128,7168]{1,0:T(8,128)(2,1)} copy-done((bf16[128,7168]{1,0:T(8,128)(2,1)}, bf16[128,7168]{1,0:T(8,128)(2,1)S(1)}, u32[]{:S(2)}) %copy-start.2) | copy-done | bytes 1835032
  21.2 1.5 %copy-done.1 = bf16[128,7168]{1,0:T(8,128)(2,1)S(1)} copy-done((bf16[128,7168]{1,0:T(8,128)(2,1)S(1)}, bf16[128,7168]{1,0:T(8,128)(2,1)}, u32[]{:S(2)}) %copy-start.1) | copy-done | bytes 1835032
  22.7 1.5 %copy-done.3 = bf16[128,7168]{1,0:T(8,128)(2,1)S(1)} copy-done((bf16[128,7168]{1,0:T(8,128)(2,1)S(1)}, bf16[128,7168]{1,0:T(8,128)(2,1)}, u32[]{:S(2)}) %copy-start.3) | copy-done | bytes 1835032
  24.2 0.9 copy-done.6
  25.1 1.1 fetch.1
  26.1 2.8 %all-to-all-done.got_ref = bf16[64,24,128]{2,1,0:T(8,128)(2,1)} async-done(((bf16[64,24,128]{2,1,0:T(8,128)(2,1)}), bf16[64,24,128]{2,1,0:T(8,128)(2,1)}, u32[]{:S(2)}, u32[]{:S(2)}) %all-to-all-start) | async-done | bytes 393248 | tf_op jit(solution)/shard_map/all_to_all | solution.py:27
  29.0 1.4 %values.1 = (bf16[224,128]{1,0:T(8,128)(2,1)S(1)}, bf16[224,128]{1,0:T(8,128)(2,1)S(1)}) custom-call(s32[3]{0:T(128)S(1)} %pad_add_fusion.place_ref, bf16[64,24,128]{2,1,0:T(8,128)(2,1)} %all-to-all-done.got_ref, bf16[2,512,128]{2,1,0:T(8,128)(2,1)S(1)} %get-tuple-element.17.uv_ref, bf16[256,3584]{1,0:T(8,128)(2,1)S(1)} %get-tuple-element.18.after_ref.weights_ref), custom_call_target="tpu_custom_call" | custom-call | tf_op jit(solution)/shard_map/values/pallas_call | solution.py:207
  30.4 1.6 %collective-permute-start.2 = (bf16[224,128]{1,0:T(8,128)(2,1)S(1)}, bf16[224,128]{1,0:T(8,128)(2,1)S(1)}, u32[]{:S(2)}, u32[]{:S(2)}) collective-permute-start(bf16[224,128]{1,0:T(8,128)(2,1)S(1)} %get-tuple-element.20), channel_id=1, source_target_pairs={{0,1},{1,0},{2,3},{3,2},{4,5},{5,4},{6,7},{7,6},{8,9},{9,8},{10,11... | collective-permute-start | bytes 172040 | tf_op jit(solution)/shard_map/ppermute | solution.py:23
  32.0 0.9 collective-permute-done.2.got_ref
  32.9 1.0 out_projection.1
  33.9 0.4 collective-permute-start.5
  34.4 22.2 %all_to_all.20 = bf16[64,8,896]{2,1,0:T(8,128)(2,1)S(1)} all-to-all(bf16[64,8,896]{2,1,0:T(8,128)(2,1)S(1)} %bitcast.26), channel_id=1, replica_groups=mesh['x'=4,'z'=4,'y'=4,'core'=2] {'z','x','y'}, dimensions={0} | all-to-all | bytes 1835008 | tf_op jit(solution)/shard_map/all_to_all | solution.py:27
  56.6 0.2 convert_reduce_fusion
  56.8 19.4 %all_to_all.21 = bf16[64,8,896]{2,1,0:T(8,128)(2,1)S(1)} all-to-all(bf16[64,8,896]{2,1,0:T(8,128)(2,1)S(1)} %broadcast_in_dim.4), channel_id=1, replica_groups=mesh['x'=4,'z'=4,'y'=4,'core'=2] {'z','x','y'}, dimensions={0} | all-to-all | bytes 1835008 | tf_op jit(solution)/shard_map/all_to_all | solution.py:27
  76.2 3.4 %collective-permute-start.3 = (bf16[64,8,896]{2,1,0:T(8,128)(2,1)S(1)}, bf16[64,8,896]{2,1,0:T(8,128)(2,1)S(1)}, u32[]{:S(2)}, u32[]{:S(2)}) collective-permute-start(bf16[64,8,896]{2,1,0:T(8,128)(2,1)S(1)} %all_to_all.21), channel_id=1, source_target_pairs={{0,1},{1,0},{2,3},{3,2},{4,5},{5,4},{6,7},{7,6},{8,9},{9,8},{10,11... | collective-permute-start | bytes 2752520 | tf_op jit(solution)/shard_map/ppermute | solution.py:23
  79.6 1.4 %gate_up_first.1 = (f32[128,128]{1,0:T(8,128)S(1)}, f32[3,128,256]{2,1,0:T(8,128)S(1)}) custom-call(s32[3]{0:T(128)S(1)} %pad_add_fusion.place_ref, bf16[16,4,8,896]{3,2,1,0:T(8,128)(2,1)S(1)} %bitcast.18, f32[1,7168]{1,0:T(1,128)S(1)} %bitcast.29, bf16[3,7168,128]{2,1,0:T(8,128)(2,1)S(1)} %bitcast.17, bf16[3,7168,128]{2,1,0:T(8,128)(2,1)S(1)} %copy-done), custom_call_target="tpu_custom_call" | custom-call | tf_op jit(solution)/shard_map/gate_up_first/pallas_call | solution.py:367
  81.1 0.6 collective-permute-done.3
  81.7 1.5 %gate_up_second.1.after_ref.act_own_ref = bf16[128,384]{1,0:T(8,128)(2,1)S(1)} custom-call(s32[3]{0:T(128)S(1)} %pad_add_fusion.place_ref, bf16[16,4,8,896]{3,2,1,0:T(8,128)(2,1)S(1)} %bitcast.24, f32[1,7168]{1,0:T(1,128)S(1)} %bitcast.30, bf16[3,7168,128]{2,1,0:T(8,128)(2,1)S(1)} %bitcast.17, bf16[3,7168,128]{2,1,0:T(8,128)(2,1)S(1)} %copy-done, ...), custom_call_target="tpu_custom_call" | custom-call | tf_op jit(solution)/shard_map/gate_up_second/pallas_call | solution.py:378
  83.3 0.5 collective-permute-start.4
  83.7 1.3 %take_rows.1 = (bf16[1,7168]{1,0:T(2,128)(2,1)}, f32[2,3584]{1,0:T(2,128)S(1)}) custom-call(s32[3]{0:T(128)S(1)} %pad_add_fusion.place_ref, bf16[16,4,8,896]{3,2,1,0:T(8,128)(2,1)S(1)} %bitcast.19, bf16[16,4,8,896]{3,2,1,0:T(8,128)(2,1)S(1)} %bitcast.25, bf16[128,384]{1,0:T(8,128)(2,1)S(1)} %gate_up_second.1.after_ref.act_own_ref), custom_call_target="tpu_custom_call" | custom-call | tf_op jit(solution)/shard_map/take_rows/pallas_call | solution.py:476
  85.0 1.8 %down.1 = bf16[64,56,128]{2,1,0:T(8,128)(2,1)S(1)} custom-call(s32[3]{0:T(128)S(1)} %pad_add_fusion.place_ref, bf16[128,384]{1,0:T(8,128)(2,1)S(1)} %gate_up_second.1.after_ref.act_own_ref, bf16[128,384]{1,0:T(8,128)(2,1)S(1)} %collective-permute-done.4.act_other_ref, bf16[384,7168]{1,0:T(8,128)(2,1)S(1)} %bitcast.23, ...), custom_call_target="tpu_custom_call" | custom-call | tf_op jit(solution)/shard_map/down/pallas_call | solution.py:428
  86.9 20.9 %all_to_all.22.got_ref = bf16[64,56,128]{2,1,0:T(8,128)(2,1)S(1)} all-to-all(bf16[64,56,128]{2,1,0:T(8,128)(2,1)S(1)} %down.1), channel_id=1, replica_groups=mesh['x'=4,'z'=4,'y'=4,'core'=2] {'z','x','y'}, dimensions={0} | all-to-all | bytes 1835008 | tf_op jit(solution)/shard_map/all_to_all | solution.py:27
  107.7 0.8 finish.1
  108.5 1.8 %collective-permute-start.6 = (bf16[1,3584]{1,0:T(2,128)(2,1)S(1)}, bf16[1,3584]{1,0:T(2,128)(2,1)S(1)}, u32[]{:S(2)}, u32[]{:S(2)}) collective-permute-start(bf16[1,3584]{1,0:T(2,128)(2,1)S(1)} %get-tuple-element.31), channel_id=1, source_target_pairs={{0,1},{1,0},{2,3},{3,2},{4,5},{5,4},{6,7},{7,6},{8,9},{9,8},{10,11... | collective-permute-start | bytes 21512 | tf_op jit(solution)/shard_map/ppermute | solution.py:23
  110.3 0.8 collective-permute-done.6
  111.1 0.7 broadcast_select_fusion
  (27 shorter events, 0.2 us)
Async XLA Ops:
  0.6 17.2 %copy-start.4 = (bf16[1,512,128]{2,1,0:T(8,128)(2,1)S(1)}, bf16[1,512,128]{2,1,0:T(8,128)(2,1)}, u32[]{:S(2)}) copy-start(bf16[1,512,128]{2,1,0:T(8,128)(2,1)} %param.18) | copy-start | bytes 393220
  0.6 19.3 %collective-permute-start.1 = (bf16[128,7168]{1,0:T(8,128)(2,1)}, bf16[128,7168]{1,0:T(8,128)(2,1)S(1)}, u32[]{:S(2)}, u32[]{:S(2)}) collective-permute-start(bf16[128,7168]{1,0:T(8,128)(2,1)} %own_hbm.1), channel_id=1, source_target_pairs={{0,1},{1,0},{2,3},{3,2},{4,5},{5,4},{6,7},{7,6},{8,9},{9,8},{10,11... | collective-permute-start | bytes 5505032 | tf_op jit(solution)/shard_map/ppermute | solution.py:23
  6.3 22.7 %all-to-all-start = ((bf16[64,24,128]{2,1,0:T(8,128)(2,1)}), bf16[64,24,128]{2,1,0:T(8,128)(2,1)}, u32[]{:S(2)}, u32[]{:S(2)}) async-start(bf16[64,24,128]{2,1,0:T(8,128)(2,1)} %attend.1), calls=%async_computation | async-start | bytes 786432 | tf_op jit(solution)/shard_map/all_to_all | solution.py:27
  17.8 1.4 %collective-permute-start = (bf16[1,512,128]{2,1,0:T(8,128)(2,1)S(1)}, bf16[1,512,128]{2,1,0:T(8,128)(2,1)S(1)}, u32[]{:S(2)}, u32[]{:S(2)}) collective-permute-start(bf16[1,512,128]{2,1,0:T(8,128)(2,1)S(1)} %copy-done.4), channel_id=1, source_target_pairs={{0,1},{1,0},{2,3},{3,2},{4,5},{5,4},{6,7},{7,6},{8,9},{9,8},{10,11... | collective-permute-start | bytes 393224 | tf_op jit(solution)/shard_map/ppermute | solution.py:23
  19.2 0.7 copy-start.5
  19.9 1.3 %copy-start.2 = (bf16[128,7168]{1,0:T(8,128)(2,1)}, bf16[128,7168]{1,0:T(8,128)(2,1)S(1)}, u32[]{:S(2)}) copy-start(bf16[128,7168]{1,0:T(8,128)(2,1)S(1)} %collective-permute-done.1.other_hbm) | copy-start | bytes 5505028
  21.2 1.5 %copy-start.1 = (bf16[128,7168]{1,0:T(8,128)(2,1)S(1)}, bf16[128,7168]{1,0:T(8,128)(2,1)}, u32[]{:S(2)}) copy-start(bf16[128,7168]{1,0:T(8,128)(2,1)} %own_hbm.1) | copy-start | bytes 5505028
  22.7 1.5 %copy-start.3 = (bf16[128,7168]{1,0:T(8,128)(2,1)S(1)}, bf16[128,7168]{1,0:T(8,128)(2,1)}, u32[]{:S(2)}) copy-start(bf16[128,7168]{1,0:T(8,128)(2,1)} %copy-done.2) | copy-start | bytes 5505028
  24.2 0.9 copy-start.6
  25.1 54.6 %slice-start = ((s8[5505024]{0:T(1024)(128)(4,1)}), s8[1310720]{0:T(1024)(128)(4,1)S(1)}, s32[]{:S(2)}) async-start(s8[5505024]{0:T(1024)(128)(4,1)} %bitcast.16), calls=%async_computation.4 | async-start | bytes 2621440
  29.0 50.6 %copy-start = (bf16[3,7168,128]{2,1,0:T(8,128)(2,1)S(1)}, bf16[3,7168,128]{2,1,0:T(8,128)(2,1)}, u32[]{:S(2)}) copy-start(bf16[3,7168,128]{2,1,0:T(8,128)(2,1)} %up_ref.3) | copy-start | bytes 16515076
  30.4 2.5 %collective-permute-start.2 = (bf16[224,128]{1,0:T(8,128)(2,1)S(1)}, bf16[224,128]{1,0:T(8,128)(2,1)S(1)}, u32[]{:S(2)}, u32[]{:S(2)}) collective-permute-start(bf16[224,128]{1,0:T(8,128)(2,1)S(1)} %get-tuple-element.20), channel_id=1, source_target_pairs={{0,1},{1,0},{2,3},{3,2},{4,5},{5,4},{6,7},{7,6},{8,9},{9,8},{10,11... | collective-permute-start | bytes 172040 | tf_op jit(solution)/shard_map/ppermute | solution.py:23
  32.9 46.7 %slice-start.1 = ((s8[5505024]{0:T(1024)(128)(4,1)}), s8[4194304]{0:T(1024)(128)(4,1)S(1)}, s32[]{:S(2)}) async-start(s8[5505024]{0:T(1024)(128)(4,1)} %bitcast.16), calls=%async_computation.5 | async-start | bytes 8388608
  33.9 51.1 %collective-permute-start.5 = (bf16[384,7168]{1,0:T(8,128)(2,1)}, bf16[384,7168]{1,0:T(8,128)(2,1)S(1)}, u32[]{:S(2)}, u32[]{:S(2)}) collective-permute-start(bf16[384,7168]{1,0:T(8,128)(2,1)} %bitcast.20), channel_id=1, source_target_pairs={{0,1},{1,0},{2,3},{3,2},{4,5},{5,4},{6,7},{7,6},{8,9},{9,8},{10,11... | collective-permute-start | bytes 16515080 | tf_op jit(solution)/shard_map/ppermute | solution.py:23
  56.6 23.0 %copy-start.7 = (f32[7168]{0:T(1024)S(1)}, f32[7168]{0:T(1024)}, u32[]{:S(2)}) copy-start(f32[7168]{0:T(1024)} %param.20) | copy-start | bytes 86020
  76.2 5.5 %collective-permute-start.3 = (bf16[64,8,896]{2,1,0:T(8,128)(2,1)S(1)}, bf16[64,8,896]{2,1,0:T(8,128)(2,1)S(1)}, u32[]{:S(2)}, u32[]{:S(2)}) collective-permute-start(bf16[64,8,896]{2,1,0:T(8,128)(2,1)S(1)} %all_to_all.21), channel_id=1, source_target_pairs={{0,1},{1,0},{2,3},{3,2},{4,5},{5,4},{6,7},{7,6},{8,9},{9,8},{10,11... | collective-permute-start | bytes 2752520 | tf_op jit(solution)/shard_map/ppermute | solution.py:23
  81.7 3.3 %slice-start.2 = ((s8[5505024]{0:T(1024)(128)(4,1)}), s8[4194304]{0:T(1024)(128)(4,1)S(1)}, s32[]{:S(2)}) async-start(s8[5505024]{0:T(1024)(128)(4,1)} %bitcast.21), calls=%async_computation.6 | async-start | bytes 8388608
  81.7 3.3 %slice-start.3 = ((s8[5505024]{0:T(1024)(128)(4,1)}), s8[1310720]{0:T(1024)(128)(4,1)S(1)}, s32[]{:S(2)}) async-start(s8[5505024]{0:T(1024)(128)(4,1)} %bitcast.21), calls=%async_computation.7 | async-start | bytes 2621440
  83.3 1.7 %collective-permute-start.4 = (bf16[128,384]{1,0:T(8,128)(2,1)S(1)}, bf16[128,384]{1,0:T(8,128)(2,1)S(1)}, u32[]{:S(2)}, u32[]{:S(2)}) collective-permute-start(bf16[128,384]{1,0:T(8,128)(2,1)S(1)} %gate_up_second.1.after_ref.act_own_ref), channel_id=1, source_target_pairs={{0,1},{1,0},{2,3},{3,2},{4,5},{5,4},{6,7},{7,6},{8,9},{9,8},{10,11... | collective-permute-start | bytes 294920 | tf_op jit(solution)/shard_map/ppermute | solution.py:23
  108.5 2.6 %collective-permute-start.6 = (bf16[1,3584]{1,0:T(2,128)(2,1)S(1)}, bf16[1,3584]{1,0:T(2,128)(2,1)S(1)}, u32[]{:S(2)}, u32[]{:S(2)}) collective-permute-start(bf16[1,3584]{1,0:T(2,128)(2,1)S(1)} %get-tuple-element.31), channel_id=1, source_target_pairs={{0,1},{1,0},{2,3},{3,2},{4,5},{5,4},{6,7},{7,6},{8,9},{9,8},{10,11... | collective-permute-start | bytes 21512 | tf_op jit(solution)/shard_map/ppermute | solution.py:23
